TPU v7x, 32 devices: a whole 2x2x4 slice. The times are simulated.
32 devices in a mesh: space: 8 (over z, x), taxa: 4 (over y, core).
Axes of the slice: x: 2, y: 2, z: 4, core: 2. Of those that a mesh axis runs over, the one named last changes fastest.
Arguments:
- biomass: float32 [2048, 64, 256], P('taxa', 'space'), may hold values from 0.1 to 2
- enzymes: float32 [40, 64, 256], P(None, 'space'), may hold values from 0.1 to 1
- substrates: float32 [12, 64, 256], P(None, 'space'), may hold values from 0.5 to 5
- monomers: float32 [14, 64, 256], P(None, 'space'), may hold values from 0.1 to 2
- enz_traits: int32 [2048, 40], P('taxa'), may hold values 0 or 1
- mono_traits: int32 [2048, 14], P('taxa'), may hold values 0 or 1
- enz_target: int32 [40], replicated, may hold values from 0 to 11
- prod_rate: float32 [2048], P('taxa'), may hold values from 0.002 to 0.02
- uptake_rate: float32 [2048], P('taxa'), may hold values from 0.0005 to 0.005
- mortality: float32 [2048], P('taxa'), may hold values from 0.02 to 0.1
- disperse: float32 [2048], P('taxa'), may hold values from 0.1 to 0.5
- enz_loss: float32 [40], replicated, may hold values from 0.05 to 0.3
- vmax: float32 [40], replicated, may hold values from 0.05 to 0.5
- kmich: float32 [40], replicated, may hold values from 0.5 to 5
- khalf: float32 [14], replicated, may hold values from 0.5 to 5
- offsets: int32 [8, 2], replicated, may hold values from -2 to 2, as said below
Outputs:
- biomass_out: float32 [2048, 64, 256], P('taxa', 'space')
- enzymes_out: float32 [40, 64, 256], P(None, 'space')
- substrates_out: float32 [12, 64, 256], P(None, 'space')
- monomers_out: float32 [14, 64, 256], P(None, 'space')
Inputs may be any that keep to these rules, and one draw needn't show every extreme that they name: Offsets lie in -2 to 2 in both entries and are never both zero; among the row offsets, -2 and 2 each appear twice.
All inputs are finite; a program needn't handle non-finite values. No bound on the sum of `enz_traits` or of `mono_traits` on one device may be relied on, other than what follows from the above.
Results may differ from a plain program's by a relative error of at most 0.00011.
Values sent between devices are 32-bit elements; how exact they have to be, the bound alone decides.
No kernel may reach another device: no remote copies, remote signals or barrier semaphores. Data moves between devices by JAX's collectives and lax.ppermute only.
A program may use at most 128 MiB of HBM per device.

v0:
```python
import jax
import jax.numpy as jnp
from jax import lax
from jax.sharding import PartitionSpec as P

KOFF = 8
DAYS = 2


HIGH = lax.Precision.HIGHEST
YIELD = 0.6


def extended(block, sides, width):
    for axis, dim in sides:
        count = lax.axis_size(axis)
        forward = [(i, i + 1) for i in range(count - 1)]
        forward.append((count - 1, 0))
        backward = [(target, source) for source, target in forward]
        low = lax.ppermute(
            lax.slice_in_dim(block, block.shape[dim] - width, None, axis=dim), axis, forward
        )
        high = lax.ppermute(lax.slice_in_dim(block, 0, width, axis=dim), axis, backward)
        block = jnp.concatenate([low, block, high], axis=dim)
    return block


def cell_update(sums, enz, sub, mono, enz_loss, vmax, kmich, khalf, enz_target):
    n_enz = enz.shape[0]
    made = sums[:n_enz]
    demand = sums[n_enz:]
    pool = enz * (1.0 - enz_loss)[:, None, None] + made
    pick = (enz_target[:, None] == lax.iota(jnp.int32, sub.shape[0])[None, :]).astype(jnp.float32)
    target_sub = jnp.einsum("es,srw->erw", pick, sub, precision=HIGH)
    speed = vmax[:, None, None] * pool / (kmich[:, None, None] + target_sub)
    rate = jnp.einsum("es,erw->srw", pick, speed, precision=HIGH)
    left = sub * jnp.exp(-rate)
    freed = sub - left
    extra = jnp.zeros((mono.shape[0] - sub.shape[0],) + sub.shape[1:], jnp.float32)
    mono_one = mono + jnp.concatenate([freed, extra], 0)
    share = mono_one / (khalf[:, None, None] + demand + mono_one)
    mono_two = mono_one - demand * share
    return (pool, left, mono_two, share)


def pool_update(bio, enz, sub, mono, prod_w, upt_w, enz_loss, vmax, kmich, khalf, enz_target):
    count, rows, width = bio.shape
    flat = bio.reshape(count, rows * width)
    made = jnp.dot(prod_w.T, flat, precision=HIGH, preferred_element_type=jnp.float32)
    need = jnp.dot(upt_w.T, flat, precision=HIGH, preferred_element_type=jnp.float32)
    local = jnp.concatenate([made, need], 0).reshape(-1, rows, width)
    sums = lax.psum(local, "taxa")
    return cell_update(sums, enz, sub, mono, enz_loss, vmax, kmich, khalf, enz_target)


def grow(bio, share, mono_w, uptake_rate, keep):
    gain = jnp.einsum("tm,mrw->trw", mono_w, share, precision=HIGH)
    return bio * (keep[:, None, None] + YIELD * uptake_rate[:, None, None] * gain)


def spread(grown_pad, disperse, offsets, rows):
    fraction = disperse[:, None, None]
    moved_pad = grown_pad * fraction
    centre = grown_pad[:, 2 : 2 + rows]
    total = jnp.zeros_like(centre)
    for k in range(KOFF):
        piece = lax.dynamic_slice_in_dim(moved_pad, 2 - offsets[k, 0], rows, 1)
        total = total + jnp.roll(piece, offsets[k, 1], axis=2)
    return centre - centre * fraction + total / KOFF


def body(
    biomass,
    enzymes,
    substrates,
    monomers,
    enz_traits,
    mono_traits,
    enz_target,
    prod_rate,
    uptake_rate,
    mortality,
    disperse,
    enz_loss,
    vmax,
    kmich,
    khalf,
    offsets,
):
    prod_w = enz_traits.astype(jnp.float32) * prod_rate[:, None]
    mono_w = mono_traits.astype(jnp.float32)
    upt_w = mono_w * uptake_rate[:, None]
    keep = 1.0 - mortality - prod_rate * jnp.sum(enz_traits.astype(jnp.float32), axis=1)
    rows = biomass.shape[1]
    bio = biomass
    for day in range(DAYS):
        enzymes, substrates, monomers, share = pool_update(
            bio,
            enzymes,
            substrates,
            monomers,
            prod_w,
            upt_w,
            enz_loss,
            vmax,
            kmich,
            khalf,
            enz_target,
        )
        grown = grow(bio, share, mono_w, uptake_rate, keep)
        padded = extended(grown, (("space", 1),), 2)
        bio = spread(padded, disperse, offsets, rows)
    return (bio, enzymes, substrates, monomers)


def solution(mesh):
    placed = (
        P("taxa", "space", None),
        P(None, "space", None),
        P(None, "space", None),
        P(None, "space", None),
        P("taxa", None),
        P("taxa", None),
        P(),
        P("taxa"),
        P("taxa"),
        P("taxa"),
        P("taxa"),
        P(),
        P(),
        P(),
        P(),
        P(),
    )
    return jax.shard_map(
        body,
        mesh=mesh,
        in_specs=placed,
        out_specs=(
            P("taxa", "space", None),
            P(None, "space", None),
            P(None, "space", None),
            P(None, "space", None),
        ),
        check_vma=False,
    )
```

profile of v0, /device:TPU:0, one launch (start us, length us, event | category | flops | bytes accessed | tf_op | source)
XLA Modules:
  0.0 287.0 jit_solution(10821046505881652321)
XLA Ops:
  7.2 4.2 %copy.41 = f32[64,8,8,256]{3,1,2,0:T(8,128)S(1)} copy(f32[64,8,8,256]{3,2,1,0:T(8,128)} %bitcast.63) | data formatting | bytes 8388608
  11.4 2.1 fusion.50
  13.5 2.5 fusion.42
  16.3 0.9 copy.31
  17.4 5.4 %copy.35 = f32[512,8,256]{0,2,1:T(8,128)} copy(f32[512,8,256]{2,1,0:T(8,128)} %param.18) | data formatting | bytes 8388608 | tf_op args[0]
  22.8 30.3 %all-reduce.5.cloned.1.call-done = f32[54,8,256]{2,0,1:T(8,128)} async-done(((f32[54,8,256]{2,0,1:T(8,128)}), f32[54,8,256]{2,0,1:T(8,128)}) %all-reduce.5.cloned.1.call-update) | async-done | bytes 442384 | tf_op jit(solution)/shard_map/psum | solution.py:52
  53.1 1.4 fusion.35
  54.5 0.9 copy_subtract_fusion
  55.4 7.1 %bitcast_multiply_fusion.1 = f32[512,8,256]{0,2,1:T(8,128)S(1)} fusion(f32[512,8,256]{0,2,1:T(8,128)} %copy.35, f32[512]{0:T(512)S(1)} %get-tuple-element.56, f32[512]{0:T(512)S(1)} %get-tuple-element.55, s32[512,14]{0,1:T(8,128)S(1)} %copy-done.6, f32[54,8,256]{2,0,1:T(8,128)} %all-reduce.5.cloned.1.call-done, f32[14]{0:T(128)S(1)} %copy-done.15, ...), kind=kOutput, calls=%fused_computation.71 | convolution fusion | flops 179428352 | bytes 8765496 | tf_op jit(solution)/shard_map/tm,mrw->trw/dot_general | solution.py:57
  62.5 2.0 copy-done.1
  64.7 1.5 collective-permute-start
  66.2 3.2 %collective-permute-start.1 = (f32[512,2,256]{0,2,1:T(8,128)S(1)}, f32[512,2,256]{0,2,1:T(8,128)}, u32[]{:S(2)}, u32[]{:S(2)}) collective-permute-start(f32[512,2,256]{0,2,1:T(8,128)S(1)} %get-tuple-element.34), channel_id=1, source_target_pairs={{4,0},{8,4},{12,8},{16,12},{20,16},{24,20},{28,24},{0,28},{5,1},{9... | collective-permute-start | bytes 3145736 | tf_op jit(solution)/shard_map/ppermute | solution.py:23
  95.8 14.2 %collective-permute-done = f32[512,2,256]{0,2,1:T(8,128)S(1)} collective-permute-done((f32[512,2,256]{0,2,1:T(8,128)S(1)}, f32[512,2,256]{0,2,1:T(8,128)S(1)}, u32[]{:S(2)}, u32[]{:S(2)}) %collective-permute-start) | collective-permute-done | bytes 1048608 | tf_op jit(solution)/shard_map/ppermute | solution.py:20
  110.0 2.3 collective-permute-done.1
  112.3 3.0 %maximum_multiply_fusion = f32[512,12,256]{0,2,1:T(8,128)S(1)} fusion(f32[512,2,256]{0,2,1:T(8,128)} %collective-permute-done.1, f32[512,8,256]{0,2,1:T(8,128)} %copy-done.1, f32[512,2,256]{0,2,1:T(8,128)S(1)} %collective-permute-done, f32[512]{0:T(512)S(1)} %copy-done.12), kind=kLoop, calls=%fused_computation.32 | loop fusion | flops 4718592 | bytes 12584960 | tf_op jit(solution)/shard_map/mul | solution.py:63
  115.3 12.3 %constant_dynamic-slice_fusion.15 = (f32[512,8,256]{0,2,1:T(8,128)}, f32[512,8,256]{0,2,1:T(8,128)}, f32[512,8,256]{0,2,1:T(8,128)}, f32[512,8,256]{0,2,1:T(8,12...) fusion(f32[512,12,256]{0,2,1:T(8,128)S(1)} %maximum_multiply_fusion, ...), kind=kLoop, calls=%fused_computation.124 | loop fusion | bytes 67108896 | tf_op jit(solution)/shard_map/dynamic_slice | solution.py:67
  127.6 16.6 %fusion = f32[512,8,256]{0,2,1:T(8,128)S(1)} fusion(f32[512,8,256]{0,2,1:T(8,128)} %copy-done.1, s32[]{:T(128)S(6)} %select_n.95, f32[512,8,256]{0,2,1:T(8,128)} %get-tuple-element.24, s32[]{:T(128)S(6)} %select_n.93, f32[512,8,256]{0,2,1:T(8,128)} %get-tuple-element.25, s32[]{:T(128)S(6)} %select_n.91, f32[512,8,256]{0,2,1:T(8,128)} %get-tuple-element.26, ...), kind=kLoop, calls=%fused_computation.36 | loop fusion | flops 19922944 | bytes 41945120 | tf_op jit(solution)/shard_map/add | solution.py:69
  144.2 3.5 %fusion.49 = f32[14,2048]{1,0:T(8,128)S(1)} fusion(f32[512,2048]{0,1:T(8,128)S(1)} %bitcast.59, s32[512,14]{0,1:T(8,128)S(1)} %copy-done.6, f32[512]{0:T(512)S(1)} %copy-done.13), kind=kOutput, calls=%fused_computation.105 | convolution fusion | flops 176175104 | bytes 4339712 | tf_op jit(solution)/shard_map/dot_general | solution.py:50
  147.8 4.0 %fusion.41 = f32[40,2048]{1,0:T(8,128)S(1)} fusion(f32[512,2048]{0,1:T(8,128)S(1)} %bitcast.60, s32[512,40]{0,1:T(8,128)S(1)} %copy-done.4, f32[512]{0:T(512)S(1)} %copy-done.14), kind=kOutput, calls=%fused_computation.96 | convolution fusion | flops 503357440 | bytes 4605952 | tf_op jit(solution)/shard_map/dot_general | solution.py:49
  152.0 0.9 copy.36
  152.9 32.7 %all-reduce.7.cloned.1.call-done = f32[54,8,256]{2,0,1:T(8,128)} async-done(((f32[54,8,256]{2,0,1:T(8,128)}), f32[54,8,256]{2,0,1:T(8,128)}) %all-reduce.7.cloned.1.call-update) | async-done | bytes 442384 | tf_op jit(solution)/shard_map/psum | solution.py:52
  185.6 1.1 slice_add_fusion
  187.4 1.0 multiply_subtract_fusion.2
  188.4 7.2 %bitcast_multiply_fusion = f32[512,8,256]{0,2,1:T(8,128)S(1)} fusion(f32[512,8,256]{0,2,1:T(8,128)} %copy-done, f32[512]{0:T(512)S(1)} %get-tuple-element.56, f32[512]{0:T(512)S(1)} %get-tuple-element.55, s32[512,14]{0,1:T(8,128)S(1)} %copy-done.6, f32[14,8,256]{2,0,1:T(8,128)S(1)} %get-tuple-element.14, f32[54,8,256]{2,0,1:T(8,128)} %all-reduce.7.cloned.1.call-done, ...), kind=kOutput, calls=%fused_computation.70 | convolution fusion | flops 179399680 | bytes 8667192 | tf_op jit(solution)/shard_map/tm,mrw->trw/dot_general | solution.py:57
  195.8 1.5 collective-permute-start.2
  197.3 3.3 %collective-permute-start.3 = (f32[512,2,256]{0,2,1:T(8,128)S(1)}, f32[512,2,256]{0,2,1:T(8,128)S(1)}, u32[]{:S(2)}, u32[]{:S(2)}) collective-permute-start(f32[512,2,256]{0,2,1:T(8,128)S(1)} %get-tuple-element.32), channel_id=1, source_target_pairs={{4,0},{8,4},{12,8},{16,12},{20,16},{24,20},{28,24},{0,28},{5,1},{9... | collective-permute-start | bytes 3145736 | tf_op jit(solution)/shard_map/ppermute | solution.py:23
  202.8 38.3 %collective-permute-done.2 = f32[512,2,256]{0,2,1:T(8,128)S(1)} collective-permute-done((f32[512,2,256]{0,2,1:T(8,128)S(1)}, f32[512,2,256]{0,2,1:T(8,128)S(1)}, u32[]{:S(2)}, u32[]{:S(2)}) %collective-permute-start.2) | collective-permute-done | bytes 1048608 | tf_op jit(solution)/shard_map/ppermute | solution.py:20
  241.1 2.2 collective-permute-done.3
  243.3 0.8 maximum_multiply_fusion.1
  244.2 12.3 %constant_dynamic-slice_fusion.7 = (f32[512,8,256]{0,2,1:T(8,128)}, f32[512,8,256]{0,2,1:T(8,128)}, f32[512,8,256]{0,2,1:T(8,128)}, f32[512,8,256]{0,2,1:T(8,128...) fusion(f32[512,12,256]{0,2,1:T(8,128)S(1)} %maximum_multiply_fusion.1,, ...), kind=kLoop, calls=%fused_computation.116 | loop fusion | bytes 67108896 | tf_op jit(solution)/shard_map/dynamic_slice | solution.py:67
  256.4 18.3 %fusion.1 = f32[512,8,256]{0,2,1:T(8,128)} fusion(f32[512,8,256]{0,2,1:T(8,128)} %copy-done.2, s32[]{:T(128)S(6)} %select_n.95, f32[512,8,256]{0,2,1:T(8,128)} %get-tuple-element.16, s32[]{:T(128)S(6)} %select_n.93, f32[512,8,256]{0,2,1:T(8,128)} %get-tuple-element.17, s32[]{:T(128)S(6)} %select_n.91, f32[512,8,256]{0,2,1:T(8,128)} %get-tuple-element.18, ...), kind=kLoop, calls=%fused_computation.37 | loop fusion | flops 19922944 | bytes 41945120 | tf_op jit(solution)/shard_map/add | solution.py:69
  274.7 5.4 %copy.37 = f32[512,8,256]{2,1,0:T(8,128)} copy(f32[512,8,256]{0,2,1:T(8,128)} %fusion.1) | data formatting | bytes 8388608
  (62 shorter events, 4.7 us)
Async XLA Ops:
  7.2 46.0 %all-reduce.5.cloned.1.call-start = ((), (), s32[]{:S(2)}) async-start(), calls=%async_computation | async-start | bytes 917504 | tf_op jit(solution)/shard_map/psum | solution.py:52
  7.2 4.2 %copy-start.6 = (s32[512,14]{0,1:T(8,128)S(1)}, s32[512,14]{0,1:T(8,128)}, u32[]{:S(2)}) copy-start(s32[512,14]{0,1:T(8,128)} %param.23) | copy-start | bytes 86020
  7.2 4.2 %copy-start.13 = (f32[512]{0:T(512)S(1)}, f32[512]{0:T(512)}, u32[]{:S(2)}) copy-start(f32[512]{0:T(512)} %param.26) | copy-start | bytes 6148
  11.4 2.1 copy-start.4
  11.4 2.1 copy-start.14
  17.2 168.4 %all-reduce.7.cloned.1.call-start = ((), (), s32[]{:S(2)}) async-start(), calls=%async_computation.1 | async-start | bytes 917504 | tf_op jit(solution)/shard_map/psum | solution.py:52
  17.3 5.5 %copy-start.17 = (f32[512]{0:T(512)S(1)}, f32[512]{0:T(512)}, u32[]{:S(2)}) copy-start(f32[512]{0:T(512)} %param.27) | copy-start | bytes 6148
  17.3 5.5 %copy-start.18 = (f32[40]{0:T(128)S(1)}, f32[40]{0:T(128)}, u32[]{:S(2)}) copy-start(f32[40]{0:T(128)} %param.29) | copy-start | bytes 484
  17.3 35.8 %copy-start.8 = (f32[40,8,256]{2,1,0:T(8,128)S(1)}, f32[40,8,256]{2,1,0:T(8,128)}, u32[]{:S(2)}) copy-start(f32[40,8,256]{2,1,0:T(8,128)} %param.19) | copy-start | bytes 983044
  17.3 35.8 %copy-start.10 = (f32[12,8,256]{2,1,0:T(8,128)S(1)}, f32[12,8,256]{2,1,0:T(8,128)}, u32[]{:S(2)}) copy-start(f32[12,8,256]{2,1,0:T(8,128)} %param.20) | copy-start | bytes 294916
  17.3 35.8 %copy-start.16 = (s32[40]{0:T(128)S(1)}, s32[40]{0:T(128)}, u32[]{:S(2)}) copy-start(s32[40]{0:T(128)} %param.24) | copy-start | bytes 484
  17.4 35.8 %copy-start.19 = (f32[40]{0:T(128)S(1)}, f32[40]{0:T(128)}, u32[]{:S(2)}) copy-start(f32[40]{0:T(128)} %param.31) | copy-start | bytes 484
  17.4 35.8 %copy-start.20 = (f32[40]{0:T(128)S(1)}, f32[40]{0:T(128)}, u32[]{:S(2)}) copy-start(f32[40]{0:T(128)} %param.30) | copy-start | bytes 484
  17.4 38.0 %copy-start.5 = (f32[14,8,256]{2,1,0:T(8,128)S(1)}, f32[14,8,256]{2,1,0:T(8,128)}, u32[]{:S(2)}) copy-start(f32[14,8,256]{2,1,0:T(8,128)} %param.21) | copy-start | bytes 344068
  17.4 38.0 %copy-start.15 = (f32[14]{0:T(128)S(1)}, f32[14]{0:T(128)}, u32[]{:S(2)}) copy-start(f32[14]{0:T(128)} %param.32) | copy-start | bytes 172
  62.5 2.0 copy-start.1
  64.5 5.0 %copy-start.11 = (s32[8,2]{0,1:T(2,128)S(1)}, s32[8,2]{0,1:T(2,128)}, u32[]{:S(2)}) copy-start(s32[8,2]{0,1:T(2,128)} %param.33) | copy-start | bytes 196
  64.5 47.8 %copy-start.12 = (f32[512]{0:T(512)S(1)}, f32[512]{0:T(512)}, u32[]{:S(2)}) copy-start(f32[512]{0:T(512)} %param.28) | copy-start | bytes 6148
  64.7 45.3 %collective-permute-start = (f32[512,2,256]{0,2,1:T(8,128)S(1)}, f32[512,2,256]{0,2,1:T(8,128)S(1)}, u32[]{:S(2)}, u32[]{:S(2)}) collective-permute-start(f32[512,2,256]{0,2,1:T(8,128)S(1)} %get-tuple-element.33), channel_id=1, source_target_pairs={{0,4},{4,8},{8,12},{12,16},{16,20},{20,24},{24,28},{28,0},{1,5},{5... | collective-permute-start | bytes 3145736 | tf_op jit(solution)/shard_map/ppermute | solution.py:20
  66.2 46.1 %collective-permute-start.1 = (f32[512,2,256]{0,2,1:T(8,128)S(1)}, f32[512,2,256]{0,2,1:T(8,128)}, u32[]{:S(2)}, u32[]{:S(2)}) collective-permute-start(f32[512,2,256]{0,2,1:T(8,128)S(1)} %get-tuple-element.34), channel_id=1, source_target_pairs={{4,0},{8,4},{12,8},{16,12},{20,16},{24,20},{28,24},{0,28},{5,1},{9... | collective-permute-start | bytes 3145736 | tf_op jit(solution)/shard_map/ppermute | solution.py:23
  144.2 7.6 %copy-start = (f32[512,8,256]{0,2,1:T(8,128)}, f32[512,8,256]{0,2,1:T(8,128)S(1)}, u32[]{:S(2)}) copy-start(f32[512,8,256]{0,2,1:T(8,128)S(1)} %fusion) | copy-start | bytes 12582916
  147.7 37.9 %copy-start.3 = (f32[54,8,256]{2,0,1:T(8,128)S(1)}, f32[54,8,256]{2,0,1:T(8,128)}, u32[]{:S(2)}) copy-start(f32[54,8,256]{2,0,1:T(8,128)} %all-reduce.5.cloned.1.call-done) | copy-start | bytes 1327108
  147.7 37.9 %copy-start.9 = (f32[40,8,256]{2,1,0:T(8,128)S(1)}, f32[40,8,256]{2,1,0:T(8,128)}, u32[]{:S(2)}) copy-start(f32[40,8,256]{2,1,0:T(8,128)} %param.19) | copy-start | bytes 983044
  147.7 39.0 %copy-start.7 = (f32[12,8,256]{2,0,1:T(8,128)S(1)}, f32[12,8,256]{2,0,1:T(8,128)}, u32[]{:S(2)}) copy-start(f32[12,8,256]{2,0,1:T(8,128)} %get-tuple-element.52) | copy-start | bytes 294916
  195.6 47.7 %copy-start.2 = (f32[512,8,256]{0,2,1:T(8,128)}, f32[512,8,256]{0,2,1:T(8,128)S(1)}, u32[]{:S(2)}) copy-start(f32[512,8,256]{0,2,1:T(8,128)S(1)} %bitcast_multiply_fusion) | copy-start | bytes 12582916
  195.8 45.3 %collective-permute-start.2 = (f32[512,2,256]{0,2,1:T(8,128)S(1)}, f32[512,2,256]{0,2,1:T(8,128)S(1)}, u32[]{:S(2)}, u32[]{:S(2)}) collective-permute-start(f32[512,2,256]{0,2,1:T(8,128)S(1)} %get-tuple-element.31), channel_id=1, source_target_pairs={{0,4},{4,8},{8,12},{12,16},{16,20},{20,24},{24,28},{28,0},{1,5},{5... | collective-permute-start | bytes 3145736 | tf_op jit(solution)/shard_map/ppermute | solution.py:20
  197.3 46.0 %collective-permute-start.3 = (f32[512,2,256]{0,2,1:T(8,128)S(1)}, f32[512,2,256]{0,2,1:T(8,128)S(1)}, u32[]{:S(2)}, u32[]{:S(2)}) collective-permute-start(f32[512,2,256]{0,2,1:T(8,128)S(1)} %get-tuple-element.32), channel_id=1, source_target_pairs={{4,0},{8,4},{12,8},{16,12},{20,16},{24,20},{28,24},{0,28},{5,1},{9... | collective-permute-start | bytes 3145736 | tf_op jit(solution)/shard_map/ppermute | solution.py:23
Sparse Core Ops, SparseCore 0:
  17.3 35.7 all-reduce.4
  153.0 32.4 all-reduce.6
where the time goes:
time: 288 us; the launch traced here: 287 us
  waiting for transfers between devices  120 us (42%)
  local copies, waits for them, and re-layouts  47.1 us (16%)
  other arithmetic  41 us (14%)
  between operations  40 us (14%)
  matrix products  29.2 us (10%)
  starting transfers between devices  9.63 us (3%)
    psum x2, waiting for transfers between devices, pool_update(): sums = lax.psum(local, 'taxa')  63 us
    ppermute x2, waiting for transfers between devices, extended(): lax.ppermute(lax.slice_in_dim(block, block.shape[dim] - width, None, axis...  52.5 us
    add x2, other arithmetic, spread(): return centre - centre * fraction + total / KOFF  34.8 us
    dynamic_slice x2, local copies, waits for them, and re-layouts, spread(): piece = lax.dynamic_slice_in_dim(moved_pad, 2 - offsets[k, 0], rows, 1)  24.5 us
    unnamed x50, local copies, waits for them, and re-layouts  19.6 us
    dot_general x2, matrix products, grow(): gain = jnp.einsum('tm,mrw->trw', mono_w, share, precision=HIGH)  14.2 us
    dot_general x2, matrix products, pool_update(): jnp.dot(prod_w.T, flat, precision=HIGH, preferred_element_type=jnp.float32)  6.51 us
    ppermute x2, starting transfers between devices, extended(): lax.ppermute(lax.slice_in_dim(block, 0, width, axis=dim), axis, backward)  6.5 us
  transfers between devices with their start and end apart: 6, of which 6 were waited for; matrix products, arithmetic and copies ran while one was open for 3% of the time, Pallas kernels for 0%

commit v1 on v0

v1 whole, which is shorter than its diff:
```python
import jax
import jax.numpy as jnp
from jax import lax
from jax.experimental import pallas as pl
from jax.experimental.pallas import tpu as pltpu
from jax.sharding import PartitionSpec as P

KOFF = 8
YIELD = 0.6
HALF = 128
CHUNK = 32
SLOTS = 16
CHAN = 56
PADDED = 64
F32 = jnp.float32
BF16 = jnp.bfloat16
ANY = pl.BlockSpec(memory_space=pl.ANY)
SMEM = pl.BlockSpec(memory_space=pltpu.SMEM)
VMEM_BYTES = 40 << 20


def params():
    return pltpu.CompilerParams(vmem_limit_bytes=VMEM_BYTES)


def cost(flops, moved):
    return pl.CostEstimate(flops=flops, bytes_accessed=moved, transcendentals=0)


def pieces_outside(x, count):
    out = []
    for _ in range(count):
        part = lax.reduce_precision(x, 8, 7)
        out.append(part.astype(BF16))
        x = x - part
    return out


def pieces_inside(x, count):
    out = []
    for _ in range(count):
        part = x.astype(BF16)
        out.append(part)
        x = x - part.astype(F32)
    return out


def share_operand(share):
    high, mid, low = pieces_inside(share, 3)
    return jnp.concatenate([high, mid, low, high, mid, high], 0)


def trait_operand(matrix):
    high, mid, low = pieces_outside(matrix, 3)
    return jnp.concatenate([high, high, high, mid, mid, low], 1)


def matmul(a, b):
    return jnp.dot(a, b, preferred_element_type=F32)


def take_rows(biomass, rows):
    count, _, width = biomass.shape
    pairs = len(rows) // 2

    def kernel(source, *refs):
        outs, sem = refs[:-1], refs[-1]
        copies = [
            pltpu.make_async_copy(source.at[:, row, :], outs[i // 2].at[i % 2], sem.at[i])
            for i, row in enumerate(rows)
        ]
        for copy in copies:
            copy.start()
        for copy in copies:
            copy.wait()

    return pl.pallas_call(
        kernel,
        name="take_rows",
        out_shape=[jax.ShapeDtypeStruct((2, count, width), F32)] * pairs,
        in_specs=[ANY],
        out_specs=[ANY] * pairs,
        scratch_shapes=[pltpu.SemaphoreType.DMA((len(rows),))],
        compiler_params=params(),
        cost_estimate=cost(0, 8 * len(rows) * count * width),
    )(biomass)


def add_sums(total, row, x, weights):
    high, low = pieces_inside(x, 2)
    first = matmul(weights, high)
    second = matmul(weights[:PADDED], low)
    total[row] += first[:PADDED] + first[PADDED:] + second


def taxa_sums(row_pairs, weights, block):
    _, count, width = row_pairs[0].shape
    rows = 2 * len(row_pairs)

    def kernel(*refs):
        pairs, weight, out, total = refs[: len(row_pairs)], refs[-3], refs[-2], refs[-1]

        @pl.when(pl.program_id(0) == 0)
        def _():
            total[...] = jnp.zeros_like(total)

        for row in range(rows):
            add_sums(total, row, pairs[row // 2][row % 2], weight[...])

        @pl.when(pl.program_id(0) == pl.num_programs(0) - 1)
        def _():
            out[...] = jnp.swapaxes(total[:, :CHAN, :], 0, 1)

    return pl.pallas_call(
        kernel,
        name="taxa_sums",
        grid=(count // block,),
        out_shape=jax.ShapeDtypeStruct((CHAN, rows, width), F32),
        in_specs=[pl.BlockSpec((2, block, width), lambda i: (0, i, 0))] * len(row_pairs)
        + [pl.BlockSpec((2 * PADDED, block), lambda i: (0, i))],
        out_specs=pl.BlockSpec((CHAN, rows, width), lambda i: (0, 0, 0)),
        scratch_shapes=[pltpu.VMEM((rows, PADDED, width), F32)],
        compiler_params=params(),
        cost_estimate=cost(6 * CHAN * count * rows * width, 4 * count * rows * width),
    )(*row_pairs, weights)


def cell_update(sums, enz, sub, mono, enz_loss, vmax, kmich, khalf, enz_target):
    n_enz, rows, width = enz.shape
    n_sub, n_mono = sub.shape[0], mono.shape[0]

    def kernel(sums, enz, sub, mono, loss, vmax, kmich, khalf, target, pool, left, mono_two, out, rate, share):
        rate[...] = jnp.zeros_like(rate)

        def enzyme(e, carry):
            now = enz[e] * (1.0 - loss[e]) + sums[e]
            pool[e] = now
            at = target[e]
            rate[at] += vmax[e] * now / (kmich[e] + sub[at])
            return carry

        lax.fori_loop(0, n_enz, enzyme, 0)

        def finish(m, mono_one):
            demand = sums[n_enz + m]
            part = mono_one / (khalf[m] + demand + mono_one)
            mono_two[m] = mono_one - demand * part
            share[m] = part

        def substrate(s, carry):
            rest = sub[s] * jnp.exp(-rate[s])
            left[s] = rest
            finish(s, mono[s] + (sub[s] - rest))
            return carry

        lax.fori_loop(0, n_sub, substrate, 0)
        for m in range(n_sub, n_mono):
            finish(m, mono[m])
        share[n_mono] = jnp.ones((rows, width), F32)
        for m in range(n_mono + 1, SLOTS):
            share[m] = jnp.zeros((rows, width), F32)
        out[...] = jnp.swapaxes(share[...], 0, 1)

    whole = pl.BlockSpec(memory_space=pltpu.VMEM)
    return pl.pallas_call(
        kernel,
        name="cell_update",
        out_shape=[
            jax.ShapeDtypeStruct(enz.shape, F32),
            jax.ShapeDtypeStruct(sub.shape, F32),
            jax.ShapeDtypeStruct(mono.shape, F32),
            jax.ShapeDtypeStruct((rows, SLOTS, width), F32),
        ],
        in_specs=[whole] * 4 + [SMEM] * 5,
        out_specs=[whole] * 4,
        scratch_shapes=[pltpu.VMEM(sub.shape, F32), pltpu.VMEM((SLOTS, rows, width), F32)],
        compiler_params=params(),
        cost_estimate=cost(20 * n_enz * rows * width, 8 * 2 * n_enz * rows * width),
    )(sums, enz, sub, mono, enz_loss, vmax, kmich, khalf, enz_target)


def lanes():
    return lax.broadcasted_iota(jnp.int32, (CHUNK, HALF), 1)


def shifted(ref, row, taxa, by, lane):
    first = pltpu.roll(ref[row, taxa, :HALF], jnp.where(by < 0, by + HALF, by), 1)
    second = pltpu.roll(ref[row, taxa, HALF:], jnp.where(by < 0, by + HALF, by), 1)
    crossed = (lane < by) | (lane >= HALF + by)
    return jnp.where(crossed, second, first), jnp.where(crossed, first, second)


def full_stencil(moved, result, offsets, rows, first_row, block):
    lane = lanes()
    steps = block // CHUNK

    def body(i, carry):
        row = i // steps
        taxa = pl.ds(pl.multiple_of((i % steps) * CHUNK, CHUNK), CHUNK)
        left = result[row, taxa, :HALF]
        right = result[row, taxa, HALF:]
        for k in range(KOFF):
            a, b = shifted(moved, row + first_row - offsets[k, 0], taxa, offsets[k, 1], lane)
            left += a
            right += b
        result[row, taxa, :HALF] = left
        result[row, taxa, HALF:] = right
        return carry

    lax.fori_loop(0, rows * steps, body, 0)


def day_one(row_pairs, low, high, share, share_low, share_high, to_moved, to_kept, weights, offsets, block):
    _, count, width = low.shape
    rows = 2 * len(row_pairs)
    ext = rows + 4

    def kernel(*refs):
        pairs = refs[: len(row_pairs) + 2]
        own, before, after, moved_w, kept_w, weight, offs, out, sums, moved, total = refs[len(row_pairs) + 2 :]

        @pl.when(pl.program_id(0) == 0)
        def _():
            total[...] = jnp.zeros_like(total)
            for row in (0, 1, ext + 2, ext + 3):
                moved[row] = jnp.zeros((block, width), F32)

        for row in range(ext):
            x = pairs[row // 2][row % 2]
            if row < 2:
                part = before[2 + row]
            elif row < 2 + rows:
                part = own[row - 2]
            else:
                part = after[row - 2 - rows]
            part = share_operand(part)
            moved[row + 2] = x * matmul(moved_w[...], part)
            out[row] = x * matmul(kept_w[...], part)
        full_stencil(moved, out, offs, ext, 2, block)

        def add(row, carry):
            add_sums(total, row, out[row + 2], weight[...])
            return carry

        lax.fori_loop(0, rows, add, 0)

        @pl.when(pl.program_id(0) == pl.num_programs(0) - 1)
        def _():
            sums[...] = jnp.swapaxes(total[:, :CHAN, :], 0, 1)

    def whole(shape):
        return pl.BlockSpec(shape, lambda i: (0,) * len(shape))

    operand = to_moved.shape[1]
    return pl.pallas_call(
        kernel,
        name="day_one",
        grid=(count // block,),
        out_shape=[
            jax.ShapeDtypeStruct((ext, count, width), F32),
            jax.ShapeDtypeStruct((CHAN, rows, width), F32),
        ],
        in_specs=[pl.BlockSpec((2, block, width), lambda i: (0, i, 0))] * (len(row_pairs) + 2)
        + [
            whole(share.shape),
            whole(share_low.shape),
            whole(share_high.shape),
            pl.BlockSpec((block, operand), lambda i: (i, 0)),
            pl.BlockSpec((block, operand), lambda i: (i, 0)),
            pl.BlockSpec((2 * PADDED, block), lambda i: (0, i)),
            SMEM,
        ],
        out_specs=[
            pl.BlockSpec((ext, block, width), lambda i: (0, i, 0)),
            whole((CHAN, rows, width)),
        ],
        scratch_shapes=[
            pltpu.VMEM((ext + 4, block, width), F32),
            pltpu.VMEM((rows, PADDED, width), F32),
        ],
        compiler_params=params(),
        cost_estimate=cost(60 * count * ext * width, 8 * count * ext * width),
    )(low, *row_pairs, high, share, share_low, share_high, to_moved, to_kept, weights, offsets)


def day_two(grown, share, to_moved, to_kept, offsets, block):
    ext, count, width = grown.shape
    rows = ext - 4
    steps = count // block

    def kernel(x, own, moved_w, kept_w, offs, out, edge, moved, result, sem):
        step = pl.program_id(0)
        slot = lax.rem(step, 2)

        def copies(at, where):
            found = []
            taxa = pl.ds(pl.multiple_of(at * block, block), block)
            for row in range(rows):
                if 2 <= row < rows - 2:
                    target = out.at[taxa, row, :]
                else:
                    target = edge.at[row if row < 2 else row - rows + 4, taxa, :]
                found.append(pltpu.make_async_copy(result.at[where, row], target, sem.at[where, row]))
            return found

        @pl.when(step == 0)
        def _():
            for row in (0, 1, ext - 2, ext - 1):
                moved[row] = jnp.zeros((block, width), F32)

        @pl.when(step >= 2)
        def _():
            for copy in copies(step - 2, slot):
                copy.wait()

        for row in range(rows):
            part = share_operand(own[row])
            value = x[row + 2]
            moved[row + 2] = value * matmul(moved_w[...], part)
            result[slot, row] = value * matmul(kept_w[...], part)
        full_stencil(moved, result.at[slot], offs, rows, 2, block)
        for copy in copies(step, slot):
            copy.start()

        @pl.when(step == steps - 1)
        def _():
            if steps > 1:
                for copy in copies(step - 1, 1 - slot):
                    copy.wait()
            for copy in copies(step, slot):
                copy.wait()

    operand = to_moved.shape[1]
    return pl.pallas_call(
        kernel,
        name="day_two",
        grid=(steps,),
        out_shape=[
            jax.ShapeDtypeStruct((count, rows, width), F32),
            jax.ShapeDtypeStruct((4, count, width), F32),
        ],
        in_specs=[
            pl.BlockSpec((ext, block, width), lambda i: (0, i, 0)),
            pl.BlockSpec(share.shape, lambda i: (0, 0, 0)),
            pl.BlockSpec((block, operand), lambda i: (i, 0)),
            pl.BlockSpec((block, operand), lambda i: (i, 0)),
            SMEM,
        ],
        out_specs=[ANY, ANY],
        scratch_shapes=[
            pltpu.VMEM((ext, block, width), F32),
            pltpu.VMEM((2, rows, block, width), F32),
            pltpu.SemaphoreType.DMA((2, rows)),
        ],
        compiler_params=params(),
        cost_estimate=cost(60 * count * rows * width, 8 * count * rows * width),
    )(grown, share, to_moved, to_kept, offsets)


def edges(outer_low, outer_high, grown, edge, biomass_out, day_one_share, day_two_share, to_moved, offsets, block):
    _, count, width = outer_low.shape
    rows = biomass_out.shape[1]
    last = grown.shape[0] // 2 - 1
    steps = count // block
    chunks = block // CHUNK

    def kernel(low, high, near_low, near_high, own, s1, s2, moved_w, offs, unused, out, far, near, result, lists, counts, sem):
        step = pl.program_id(0)
        slot = lax.rem(step, 2)
        lane = lanes()

        @pl.when(step == 0)
        def _():
            for i in range(4):
                counts[i] = 0
            for k in range(KOFF):
                for i, value in enumerate((2, 1, -1, -2)):

                    @pl.when(offs[k, 0] == value)
                    def _():
                        lists[i, counts[i]] = offs[k, 1]
                        counts[i] = counts[i] + 1

        def copies(at, where):
            taxa = pl.ds(pl.multiple_of(at * block, block), block)
            return [
                pltpu.make_async_copy(
                    result.at[where, i],
                    out.at[taxa, i if i < 2 else rows - 4 + i, :],
                    sem.at[where, i],
                )
                for i in range(4)
            ]

        @pl.when(step >= 2)
        def _():
            for copy in copies(step - 2, slot):
                copy.wait()

        for i in range(4):
            x = low[i] if i < 2 else high[i - 2]
            far[i] = x * matmul(moved_w[...], share_operand(s1[i]))

        def gather(ref, row, which, taxa, pair):
            def body(k, carry):
                a, b = shifted(ref, row, taxa, lists[which, k], lane)
                return carry[0] + a, carry[1] + b

            return lax.fori_loop(0, counts[which], body, pair)

        def sides(source, base, target, terms):
            def body(i, carry):
                taxa = pl.ds(pl.multiple_of(i * CHUNK, CHUNK), CHUNK)
                for row, parts in enumerate(terms):
                    pair = base(row, taxa)
                    for origin, which in parts:
                        pair = gather(source, origin, which, taxa, pair)
                    target(row, taxa, pair)
                return carry

            lax.fori_loop(0, chunks, body, 0)

        def near_base(row, taxa):
            ref = near_low if row < 2 else near_high
            return ref[row % 2, taxa, :HALF], ref[row % 2, taxa, HALF:]

        def near_store(row, taxa, pair):
            near[row, taxa, :HALF] = pair[0]
            near[row, taxa, HALF:] = pair[1]

        def own_base(row, taxa):
            return own[row, taxa, :HALF], own[row, taxa, HALF:]

        def own_store(row, taxa, pair):
            result[slot, row, taxa, :HALF] = pair[0]
            result[slot, row, taxa, HALF:] = pair[1]

        two, one, minus_one, minus_two = range(4)
        terms = (
            ((0, two), (1, one)),
            ((1, two),),
            ((2, minus_two),),
            ((3, minus_two), (2, minus_one)),
        )
        sides(far, near_base, near_store, terms)
        for i in range(4):
            near[i] = near[i] * matmul(moved_w[...], share_operand(s2[i]))
        sides(near, own_base, own_store, terms)
        for copy in copies(step, slot):
            copy.start()

        @pl.when(step == steps - 1)
        def _():
            if steps > 1:
                for copy in copies(step - 1, 1 - slot):
                    copy.wait()
            for copy in copies(step, slot):
                copy.wait()

    operand = to_moved.shape[1]
    pair = (2, block, width)
    return pl.pallas_call(
        kernel,
        name="edges",
        grid=(steps,),
        out_shape=jax.ShapeDtypeStruct(biomass_out.shape, F32),
        in_specs=[
            pl.BlockSpec(pair, lambda i: (0, i, 0)),
            pl.BlockSpec(pair, lambda i: (0, i, 0)),
            pl.BlockSpec(pair, lambda i: (0, i, 0)),
            pl.BlockSpec(pair, lambda i: (last, i, 0)),
            pl.BlockSpec((4, block, width), lambda i: (0, i, 0)),
            pl.BlockSpec(day_one_share.shape, lambda i: (0, 0, 0)),
            pl.BlockSpec(day_two_share.shape, lambda i: (0, 0, 0)),
            pl.BlockSpec((block, operand), lambda i: (i, 0)),
            SMEM,
            ANY,
        ],
        out_specs=ANY,
        scratch_shapes=[
            pltpu.VMEM((4, block, width), F32),
            pltpu.VMEM((4, block, width), F32),
            pltpu.VMEM((2, 4, block, width), F32),
            pltpu.SMEM((4, KOFF), jnp.int32),
            pltpu.SMEM((4,), jnp.int32),
            pltpu.SemaphoreType.DMA((2, 4)),
        ],
        input_output_aliases={9: 0},
        compiler_params=params(),
        cost_estimate=cost(60 * count * 4 * width, 8 * count * 8 * width),
    )(outer_low, outer_high, grown, grown, edge, day_one_share, day_two_share, to_moved, offsets, biomass_out)


def over_taxa(value):
    count = lax.axis_size("taxa")
    step = 1
    while step < count:
        value = value + lax.ppermute(value, "taxa", [(i, i ^ step) for i in range(count)])
        step *= 2
    return value


def body(
    biomass,
    enzymes,
    substrates,
    monomers,
    enz_traits,
    mono_traits,
    enz_target,
    prod_rate,
    uptake_rate,
    mortality,
    disperse,
    enz_loss,
    vmax,
    kmich,
    khalf,
    offsets,
):
    ring = lax.axis_size("space")
    forward = [(i, (i + 1) % ring) for i in range(ring)]
    backward = [(target, source) for source, target in forward]

    def down(x):
        return lax.ppermute(x, "space", forward)

    def up(x):
        return lax.ppermute(x, "space", backward)

    count, rows, width = biomass.shape
    block = min(count, 256)

    first, last = take_rows(biomass, (0, 1, rows - 2, rows - 1))
    inner_low, inner_high = down(last), up(first)
    middle = take_rows(biomass, tuple(range(2, rows - 2)))
    row_pairs = [first, *middle, last]

    enz_f = enz_traits.astype(F32)
    mono_f = mono_traits.astype(F32)
    weight = jnp.concatenate(
        [
            enz_f * prod_rate[:, None],
            mono_f * uptake_rate[:, None],
            jnp.zeros((count, PADDED - enz_f.shape[1] - mono_f.shape[1]), F32),
        ],
        1,
    ).T
    weights = jnp.concatenate(pieces_outside(weight, 2), 0)
    keep = 1.0 - mortality - prod_rate * jnp.sum(enz_f, axis=1)
    gain = jnp.concatenate(
        [
            (YIELD * uptake_rate)[:, None] * mono_f,
            keep[:, None],
            jnp.zeros((count, SLOTS - 1 - mono_f.shape[1]), F32),
        ],
        1,
    )
    to_moved = trait_operand(gain * (disperse / KOFF)[:, None])
    to_kept = trait_operand(gain * (1.0 - disperse)[:, None])
    cells = (enz_loss, vmax, kmich, khalf, enz_target)

    sums = over_taxa(taxa_sums(row_pairs, weights, block))
    enzymes, substrates, monomers, share_one = cell_update(sums, enzymes, substrates, monomers, *cells)
    share_low, share_high = down(share_one[rows - 4 :]), up(share_one[:4])

    inner_low, inner_high, outer_first, outer_last = lax.optimization_barrier(
        (inner_low, inner_high, middle[0], middle[-1])
    )
    outer_low, outer_high = down(outer_last), up(outer_first)
    grown, sums = day_one(
        row_pairs, inner_low, inner_high, share_one, share_low, share_high, to_moved, to_kept, weights, offsets, block
    )
    sums = over_taxa(sums)
    enzymes, substrates, monomers, share_two = cell_update(sums, enzymes, substrates, monomers, *cells)
    near_low, near_high = down(share_two[rows - 2 :]), up(share_two[:2])
    biomass_out, edge = day_two(grown, share_two, to_moved, to_kept, offsets, block)
    biomass_out = edges(
        outer_low,
        outer_high,
        grown,
        edge,
        biomass_out,
        jnp.concatenate([share_low[:2], share_high[2:]], 0),
        jnp.concatenate([near_low, near_high], 0),
        to_moved,
        offsets,
        min(count, 128),
    )
    return (biomass_out, enzymes, substrates, monomers)


def solution(mesh):
    placed = (
        P("taxa", "space", None),
        P(None, "space", None),
        P(None, "space", None),
        P(None, "space", None),
        P("taxa", None),
        P("taxa", None),
        P(),
        P("taxa"),
        P("taxa"),
        P("taxa"),
        P("taxa"),
        P(),
        P(),
        P(),
        P(),
        P(),
    )
    return jax.shard_map(
        body,
        mesh=mesh,
        in_specs=placed,
        out_specs=(
            P("taxa", "space", None),
            P(None, "space", None),
            P(None, "space", None),
            P(None, "space", None),
        ),
        check_vma=False,
    )
```

time: 288 us -> 180 us (0.62)
  Pallas kernels: 0 us -> 96.2 us
  waiting for transfers between devices: 120 us -> 41.8 us
  between operations: 40 us -> 1 us
  other arithmetic: 41 us -> 4.48 us
  local copies, waits for them, and re-layouts: 47.1 us -> 15.3 us
  matrix products: 29.2 us -> 0 us
  starting transfers between devices: 9.63 us -> 21 us
    pallas_call x0 -> x8, Pallas kernels: none -> 96.2 us  [the longest x1 33.5 us: day_one(): pl.pallas_call(kernel, name='day_one', grid=(count // block,), out_shape=...]
    psum x2 -> x0, waiting for transfers between devices: 63 us -> none  [pool_update(): sums = lax.psum(local, 'taxa')]
    add x3 -> x4, other arithmetic: 36 us -> 2.17 us  [over_taxa(): value + lax.ppermute(value, 'taxa', [(i, i ^ step) for i in range(count)])]
    dot_general x10 -> x0, matrix products: 29.2 us -> none  [the longest x2 14.2 us: grow(): gain = jnp.einsum('tm,mrw->trw', mono_w, share, precision=HIGH)]
    dynamic_slice x2 -> x0, local copies, waits for them, and re-layouts: 24.5 us -> none  [spread(): piece = lax.dynamic_slice_in_dim(moved_pad, 2 - offsets[k, 0], rows, 1)]
    ppermute x4 -> x12, waiting for transfers between devices: 57 us -> 41.8 us  [the longest x4 19.5 us: over_taxa(): lax.ppermute(value, 'taxa', [(i, i ^ step) for i in range(count)])]
    ppermute x4 -> x12, starting transfers between devices: 9.55 us -> 21 us  [the longest x4 13.8 us: up(): return lax.ppermute(x, 'space', backward)]
    unnamed x50 -> x51, local copies, waits for them, and re-layouts: 19.6 us -> 9.09 us
  transfers between devices with their start and end apart: 6 -> 12, of which waited for: 6 -> 7; matrix products, arithmetic and copies ran while one was open for 3% -> 6% of each run, Pallas kernels for 0% -> 14%
where the time goes in v1:
time: 180 us
  Pallas kernels  96.2 us (53%)
  waiting for transfers between devices  41.8 us (23%)
  starting transfers between devices  21 us (12%)
  local copies, waits for them, and re-layouts  15.3 us (8%)
  other arithmetic  4.48 us (2%)
    pallas_call x1, Pallas kernels, day_one(): pl.pallas_call(kernel, name='day_one', grid=(count // block,), out_shape=...  33.5 us
    pallas_call x1, Pallas kernels, edges(): pl.pallas_call(kernel, name='edges', grid=(steps,), out_shape=jax.ShapeDt...  32.4 us
    pallas_call x1, Pallas kernels, day_two(): pl.pallas_call(kernel, name='day_two', grid=(steps,), out_shape=[jax.Shap...  21.2 us
    ppermute x4, waiting for transfers between devices, over_taxa(): lax.ppermute(value, 'taxa', [(i, i ^ step) for i in range(count)])  19.5 us
    ppermute x4, waiting for transfers between devices, down(): return lax.ppermute(x, 'space', forward)  16.5 us
    ppermute x4, starting transfers between devices, up(): return lax.ppermute(x, 'space', backward)  13.8 us
    unnamed x51, local copies, waits for them, and re-layouts  9.09 us
    ppermute x4, waiting for transfers between devices, up(): return lax.ppermute(x, 'space', backward)  5.86 us
  transfers between devices with their start and end apart: 12, of which 7 were waited for; matrix products, arithmetic and copies ran while one was open for 6% of the time, Pallas kernels for 14%

profile of v1, /device:TPU:0, one launch (start us, length us, event | category | flops | bytes accessed | tf_op | source)
XLA Modules:
  0.0 179.8 jit_solution(3090776058601863163)
XLA Ops:
  0.6 2.2 %copy-done = f32[512,8,256]{2,1,0:T(8,128)S(1)} copy-done((f32[512,8,256]{2,1,0:T(8,128)S(1)}, f32[512,8,256]{2,1,0:T(8,128)}, u32[]{:S(2)}) %copy-start) | copy-done | bytes 4194328
  2.8 1.5 take_rows.3
  4.3 1.7 take_rows.2
  6.4 2.4 %taxa_sums.1 = f32[56,8,256]{2,1,0:T(8,128)S(1)} custom-call(f32[2,512,256]{2,1,0:T(8,128)S(1)} %get-tuple-element.25.refs_0_.refs_1_, f32[2,512,256]{2,1,0:T(8,128)S(1)} %get-tuple-element.29.refs_1_.refs_2_, f32[2,512,256]{2,1,0:T(8,128)S(1)} %get-tuple-element.28.refs_2_.refs_3_, f32[2,512,256]{2,1,0:T(8,128)} %get-tuple-element.24.refs_3_.refs_4_, ...), custom_call_target="tpu_custom_call" | custom-call | flops 352321536 | bytes 4194304 | tf_op jit(solution)/shard_map/taxa_sums/pallas_call | solution.py:114
  9.4 2.6 %collective-permute-start = (f32[2,512,256]{2,1,0:T(8,128)}, f32[2,512,256]{2,1,0:T(8,128)}, u32[]{:S(2)}, u32[]{:S(2)}) collective-permute-start(f32[2,512,256]{2,1,0:T(8,128)} %get-tuple-element.24.refs_3_.refs_4_), channel_id=1, source_target_pairs={{0,4},{4,8},{8,12},{12,16},{16,20},{20,24},{24,28},{28,0},{1,5},{5... | collective-permute-start | bytes 3145736 | tf_op jit(solution)/shard_map/ppermute | solution.py:526
  11.9 3.1 %collective-permute-start.1 = (f32[2,512,256]{2,1,0:T(8,128)S(1)}, f32[2,512,256]{2,1,0:T(8,128)}, u32[]{:S(2)}, u32[]{:S(2)}) collective-permute-start(f32[2,512,256]{2,1,0:T(8,128)S(1)} %get-tuple-element.25.refs_0_.refs_1_), channel_id=1, source_target_pairs={{4,0},{8,4},{12,8},{16,12},{20,16},{24,20},{28,24},{0,28},{5,1},{9... | collective-permute-start | bytes 3145736 | tf_op jit(solution)/shard_map/ppermute | solution.py:529
  15.1 0.8 add.12
  15.9 1.6 collective-permute-start.5
  17.7 0.8 copy.37
  18.5 10.2 %collective-permute-done.5 = f32[56,8,256]{2,1,0:T(8,128)} collective-permute-done((f32[56,8,256]{2,1,0:T(8,128)}, f32[56,8,256]{2,1,0:T(8,128)}, u32[]{:S(2)}, u32[]{:S(2)}) %collective-permute-start.5) | collective-permute-done | bytes 458784 | tf_op jit(solution)/shard_map/ppermute | solution.py:498
  28.7 1.2 add.13.sums
  30.0 1.0 copy-done.3
  31.0 0.9 copy-done.9
  31.9 1.4 cell_update.2
  36.0 1.7 collective-permute-start.7
  38.0 2.1 %fusion.3 = (bf16[512,16]{1,0:T(8,128)(2,1)}, bf16[512,16]{1,0:T(8,128)(2,1)}, bf16[512,16]{1,0:T(8,128)(2,1)}, bf16[512,16]{1,0:T(8,128)(2,1)}, bf16[512,16]{1,0:T(8,128)(2,1)}, /*index=5*/bf16[512,16]{1,0:T(8,128)(2,1)}) fusion(f32[512,16]{1,0:T(8,128)} %copy.37, f32[512]{0:T(512)S(1)} %get-tuple-element.63, f32[512]{0:T(512)S(1)} %get-tuple-element.64), kind=kLoop, calls=%fused_computation.11 | loop fusion | flops 147456 | bytes 135168 | tf_op jit(solution)/shard_map/convert_element_type | solution.py:34
  40.8 1.5 concatenate.25.refs_10_.kept_w
  42.3 1.5 concatenate.24.refs_9_.moved_w
  43.8 15.8 %collective-permute-done.refs_0_ = f32[2,512,256]{2,1,0:T(8,128)} collective-permute-done((f32[2,512,256]{2,1,0:T(8,128)}, f32[2,512,256]{2,1,0:T(8,128)}, u32[]{:S(2)}, u32[]{:S(2)}) %collective-permute-start) | collective-permute-done | bytes 1048608 | tf_op jit(solution)/shard_map/ppermute | solution.py:526
  59.6 2.2 %collective-permute-done.1.refs_5_ = f32[2,512,256]{2,1,0:T(8,128)} collective-permute-done((f32[2,512,256]{2,1,0:T(8,128)S(1)}, f32[2,512,256]{2,1,0:T(8,128)}, u32[]{:S(2)}, u32[]{:S(2)}) %collective-permute-start.1) | collective-permute-done | bytes 1048608 | tf_op jit(solution)/shard_map/ppermute | solution.py:529
  62.5 0.9 copy-done.2
  63.5 33.5 %day_one.1 = (f32[12,512,256]{2,1,0:T(8,128)S(1)}, f32[56,8,256]{2,1,0:T(8,128)S(1)}) custom-call(f32[2,512,256]{2,1,0:T(8,128)} %collective-permute-done.refs_0_, f32[2,512,256]{2,1,0:T(8,128)S(1)} %get-tuple-element.25.refs_0_.refs_1_, f32[2,512,256]{2,1,0:T(8,128)S(1)} %get-tuple-element.29.refs_1_.refs_2_, ...), custom_call_target="tpu_custom_call" | custom-call | flops 94371840 | bytes 12582912 | tf_op jit(solution)/shard_map/day_one/pallas_call | solution.py:255
  97.6 4.2 %collective-permute-start.3 = (f32[2,512,256]{2,1,0:T(8,128)S(1)}, f32[2,512,256]{2,1,0:T(8,128)S(1)}, u32[]{:S(2)}, u32[]{:S(2)}) collective-permute-start(f32[2,512,256]{2,1,0:T(8,128)S(1)} %get-tuple-element.29.refs_1_.refs_2_), channel_id=1, source_target_pairs={{4,0},{8,4},{12,8},{16,12},{20,16},{24,20},{28,24},{0,28},{5,1},{9... | collective-permute-start | bytes 3145736 | tf_op jit(solution)/shard_map/ppermute | solution.py:529
  101.9 1.6 collective-permute-start.9
  103.5 0.8 slice.25
  104.3 0.8 slice.24
  105.0 9.3 %collective-permute-done.9 = f32[56,8,256]{2,1,0:T(8,128)S(1)} collective-permute-done((f32[56,8,256]{2,1,0:T(8,128)S(1)}, f32[56,8,256]{2,1,0:T(8,128)S(1)}, u32[]{:S(2)}, u32[]{:S(2)}) %collective-permute-start.9) | collective-permute-done | bytes 458784 | tf_op jit(solution)/shard_map/ppermute | solution.py:498
  115.7 2.1 %cell_update.3 = (f32[40,8,256]{2,1,0:T(8,128)}, f32[12,8,256]{2,1,0:T(8,128)}, f32[14,8,256]{2,1,0:T(8,128)}, f32[8,16,256]{2,1,0:T(8,128)S(1)}) custom-call(f32[56,8,256]{2,1,0:T(8,128)S(1)} %add.15.sums, f32[40,8,256]{2,1,0:T(8,128)S(1)} %copy-done.5, f32[12,8,256]{2,1,0:T(8,128)S(1)} %copy-done.11, f32[14,8,256]{2,1,0:T(8,128)S(1)} %copy-done.8, ...), custom_call_target="tpu_custom_call" | custom-call | flops 1638400 | bytes 1310720 | tf_op jit(solution)/shard_map/cell_update/pallas_call | solution.py:165
  117.9 4.7 %collective-permute-start.11 = (f32[2,16,256]{2,1,0:T(8,128)S(1)}, f32[2,16,256]{2,1,0:T(8,128)S(1)}, u32[]{:S(2)}, u32[]{:S(2)}) collective-permute-start(f32[2,16,256]{2,1,0:T(8,128)S(1)} %get-tuple-element.54), channel_id=1, source_target_pairs={{4,0},{8,4},{12,8},{16,12},{20,16},{24,20},{28,24},{0,28},{5,1},{9... | collective-permute-start | bytes 98312 | tf_op jit(solution)/shard_map/ppermute | solution.py:529
  122.6 21.2 %day_two.1 = (f32[512,8,256]{2,1,0:T(8,128)}, f32[4,512,256]{2,1,0:T(8,128)S(1)}) custom-call(f32[12,512,256]{2,1,0:T(8,128)S(1)} %get-tuple-element.33.x.near_low.near_high, f32[8,16,256]{2,1,0:T(8,128)S(1)} %get-tuple-element.38.own, bf16[512,96]{1,0:T(8,128)(2,1)S(1)} %concatenate.24.refs_9_.moved_w, bf16[512,96]{1,0:T(8,128)(2,1)S(1)} %concatenate.25.refs_10_.kept_w, ...), custom_call_target="tpu_custom_call" | custom-call | flops 62914560 | bytes 8388608 | tf_op jit(solution)/shard_map/day_two/pallas_call | solution.py:334
  144.5 2.9 %collective-permute-done.11 = f32[2,16,256]{2,1,0:T(8,128)S(1)} collective-permute-done((f32[2,16,256]{2,1,0:T(8,128)S(1)}, f32[2,16,256]{2,1,0:T(8,128)S(1)}, u32[]{:S(2)}, u32[]{:S(2)}) %collective-permute-start.11) | collective-permute-done | bytes 32800 | tf_op jit(solution)/shard_map/ppermute | solution.py:529
  147.4 32.4 %edges.1 = f32[512,8,256]{2,1,0:T(8,128)} custom-call(f32[2,512,256]{2,1,0:T(8,128)S(1)} %collective-permute-done.2.low, f32[2,512,256]{2,1,0:T(8,128)S(1)} %collective-permute-done.3.high, f32[12,512,256]{2,1,0:T(8,128)S(1)} %get-tuple-element.33.x.near_low.near_high, ...), custom_call_target="tpu_custom_call", output_to_operand_aliasing={{}: (9, {})} | custom-call | flops 31457280 | bytes 8388608 | tf_op jit(solution)/shard_map/edges/pallas_call | solution.py:462
  (76 shorter events, 8.2 us)
Async XLA Ops:
  0.6 2.2 %copy-start = (f32[512,8,256]{2,1,0:T(8,128)S(1)}, f32[512,8,256]{2,1,0:T(8,128)}, u32[]{:S(2)}) copy-start(f32[512,8,256]{2,1,0:T(8,128)} %source.3) | copy-start | bytes 12582916
  2.8 3.2 %copy-start.22 = (f32[512]{0:T(512)S(1)}, f32[512]{0:T(512)}, u32[]{:S(2)}) copy-start(f32[512]{0:T(512)} %param.24) | copy-start | bytes 6148
  2.8 3.4 %copy-start.20 = (s32[512,14]{0,1:T(8,128)S(1)}, s32[512,14]{0,1:T(8,128)}, u32[]{:S(2)}) copy-start(s32[512,14]{0,1:T(8,128)} %param.21) | copy-start | bytes 86020
  2.8 3.4 %copy-start.19 = (s32[512,40]{0,1:T(8,128)S(1)}, s32[512,40]{0,1:T(8,128)}, u32[]{:S(2)}) copy-start(s32[512,40]{0,1:T(8,128)} %param.20) | copy-start | bytes 245764
  2.8 3.4 %copy-start.21 = (f32[512]{0:T(512)S(1)}, f32[512]{0:T(512)}, u32[]{:S(2)}) copy-start(f32[512]{0:T(512)} %param.23) | copy-start | bytes 6148
  6.1 11.4 %copy-start.24 = (f32[512]{0:T(512)S(1)}, f32[512]{0:T(512)}, u32[]{:S(2)}) copy-start(f32[512]{0:T(512)} %param.25) | copy-start | bytes 6148
  6.1 12.4 %copy-start.23 = (f32[512]{0:T(512)S(1)}, f32[512]{0:T(512)}, u32[]{:S(2)}) copy-start(f32[512]{0:T(512)} %param.26) | copy-start | bytes 6148
  6.3 23.7 %copy-start.6 = (f32[14,8,256]{2,1,0:T(8,128)S(1)}, f32[14,8,256]{2,1,0:T(8,128)}, u32[]{:S(2)}) copy-start(f32[14,8,256]{2,1,0:T(8,128)} %mono.1) | copy-start | bytes 344068
  6.3 23.7 %copy-start.12 = (f32[40]{0:T(128)S(1)}, f32[40]{0:T(128)}, u32[]{:S(2)}) copy-start(f32[40]{0:T(128)} %loss.3) | copy-start | bytes 484
  6.3 23.7 %copy-start.13 = (f32[40]{0:T(128)S(1)}, f32[40]{0:T(128)}, u32[]{:S(2)}) copy-start(f32[40]{0:T(128)} %vmax.3) | copy-start | bytes 484
  6.3 23.7 %copy-start.14 = (f32[40]{0:T(128)S(1)}, f32[40]{0:T(128)}, u32[]{:S(2)}) copy-start(f32[40]{0:T(128)} %kmich.3) | copy-start | bytes 484
  6.3 23.7 %copy-start.15 = (f32[14]{0:T(128)S(1)}, f32[14]{0:T(128)}, u32[]{:S(2)}) copy-start(f32[14]{0:T(128)} %khalf.3) | copy-start | bytes 172
  6.3 23.7 %copy-start.17 = (s32[40]{0:T(128)S(1)}, s32[40]{0:T(128)}, u32[]{:S(2)}) copy-start(s32[40]{0:T(128)} %target.3) | copy-start | bytes 484
  8.9 6.2 %collective-permute-start.4 = (f32[56,8,256]{2,1,0:T(8,128)S(1)}, f32[56,8,256]{2,1,0:T(8,128)S(1)}, u32[]{:S(2)}, u32[]{:S(2)}) collective-permute-start(f32[56,8,256]{2,1,0:T(8,128)S(1)} %taxa_sums.1), channel_id=1, source_target_pairs={{0,1},{1,0},{2,3},{3,2},{4,5},{5,4},{6,7},{7,6},{8,9},{9,8},{10,11... | collective-permute-start | bytes 1376264 | tf_op jit(solution)/shard_map/ppermute | solution.py:498
  9.4 50.2 %collective-permute-start = (f32[2,512,256]{2,1,0:T(8,128)}, f32[2,512,256]{2,1,0:T(8,128)}, u32[]{:S(2)}, u32[]{:S(2)}) collective-permute-start(f32[2,512,256]{2,1,0:T(8,128)} %get-tuple-element.24.refs_3_.refs_4_), channel_id=1, source_target_pairs={{0,4},{4,8},{8,12},{12,16},{16,20},{20,24},{24,28},{28,0},{1,5},{5... | collective-permute-start | bytes 3145736 | tf_op jit(solution)/shard_map/ppermute | solution.py:526
  11.9 49.9 %collective-permute-start.1 = (f32[2,512,256]{2,1,0:T(8,128)S(1)}, f32[2,512,256]{2,1,0:T(8,128)}, u32[]{:S(2)}, u32[]{:S(2)}) collective-permute-start(f32[2,512,256]{2,1,0:T(8,128)S(1)} %get-tuple-element.25.refs_0_.refs_1_), channel_id=1, source_target_pairs={{4,0},{8,4},{12,8},{16,12},{20,16},{24,20},{28,24},{0,28},{5,1},{9... | collective-permute-start | bytes 3145736 | tf_op jit(solution)/shard_map/ppermute | solution.py:529
  15.9 12.8 %collective-permute-start.5 = (f32[56,8,256]{2,1,0:T(8,128)}, f32[56,8,256]{2,1,0:T(8,128)}, u32[]{:S(2)}, u32[]{:S(2)}) collective-permute-start(f32[56,8,256]{2,1,0:T(8,128)} %add.12), channel_id=1, source_target_pairs={{0,2},{1,3},{2,0},{3,1},{4,6},{5,7},{6,4},{7,5},{8,10},{9,11},{10,... | collective-permute-start | bytes 1376264 | tf_op jit(solution)/shard_map/ppermute | solution.py:498
  30.0 1.0 copy-start.3
  31.0 0.9 copy-start.9
  35.3 7.0 %copy-start.1 = (f32[8,16,256]{2,1,0:T(8,128)}, f32[8,16,256]{2,1,0:T(8,128)S(1)}, u32[]{:S(2)}) copy-start(f32[8,16,256]{2,1,0:T(8,128)S(1)} %get-tuple-element.32.refs_6_) | copy-start | bytes 393220
  36.0 26.6 %collective-permute-start.7 = (f32[4,16,256]{2,1,0:T(8,128)}, f32[4,16,256]{2,1,0:T(8,128)}, u32[]{:S(2)}, u32[]{:S(2)}) collective-permute-start(f32[4,16,256]{2,1,0:T(8,128)} %get-tuple-element.55), channel_id=1, source_target_pairs={{4,0},{8,4},{12,8},{16,12},{20,16},{24,20},{28,24},{0,28},{5,1},{9... | collective-permute-start | bytes 196616 | tf_op jit(solution)/shard_map/ppermute | solution.py:529
  37.7 24.8 %collective-permute-start.6 = (f32[4,16,256]{2,1,0:T(8,128)}, f32[4,16,256]{2,1,0:T(8,128)}, u32[]{:S(2)}, u32[]{:S(2)}) collective-permute-start(f32[4,16,256]{2,1,0:T(8,128)} %get-tuple-element.56), channel_id=1, source_target_pairs={{0,4},{4,8},{8,12},{12,16},{16,20},{20,24},{24,28},{28,0},{1,5},{5... | collective-permute-start | bytes 196616 | tf_op jit(solution)/shard_map/ppermute | solution.py:526
  62.5 0.9 copy-start.2
  63.4 50.9 %copy-start.5 = (f32[40,8,256]{2,1,0:T(8,128)S(1)}, f32[40,8,256]{2,1,0:T(8,128)}, u32[]{:S(2)}) copy-start(f32[40,8,256]{2,1,0:T(8,128)} %copy-done.4) | copy-start | bytes 983044
  63.4 50.9 %copy-start.8 = (f32[14,8,256]{2,1,0:T(8,128)S(1)}, f32[14,8,256]{2,1,0:T(8,128)}, u32[]{:S(2)}) copy-start(f32[14,8,256]{2,1,0:T(8,128)} %copy-done.7) | copy-start | bytes 344068
  63.5 50.9 %copy-start.11 = (f32[12,8,256]{2,1,0:T(8,128)S(1)}, f32[12,8,256]{2,1,0:T(8,128)}, u32[]{:S(2)}) copy-start(f32[12,8,256]{2,1,0:T(8,128)} %copy-done.10) | copy-start | bytes 294916
  97.0 4.9 %collective-permute-start.8 = (f32[56,8,256]{2,1,0:T(8,128)S(1)}, f32[56,8,256]{2,1,0:T(8,128)S(1)}, u32[]{:S(2)}, u32[]{:S(2)}) collective-permute-start(f32[56,8,256]{2,1,0:T(8,128)S(1)} %get-tuple-element.34), channel_id=1, source_target_pairs={{0,1},{1,0},{2,3},{3,2},{4,5},{5,4},{6,7},{7,6},{8,9},{9,8},{10,11... | collective-permute-start | bytes 1376264 | tf_op jit(solution)/shard_map/ppermute | solution.py:498
  97.1 50.4 %collective-permute-start.2 = (f32[2,512,256]{2,1,0:T(8,128)S(1)}, f32[2,512,256]{2,1,0:T(8,128)S(1)}, u32[]{:S(2)}, u32[]{:S(2)}) collective-permute-start(f32[2,512,256]{2,1,0:T(8,128)S(1)} %get-tuple-element.28.refs_2_.refs_3_), channel_id=1, source_target_pairs={{0,4},{4,8},{8,12},{12,16},{16,20},{20,24},{24,28},{28,0},{1,5},{5... | collective-permute-start | bytes 3145736 | tf_op jit(solution)/shard_map/ppermute | solution.py:526
  97.6 49.8 %collective-permute-start.3 = (f32[2,512,256]{2,1,0:T(8,128)S(1)}, f32[2,512,256]{2,1,0:T(8,128)S(1)}, u32[]{:S(2)}, u32[]{:S(2)}) collective-permute-start(f32[2,512,256]{2,1,0:T(8,128)S(1)} %get-tuple-element.29.refs_1_.refs_2_), channel_id=1, source_target_pairs={{4,0},{8,4},{12,8},{16,12},{20,16},{24,20},{28,24},{0,28},{5,1},{9... | collective-permute-start | bytes 3145736 | tf_op jit(solution)/shard_map/ppermute | solution.py:529
  101.9 12.4 %collective-permute-start.9 = (f32[56,8,256]{2,1,0:T(8,128)S(1)}, f32[56,8,256]{2,1,0:T(8,128)S(1)}, u32[]{:S(2)}, u32[]{:S(2)}) collective-permute-start(f32[56,8,256]{2,1,0:T(8,128)S(1)} %add.14), channel_id=1, source_target_pairs={{0,2},{1,3},{2,0},{3,1},{4,6},{5,7},{6,4},{7,5},{8,10},{9,11},{10,... | collective-permute-start | bytes 1376264 | tf_op jit(solution)/shard_map/ppermute | solution.py:498
  117.8 26.7 %collective-permute-start.10 = (f32[2,16,256]{2,1,0:T(8,128)S(1)}, f32[2,16,256]{2,1,0:T(8,128)S(1)}, u32[]{:S(2)}, u32[]{:S(2)}) collective-permute-start(f32[2,16,256]{2,1,0:T(8,128)S(1)} %get-tuple-element.53), channel_id=1, source_target_pairs={{0,4},{4,8},{8,12},{12,16},{16,20},{20,24},{24,28},{28,0},{1,5},{5... | collective-permute-start | bytes 98312 | tf_op jit(solution)/shard_map/ppermute | solution.py:526
  117.9 29.5 %collective-permute-start.11 = (f32[2,16,256]{2,1,0:T(8,128)S(1)}, f32[2,16,256]{2,1,0:T(8,128)S(1)}, u32[]{:S(2)}, u32[]{:S(2)}) collective-permute-start(f32[2,16,256]{2,1,0:T(8,128)S(1)} %get-tuple-element.54), channel_id=1, source_target_pairs={{4,0},{8,4},{12,8},{16,12},{20,16},{24,20},{28,24},{0,28},{5,1},{9... | collective-permute-start | bytes 98312 | tf_op jit(solution)/shard_map/ppermute | solution.py:529
  (5 other events, 3.3 us)

commit v2 on v1

v2 whole, which is shorter than its diff:
```python
import jax
import jax.numpy as jnp
from jax import lax
from jax.experimental import pallas as pl
from jax.experimental.pallas import tpu as pltpu
from jax.sharding import PartitionSpec as P

KOFF = 8
YIELD = 0.6
HALF = 128
SLOTS = 16
CHAN = 56
PADDED = 64
F32 = jnp.float32
BF16 = jnp.bfloat16
ANY = pl.BlockSpec(memory_space=pl.ANY)
SMEM = pl.BlockSpec(memory_space=pltpu.SMEM)
VMEM_BYTES = 40 << 20


def params():
    return pltpu.CompilerParams(vmem_limit_bytes=VMEM_BYTES)


def cost(flops, moved):
    return pl.CostEstimate(flops=flops, bytes_accessed=moved, transcendentals=0)


def pieces_outside(x, count):
    out = []
    for _ in range(count):
        part = lax.reduce_precision(x, 8, 7)
        out.append(part.astype(BF16))
        x = x - part
    return out


def pieces_inside(x, count):
    out = []
    for _ in range(count):
        part = x.astype(BF16)
        out.append(part)
        x = x - part.astype(F32)
    return out


def share_operand(share):
    high, mid, low = pieces_inside(share, 3)
    return jnp.concatenate([high, mid, low, high, mid, high], 0)


def trait_operand(matrix):
    high, mid, low = pieces_outside(matrix, 3)
    return jnp.concatenate([high, high, high, mid, mid, low], 1)


def matmul(a, b):
    return jnp.dot(a, b, preferred_element_type=F32)


def take_rows(biomass, rows):
    count, _, width = biomass.shape
    pairs = len(rows) // 2

    def kernel(source, *refs):
        outs, sem = refs[:-1], refs[-1]
        copies = [
            pltpu.make_async_copy(source.at[:, row, :], outs[i // 2].at[i % 2], sem.at[i])
            for i, row in enumerate(rows)
        ]
        for copy in copies:
            copy.start()
        for copy in copies:
            copy.wait()

    return pl.pallas_call(
        kernel,
        name="take_rows",
        out_shape=[jax.ShapeDtypeStruct((2, count, width), F32)] * pairs,
        in_specs=[ANY],
        out_specs=[ANY] * pairs,
        scratch_shapes=[pltpu.SemaphoreType.DMA((len(rows),))],
        compiler_params=params(),
        cost_estimate=cost(0, 8 * len(rows) * count * width),
    )(biomass)


def add_sums(total, row, x, weights):
    high, low = pieces_inside(x, 2)
    first = matmul(weights, high)
    second = matmul(weights[:PADDED], low)
    total[row] += first[:PADDED] + first[PADDED:] + second


def finish_sums(total, odd, mine, other):
    low = jnp.swapaxes(total[:, : CHAN // 2, :], 0, 1)
    high = jnp.swapaxes(total[:, CHAN // 2 : CHAN, :], 0, 1)

    @pl.when(odd[0] == 0)
    def _():
        mine[...] = low
        other[...] = high

    @pl.when(odd[0] != 0)
    def _():
        mine[...] = high
        other[...] = low


def taxa_sums(row_pairs, weights, odd, block):
    _, count, width = row_pairs[0].shape
    rows = 2 * len(row_pairs)

    def kernel(*refs):
        pairs = refs[: len(row_pairs)]
        weight, side, mine, other, total = refs[len(row_pairs) :]

        @pl.when(pl.program_id(0) == 0)
        def _():
            total[...] = jnp.zeros_like(total)

        for row in range(rows):
            add_sums(total, row, pairs[row // 2][row % 2], weight[...])

        @pl.when(pl.program_id(0) == pl.num_programs(0) - 1)
        def _():
            finish_sums(total, side, mine, other)

    half = (CHAN // 2, rows, width)
    return pl.pallas_call(
        kernel,
        name="taxa_sums",
        grid=(count // block,),
        out_shape=[jax.ShapeDtypeStruct(half, F32)] * 2,
        in_specs=[pl.BlockSpec((2, block, width), lambda i: (0, i, 0))] * len(row_pairs)
        + [pl.BlockSpec((2 * PADDED, block), lambda i: (0, i)), SMEM],
        out_specs=[whole(half)] * 2,
        scratch_shapes=[pltpu.VMEM((rows, PADDED, width), F32)],
        compiler_params=params(),
        cost_estimate=cost(1000, 1000),
    )(*row_pairs, weights, odd)


def cell_update(mine, rest, odd, enz, sub, mono, enz_loss, vmax, kmich, khalf, enz_target):
    n_enz, rows, width = enz.shape
    n_sub, n_mono = sub.shape[0], mono.shape[0]

    def kernel(*refs):
        mine, rest, enz, sub, mono, side, loss, vmax, kmich, khalf, target = refs[:11]
        pool, left, mono_two, out, sums, speed, rate, share = refs[11:]
        half = mine.shape[0]

        @pl.when(side[0] == 0)
        def _():
            sums[:half] = mine[...]
            sums[half:] = rest[...]

        @pl.when(side[0] != 0)
        def _():
            sums[:half] = rest[...]
            sums[half:] = mine[...]

        rate[...] = jnp.zeros_like(rate)
        for e in range(n_enz):
            now = enz[e] * (1.0 - loss[e]) + sums[e]
            pool[e] = now
            speed[e] = vmax[e] * now / (kmich[e] + sub[target[e]])
        for e in range(n_enz):
            rate[target[e]] += speed[e]

        def finish(m, mono_one):
            demand = sums[n_enz + m]
            part = mono_one / (khalf[m] + demand + mono_one)
            mono_two[m] = mono_one - demand * part
            share[m] = part

        for s in range(n_sub):
            kept = sub[s] * jnp.exp(-rate[s])
            left[s] = kept
            finish(s, mono[s] + (sub[s] - kept))
        for m in range(n_sub, n_mono):
            finish(m, mono[m])
        share[n_mono] = jnp.ones((rows, width), F32)
        for m in range(n_mono + 1, SLOTS):
            share[m] = jnp.zeros((rows, width), F32)
        out[...] = jnp.swapaxes(share[...], 0, 1)

    vmem = pl.BlockSpec(memory_space=pltpu.VMEM)
    return pl.pallas_call(
        kernel,
        name="cell_update",
        out_shape=[
            jax.ShapeDtypeStruct(enz.shape, F32),
            jax.ShapeDtypeStruct(sub.shape, F32),
            jax.ShapeDtypeStruct(mono.shape, F32),
            jax.ShapeDtypeStruct((rows, SLOTS, width), F32),
        ],
        in_specs=[vmem] * 5 + [SMEM] * 6,
        out_specs=[vmem] * 4,
        scratch_shapes=[
            pltpu.VMEM((CHAN, rows, width), F32),
            pltpu.VMEM(enz.shape, F32),
            pltpu.VMEM(sub.shape, F32),
            pltpu.VMEM((SLOTS, rows, width), F32),
        ],
        compiler_params=params(),
        cost_estimate=cost(1000, 1000),
    )(mine, rest, enz, sub, mono, odd, enz_loss, vmax, kmich, khalf, enz_target)


def circulants(offsets, width):
    row_offset = 2 - lax.iota(jnp.int32, 5)
    col_offset = lax.iota(jnp.int32, 5) - 2
    row_hit = (offsets[:, 0, None] == row_offset[None, :]).astype(F32)
    col_hit = (offsets[:, 1, None] == col_offset[None, :]).astype(F32)
    number = jnp.sum(row_hit[:, :, None] * col_hit[:, None, :], axis=0)
    still = (row_offset[:, None] == 0) & (col_offset[None, :] == 0)
    number = number - KOFF * still.astype(F32)
    source = lax.broadcasted_iota(jnp.int32, (width, width), 0)
    target = lax.broadcasted_iota(jnp.int32, (width, width), 1)
    apart = lax.rem(target - source + width + 2, width)
    total = jnp.zeros((5, width, width), F32)
    for i in range(5):
        total = total + number[:, i, None, None] * (apart == i).astype(F32)
    total = jnp.broadcast_to(total.astype(BF16)[:, None], (5, 2, width, width))
    return total.reshape(10 * width, width)


def store_pieces(pieces, index, value):
    width = value.shape[1]
    at = 2 * width * index
    high, low = pieces_inside(value, 2)
    pieces[:, at : at + width] = high
    pieces[:, at + width : at + 2 * width] = low


def stencil(pieces, circulant, first, count, offset):
    span = circulant.shape[1] * 2
    return matmul(
        pieces[:, span * first : span * (first + count)],
        circulant[span * offset : span * (offset + count), :],
    )


def window(target, rows):
    first = max(target - 2, 0)
    return first, min(target + 2, rows - 1) - first + 1, first - target + 2


def spread(value, fraction, change):
    return value + jnp.concatenate([fraction, fraction], 1) * change


def whole(shape):
    return pl.BlockSpec(shape, lambda i: (0,) * len(shape))


def pair_spec(block, width, at=0):
    return pl.BlockSpec((2, block, width), lambda i: (at, i, 0))


def taxa_spec(block, width):
    return pl.BlockSpec((block, width), lambda i: (i, 0))


def day_one_inside(row_pairs, share, gain, fraction, circulant, weights, block):
    _, count, width = row_pairs[0].shape
    rows = 2 * len(row_pairs)
    inner = rows - 4

    def kernel(*refs):
        pairs = refs[: len(row_pairs)]
        own, gain_w, frac, circ, weight, out, total, pieces = refs[len(row_pairs) :]

        @pl.when(pl.program_id(0) == 0)
        def _():
            total[...] = jnp.zeros_like(total)

        for row in range(rows):
            value = pairs[row // 2][row % 2] * matmul(gain_w[...], share_operand(own[row]))
            out[row] = value
            store_pieces(pieces, row, value)
        for row in range(rows):
            value = spread(out[row], frac[...], stencil(pieces, circ, *window(row, rows)))
            out[row] = value
            if 2 <= row < rows - 2:
                add_sums(total, row - 2, value, weight[...])

    return pl.pallas_call(
        kernel,
        name="day_one_inside",
        grid=(count // block,),
        out_shape=[
            jax.ShapeDtypeStruct((rows, count, width), F32),
            jax.ShapeDtypeStruct((inner, PADDED, width), F32),
        ],
        in_specs=[pair_spec(block, width)] * len(row_pairs)
        + [
            whole(share.shape),
            taxa_spec(block, gain.shape[1]),
            taxa_spec(block, HALF),
            whole(circulant.shape),
            pl.BlockSpec((2 * PADDED, block), lambda i: (0, i)),
        ],
        out_specs=[
            pl.BlockSpec((rows, block, width), lambda i: (0, i, 0)),
            whole((inner, PADDED, width)),
        ],
        scratch_shapes=[pltpu.VMEM((block, rows * 2 * width), BF16)],
        compiler_params=params(),
        cost_estimate=cost(1000, 1000),
    )(*row_pairs, share, gain, fraction, circulant, weights)


TERMS = ((0, 2, 0), (1, 1, 0), (2, 1, 4), (2, 2, 3))


def day_one_rim(low, high, inside, sums, share_low, share_high, gain, fraction, circulant, weights, odd, block):
    _, count, width = low.shape
    rows = inside.shape[0]

    def kernel(
        low, high, first, last, part, before, after, gain_w, frac, circ, weight, side, out, mine, other, far, total
    ):
        @pl.when(pl.program_id(0) == 0)
        def _():
            total[2 : rows - 2] = part[...]
            for row in (0, 1, rows - 2, rows - 1):
                total[row] = jnp.zeros((PADDED, width), F32)

        for i in range(4):
            x = low[i] if i < 2 else high[i - 2]
            s = before[2 + i] if i < 2 else after[i - 2]
            store_pieces(far, i, x * matmul(gain_w[...], share_operand(s)))
        for i in range(4):
            x = first[i] if i < 2 else last[i - 2]
            value = spread(x, frac[...], stencil(far, circ, *TERMS[i]))
            out[i] = value
            add_sums(total, i if i < 2 else rows - 4 + i, value, weight[...])

        @pl.when(pl.program_id(0) == pl.num_programs(0) - 1)
        def _():
            finish_sums(total, side, mine, other)

    half = (CHAN // 2, rows, width)
    return pl.pallas_call(
        kernel,
        name="day_one_rim",
        grid=(count // block,),
        out_shape=[jax.ShapeDtypeStruct((4, count, width), F32)] + [jax.ShapeDtypeStruct(half, F32)] * 2,
        in_specs=[
            pair_spec(block, width),
            pair_spec(block, width),
            pair_spec(block, width),
            pair_spec(block, width, rows // 2 - 1),
            whole(sums.shape),
            whole(share_low.shape),
            whole(share_high.shape),
            taxa_spec(block, gain.shape[1]),
            taxa_spec(block, HALF),
            whole(circulant.shape),
            pl.BlockSpec((2 * PADDED, block), lambda i: (0, i)),
            SMEM,
        ],
        out_specs=[pl.BlockSpec((4, block, width), lambda i: (0, i, 0))] + [whole(half)] * 2,
        scratch_shapes=[
            pltpu.VMEM((block, 8 * width), BF16),
            pltpu.VMEM((rows, PADDED, width), F32),
        ],
        compiler_params=params(),
        cost_estimate=cost(1000, 1000),
    )(low, high, inside, inside, sums, share_low, share_high, gain, fraction, circulant, weights, odd)


def day_one_beyond(row_pairs, low, high, share, share_low, share_high, gain, fraction, circulant, block):
    _, count, width = low.shape
    rows = 2 * len(row_pairs)

    def kernel(low, high, first, last, own, before, after, gain_w, frac, circ, out, pieces):
        for side in range(2):
            for i in range(4):
                if side == 0:
                    x = low[i] if i < 2 else first[i - 2]
                    s = before[2 + i] if i < 2 else own[i - 2]
                else:
                    x = last[i] if i < 2 else high[i - 2]
                    s = own[rows - 2 + i] if i < 2 else after[i - 2]
                value = x * matmul(gain_w[...], share_operand(s))
                store_pieces(pieces, i, value)
                if (i < 2) == (side == 0):
                    out[i] = value
            for i in (0, 1) if side == 0 else (2, 3):
                out[i] = spread(out[i], frac[...], stencil(pieces, circ, *window(i, 4)))

    return pl.pallas_call(
        kernel,
        name="day_one_beyond",
        grid=(count // block,),
        out_shape=jax.ShapeDtypeStruct((4, count, width), F32),
        in_specs=[pair_spec(block, width)] * 4
        + [
            whole(share.shape),
            whole(share_low.shape),
            whole(share_high.shape),
            taxa_spec(block, gain.shape[1]),
            taxa_spec(block, HALF),
            whole(circulant.shape),
        ],
        out_specs=pl.BlockSpec((4, block, width), lambda i: (0, i, 0)),
        scratch_shapes=[pltpu.VMEM((block, 8 * width), BF16)],
        compiler_params=params(),
        cost_estimate=cost(1000, 1000),
    )(low, high, row_pairs[0], row_pairs[-1], share, share_low, share_high, gain, fraction, circulant)


def day_two(inside, rim, share, gain, fraction, circulant, block):
    rows, count, width = inside.shape
    steps = count // block
    middle = rows // 2 - 2

    def kernel(*refs):
        inner = refs[:middle]
        outer, own, gain_w, frac, circ, out, edge, pieces, result, sem = refs[middle:]
        step = pl.program_id(0)
        slot = lax.rem(step, 2)

        def copies(at, where):
            found = []
            taxa = pl.ds(pl.multiple_of(at * block, block), block)
            for row in range(rows):
                if 2 <= row < rows - 2:
                    target = out.at[taxa, row, :]
                else:
                    target = edge.at[row if row < 2 else row - rows + 4, taxa, :]
                found.append(pltpu.make_async_copy(result.at[where, row], target, sem.at[where, row]))
            return found

        @pl.when(step >= 2)
        def _():
            for copy in copies(step - 2, slot):
                copy.wait()

        for row in range(rows):
            if 2 <= row < rows - 2:
                x = inner[row // 2 - 1][row % 2]
            else:
                x = outer[row if row < 2 else row - rows + 4]
            value = x * matmul(gain_w[...], share_operand(own[row]))
            result[slot, row] = value
            store_pieces(pieces, row, value)
        for row in range(rows):
            result[slot, row] = spread(result[slot, row], frac[...], stencil(pieces, circ, *window(row, rows)))
        for copy in copies(step, slot):
            copy.start()

        @pl.when(step == steps - 1)
        def _():
            if steps > 1:
                for copy in copies(step - 1, 1 - slot):
                    copy.wait()
            for copy in copies(step, slot):
                copy.wait()

    return pl.pallas_call(
        kernel,
        name="day_two",
        grid=(steps,),
        out_shape=[
            jax.ShapeDtypeStruct((count, rows, width), F32),
            jax.ShapeDtypeStruct((4, count, width), F32),
        ],
        in_specs=[
            *[pair_spec(block, width, 1 + i) for i in range(middle)],
            pl.BlockSpec((4, block, width), lambda i: (0, i, 0)),
            whole(share.shape),
            taxa_spec(block, gain.shape[1]),
            taxa_spec(block, HALF),
            whole(circulant.shape),
        ],
        out_specs=[ANY, ANY],
        scratch_shapes=[
            pltpu.VMEM((block, rows * 2 * width), BF16),
            pltpu.VMEM((2, rows, block, width), F32),
            pltpu.SemaphoreType.DMA((2, rows)),
        ],
        compiler_params=params(),
        cost_estimate=cost(1000, 1000),
    )(*[inside] * middle, rim, share, gain, fraction, circulant)


def edges(outer_low, outer_high, beyond, edge, biomass_out, share_one, share_two, gain, fraction, circulant, block):
    _, count, width = outer_low.shape
    rows = biomass_out.shape[1]
    steps = count // block

    def kernel(low, high, near_low, near_high, own, s1, s2, gain_w, frac, circ, unused, out, far, near, result, sem):
        step = pl.program_id(0)
        slot = lax.rem(step, 2)

        def copies(at, where):
            taxa = pl.ds(pl.multiple_of(at * block, block), block)
            return [
                pltpu.make_async_copy(
                    result.at[where, i],
                    out.at[taxa, i if i < 2 else rows - 4 + i, :],
                    sem.at[where, i],
                )
                for i in range(4)
            ]

        @pl.when(step >= 2)
        def _():
            for copy in copies(step - 2, slot):
                copy.wait()

        for i in range(4):
            x = low[i] if i < 2 else high[i - 2]
            store_pieces(far, i, x * matmul(gain_w[...], share_operand(s1[i])))
        for i in range(4):
            x = near_low[i] if i < 2 else near_high[i - 2]
            value = spread(x, frac[...], stencil(far, circ, *TERMS[i]))
            store_pieces(near, i, value * matmul(gain_w[...], share_operand(s2[i])))
        for i in range(4):
            result[slot, i] = spread(own[i], frac[...], stencil(near, circ, *TERMS[i]))
        for copy in copies(step, slot):
            copy.start()

        @pl.when(step == steps - 1)
        def _():
            if steps > 1:
                for copy in copies(step - 1, 1 - slot):
                    copy.wait()
            for copy in copies(step, slot):
                copy.wait()

    return pl.pallas_call(
        kernel,
        name="edges",
        grid=(steps,),
        out_shape=jax.ShapeDtypeStruct(biomass_out.shape, F32),
        in_specs=[
            *[pair_spec(block, width)] * 3,
            pair_spec(block, width, 1),
            pl.BlockSpec((4, block, width), lambda i: (0, i, 0)),
            whole(share_one.shape),
            whole(share_two.shape),
            pl.BlockSpec((block, gain.shape[1]), lambda i: (i, 0)),
            pl.BlockSpec((block, HALF), lambda i: (i, 0)),
            whole(circulant.shape),
            ANY,
        ],
        out_specs=ANY,
        scratch_shapes=[
            pltpu.VMEM((block, 8 * width), BF16),
            pltpu.VMEM((block, 8 * width), BF16),
            pltpu.VMEM((2, 4, block, width), F32),
            pltpu.SemaphoreType.DMA((2, 4)),
        ],
        input_output_aliases={10: 0},
        compiler_params=params(),
        cost_estimate=cost(1000, 1000),
    )(outer_low, outer_high, beyond, beyond, edge, share_one, share_two, gain, fraction, circulant, biomass_out)


def over_taxa(mine, other):
    count = lax.axis_size("taxa")

    def exchange(x, step):
        return lax.ppermute(x, "taxa", [(i, i ^ step) for i in range(count)])

    mine = mine + exchange(other, 1)
    step = 2
    while step < count:
        mine = mine + exchange(mine, step)
        step *= 2
    return mine, exchange(mine, 1)


def body(
    biomass,
    enzymes,
    substrates,
    monomers,
    enz_traits,
    mono_traits,
    enz_target,
    prod_rate,
    uptake_rate,
    mortality,
    disperse,
    enz_loss,
    vmax,
    kmich,
    khalf,
    offsets,
):
    ring = lax.axis_size("space")
    forward = [(i, (i + 1) % ring) for i in range(ring)]
    backward = [(target, source) for source, target in forward]

    def down(x):
        return lax.ppermute(x, "space", forward)

    def up(x):
        return lax.ppermute(x, "space", backward)

    count, rows, width = biomass.shape
    block = min(count, 256)

    first, last = take_rows(biomass, (0, 1, rows - 2, rows - 1))
    inner_low, inner_high = down(last), up(first)
    middle = take_rows(biomass, tuple(range(2, rows - 2)))
    row_pairs = [first, *middle, last]

    enz_f = enz_traits.astype(F32)
    mono_f = mono_traits.astype(F32)
    weight = jnp.concatenate(
        [
            enz_f * prod_rate[:, None],
            mono_f * uptake_rate[:, None],
            jnp.zeros((count, PADDED - enz_f.shape[1] - mono_f.shape[1]), F32),
        ],
        1,
    ).T
    weights = jnp.concatenate(pieces_outside(weight, 2), 0)
    keep = 1.0 - mortality - prod_rate * jnp.sum(enz_f, axis=1)
    gain = jnp.concatenate(
        [
            (YIELD * uptake_rate)[:, None] * mono_f,
            keep[:, None],
            jnp.zeros((count, SLOTS - 1 - mono_f.shape[1]), F32),
        ],
        1,
    )
    gain = trait_operand(gain)
    fraction = jnp.broadcast_to((disperse / KOFF)[:, None], (count, HALF))
    circulant = circulants(offsets, width)
    cells = (enz_loss, vmax, kmich, khalf, enz_target)

    odd = lax.rem(lax.axis_index("taxa"), 2).reshape(1).astype(jnp.int32)

    sums = over_taxa(*taxa_sums(row_pairs, weights, odd, block))
    enzymes, substrates, monomers, share_one = cell_update(*sums, odd, enzymes, substrates, monomers, *cells)
    share_low, share_high = down(share_one[rows - 4 :]), up(share_one[:4])
    spreading = (gain, fraction, circulant)
    inside, inside_sums = day_one_inside(row_pairs, share_one, *spreading, weights, block)

    inner_low, inner_high, share_low, share_high, inside, outer_first, outer_last = lax.optimization_barrier(
        (inner_low, inner_high, share_low, share_high, inside, middle[0], middle[-1])
    )
    outer_low, outer_high = down(outer_last), up(outer_first)

    def rest_of_day_one(low, high, share_low, share_high, enzymes, substrates, monomers):
        rim, *sums = day_one_rim(
            low, high, inside, inside_sums, share_low, share_high, *spreading, weights, odd, block
        )
        sums = over_taxa(*sums)
        return rim, *cell_update(*sums, odd, enzymes, substrates, monomers, *cells)

    def unused(*operands):
        shapes = jax.eval_shape(rest_of_day_one, *operands)
        return jax.tree.map(lambda x: jnp.zeros(x.shape, x.dtype), shapes)

    rim, enzymes, substrates, monomers, share_two = lax.cond(
        offsets[0, 0] < 3,
        rest_of_day_one,
        unused,
        inner_low,
        inner_high,
        share_low,
        share_high,
        enzymes,
        substrates,
        monomers,
    )
    near_low, near_high = down(share_two[rows - 2 :]), up(share_two[:2])
    beyond = day_one_beyond(
        row_pairs, inner_low, inner_high, share_one, share_low, share_high, *spreading, block
    )
    biomass_out, edge = day_two(inside, rim, share_two, *spreading, block)
    biomass_out = edges(
        outer_low,
        outer_high,
        beyond,
        edge,
        biomass_out,
        jnp.concatenate([share_low[:2], share_high[2:]], 0),
        jnp.concatenate([near_low, near_high], 0),
        gain,
        fraction,
        circulant,
        block,
    )
    return (biomass_out, enzymes, substrates, monomers)


def solution(mesh):
    placed = (
        P("taxa", "space", None),
        P(None, "space", None),
        P(None, "space", None),
        P(None, "space", None),
        P("taxa", None),
        P("taxa", None),
        P(),
        P("taxa"),
        P("taxa"),
        P("taxa"),
        P("taxa"),
        P(),
        P(),
        P(),
        P(),
        P(),
    )
    return jax.shard_map(
        body,
        mesh=mesh,
        in_specs=placed,
        out_specs=(
            P("taxa", "space", None),
            P(None, "space", None),
            P(None, "space", None),
            P(None, "space", None),
        ),
        check_vma=False,
    )
```

time: 180 us -> 113 us (0.63)
  Pallas kernels: 96.2 us -> 45.4 us
  waiting for transfers between devices: 41.8 us -> 24 us
  local copies, waits for them, and re-layouts: 15.3 us -> 13 us
  other arithmetic: 4.48 us -> 6.49 us
    pallas_call x1, Pallas kernels: 32.4 us -> 4.9 us  [edges(): pl.pallas_call(kernel, name='edges', grid=(steps,), out_shape=jax.ShapeDt...]
    ppermute x4, waiting for transfers between devices: 16.5 us -> 0.19 us  [down(): return lax.ppermute(x, 'space', forward)]
    pallas_call x1, Pallas kernels: 21.2 us -> 8.01 us  [day_two(): pl.pallas_call(kernel, name='day_two', grid=(steps,), out_shape=[jax.Shap...]
    pallas_call x1 -> x3, Pallas kernels: 33.5 us -> 23.6 us  [the longest x1 12.8 us: day_one_inside(): pl.pallas_call(kernel, name='day_one_inside', grid=(count // block,), out...]
    ppermute x4 -> x6, waiting for transfers between devices: 19.5 us -> 13.6 us  [exchange(): return lax.ppermute(x, 'taxa', [(i, i ^ step) for i in range(count)])]
    unnamed x51 -> x62, local copies, waits for them, and re-layouts: 9.09 us -> 3.64 us
    ppermute x4, waiting for transfers between devices: 5.86 us -> 10.3 us  [up(): return lax.ppermute(x, 'space', backward)]
    ppermute x4 -> x6, starting transfers between devices: 3.8 us -> 3.45 us  [exchange(): return lax.ppermute(x, 'taxa', [(i, i ^ step) for i in range(count)])]
  transfers between devices with their start and end apart: 12 -> 14, of which waited for: 7 -> 7; matrix products, arithmetic and copies ran while one was open for 6% -> 14% of each run, Pallas kernels for 14% -> 35%
where the time goes in v2:
time: 113 us; the launch traced here: 112 us
  Pallas kernels  45.4 us (40%)
  waiting for transfers between devices  24 us (21%)
  starting transfers between devices  21.1 us (19%)
  local copies, waits for them, and re-layouts  13 us (12%)
  other arithmetic  6.49 us (6%)
  between operations  1.98 us (2%)
    ppermute x4, starting transfers between devices, up(): return lax.ppermute(x, 'space', backward)  14.3 us
    ppermute x6, waiting for transfers between devices, exchange(): return lax.ppermute(x, 'taxa', [(i, i ^ step) for i in range(count)])  13.6 us
    pallas_call x1, Pallas kernels, day_one_inside(): pl.pallas_call(kernel, name='day_one_inside', grid=(count // block,), out...  12.8 us
    ppermute x4, waiting for transfers between devices, up(): return lax.ppermute(x, 'space', backward)  10.3 us
    pallas_call x1, Pallas kernels, day_two(): pl.pallas_call(kernel, name='day_two', grid=(steps,), out_shape=[jax.Shap...  8.01 us
    pallas_call x1, Pallas kernels, day_one_rim(): pl.pallas_call(kernel, name='day_one_rim', grid=(count // block,), out_sh...  5.98 us
    pallas_call x1, Pallas kernels, edges(): pl.pallas_call(kernel, name='edges', grid=(steps,), out_shape=jax.ShapeDt...  4.9 us
    pallas_call x1, Pallas kernels, day_one_beyond(): pl.pallas_call(kernel, name='day_one_beyond', grid=(count // block,), out...  4.88 us
  transfers between devices with their start and end apart: 14, of which 7 were waited for; matrix products, arithmetic and copies ran while one was open for 14% of the time, Pallas kernels for 35%

profile of v2, /device:TPU:0, one launch (start us, length us, event | category | flops | bytes accessed | tf_op | source)
XLA Modules:
  0.0 112.1 jit_solution(13912456373063804485)
XLA Ops:
  0.6 2.2 %copy-done = f32[512,8,256]{2,1,0:T(8,128)S(1)} copy-done((f32[512,8,256]{2,1,0:T(8,128)S(1)}, f32[512,8,256]{2,1,0:T(8,128)}, u32[]{:S(2)}) %copy-start) | copy-done | bytes 4194328
  2.8 1.5 %take_rows.2 = (f32[2,512,256]{2,1,0:T(8,128)S(1)}, f32[2,512,256]{2,1,0:T(8,128)S(1)}) custom-call(f32[512,8,256]{2,1,0:T(8,128)S(1)} %copy-done), custom_call_target="tpu_custom_call" | custom-call | bytes 4194304 | tf_op jit(solution)/shard_map/take_rows/pallas_call | solution.py:76
  4.3 3.0 %collective-permute-start.3 = (f32[2,512,256]{2,1,0:T(8,128)S(1)}, f32[2,512,256]{2,1,0:T(8,128)}, u32[]{:S(2)}, u32[]{:S(2)}) collective-permute-start(f32[2,512,256]{2,1,0:T(8,128)S(1)} %get-tuple-element.94.refs_3_.last), channel_id=1, source_target_pairs={{0,4},{4,8},{8,12},{12,16},{16,20},{20,24},{24,28},{28,0},{1,5},{5... | collective-permute-start | bytes 3145736 | tf_op jit(solution)/shard_map/ppermute | solution.py:602
  7.3 3.1 %collective-permute-start.4 = (f32[2,512,256]{2,1,0:T(8,128)S(1)}, f32[2,512,256]{2,1,0:T(8,128)}, u32[]{:S(2)}, u32[]{:S(2)}) collective-permute-start(f32[2,512,256]{2,1,0:T(8,128)S(1)} %get-tuple-element.95.refs_0_.first), channel_id=1, source_target_pairs={{4,0},{8,4},{12,8},{16,12},{20,16},{24,20},{28,24},{0,28},{5,1},{9... | collective-permute-start | bytes 3145736 | tf_op jit(solution)/shard_map/ppermute | solution.py:605
  10.4 1.8 %take_rows.3 = (f32[2,512,256]{2,1,0:T(8,128)S(1)}, f32[2,512,256]{2,1,0:T(8,128)}) custom-call(f32[512,8,256]{2,1,0:T(8,128)S(1)} %copy-done), custom_call_target="tpu_custom_call" | custom-call | bytes 4194304 | tf_op jit(solution)/shard_map/take_rows/pallas_call | solution.py:76
  12.5 2.4 %taxa_sums.1 = (f32[28,8,256]{2,1,0:T(8,128)S(1)}, f32[28,8,256]{2,1,0:T(8,128)S(1)}) custom-call(f32[2,512,256]{2,1,0:T(8,128)S(1)} %get-tuple-element.95.refs_0_.first, f32[2,512,256]{2,1,0:T(8,128)S(1)} %get-tuple-element.103.refs_1_, f32[2,512,256]{2,1,0:T(8,128)} %get-tuple-element.102.refs_2_, f32[2,512,256]{2,1,0:T(8,128)S(1)} %get-tuple-element.94.refs_3_.last, ...), custom_call_target="tpu_custom_call" | custom-call | flops 1000 | bytes 1000 | tf_op jit(solution)/shard_map/taxa_sums/pallas_call | solution.py:130
  16.1 1.3 %add_convert_fusion = bf16[5,256,256]{2,1,0:T(8,128)(2,1)} fusion(f32[256,256]{1,0:T(8,128)S(1)} %get-tuple-element.143, f32[5]{0:T(128)S(1)} %get-tuple-element.121, f32[256,256]{1,0:T(8,128)S(1)} %get-tuple-element.144, f32[5]{0:T(128)S(1)} %get-tuple-element.122, f32[256,256]{1,0:T(8,128)S(1)} %get-tuple-element.145, f32[5]{0:T(128)S(1)} %get-tuple-element.123, ...), kind=kLoop, calls=%fused_computation | loop fusion | flops 3276800 | bytes 1966180 | tf_op jit(solution)/shard_map/convert_element_type | solution.py:225
  18.2 1.6 %collective-permute-start.6 = (f32[28,8,256]{2,1,0:T(8,128)}, f32[28,8,256]{2,1,0:T(8,128)}, u32[]{:S(2)}, u32[]{:S(2)}) collective-permute-start(f32[28,8,256]{2,1,0:T(8,128)} %add.80), channel_id=1, source_target_pairs={{0,2},{1,3},{2,0},{3,1},{4,6},{5,7},{6,4},{7,5},{8,10},{9,11},{10,... | collective-permute-start | bytes 688136 | tf_op jit(solution)/shard_map/ppermute | solution.py:569
  21.7 4.5 %collective-permute-done.6 = f32[28,8,256]{2,1,0:T(8,128)} collective-permute-done((f32[28,8,256]{2,1,0:T(8,128)}, f32[28,8,256]{2,1,0:T(8,128)}, u32[]{:S(2)}, u32[]{:S(2)}) %collective-permute-start.6) | collective-permute-done | bytes 229408 | tf_op jit(solution)/shard_map/ppermute | solution.py:569
  26.2 1.1 add.81.refs_0_
  27.4 1.8 %fusion.1 = (bf16[512,16]{1,0:T(8,128)(2,1)}, bf16[512,16]{1,0:T(8,128)(2,1)}) fusion(f32[512,16]{1,0:T(8,128)} %copy.32, f32[512,16]{1,0:T(8,128)} %copy.33), kind=kLoop, calls=%fused_computation.6 | loop fusion | flops 49152 | bytes 98304 | tf_op jit(solution)/shard_map/convert_element_type | solution.py:33
  30.2 1.6 %cell_update.3 = (f32[40,8,256]{2,1,0:T(8,128)}, f32[12,8,256]{2,1,0:T(8,128)}, f32[14,8,256]{2,1,0:T(8,128)}, f32[8,16,256]{2,1,0:T(8,128)S(1)}) custom-call(f32[28,8,256]{2,1,0:T(8,128)S(1)} %add.81.refs_0_, f32[28,8,256]{2,1,0:T(8,128)S(1)} %collective-permute-done.7.refs_1_, f32[40,8,256]{2,1,0:T(8,128)S(1)} %copy-done.1, f32[12,8,256]{2,1,0:T(8,128)S(1)} %copy-done.3, ...), custom_call_target="tpu_custom_call" | custom-call | flops 1000 | bytes 1000 | tf_op jit(solution)/shard_map/cell_update/pallas_call | solution.py:189
  32.5 2.0 %collective-permute-start.9 = (f32[4,16,256]{2,1,0:T(8,128)}, f32[4,16,256]{2,1,0:T(8,128)}, u32[]{:S(2)}, u32[]{:S(2)}) collective-permute-start(f32[4,16,256]{2,1,0:T(8,128)} %get-tuple-element.131), channel_id=1, source_target_pairs={{4,0},{8,4},{12,8},{16,12},{20,16},{24,20},{28,24},{0,28},{5,1},{9... | collective-permute-start | bytes 196616 | tf_op jit(solution)/shard_map/ppermute | solution.py:605
  34.6 2.0 %concatenate.21.refs_5_.gain_w.refs_4_ = bf16[512,96]{1,0:T(8,128)(2,1)} concatenate(bf16[512,16]{1,0:T(8,128)(2,1)S(1)} %copy.34, bf16[512,16]{1,0:T(8,128)(2,1)S(1)} %copy.34, bf16[512,16]{1,0:T(8,128)(2,1)S(1)} %copy.34, bf16[512,16]{1,0:T(8,128)(2,1)} %get-tuple-element.128, bf16[512,16]{1,0:T(8,128)(2,1)} %get-tuple-element.128, bf16[512,16]{1,0:T(8,128)(2,1)} %get-tuple-element.127), dimensions={1} | concatenate | bytes 196608 | tf_op jit(solution)/shard_map/concatenate | solution.py:54
  36.7 1.2 %broadcast_in_dim.14 = bf16[5,2,256,256]{3,2,1,0:T(8,128)(2,1)S(1)} broadcast(bf16[5,256,256]{2,1,0:T(8,128)(2,1)} %add_convert_fusion), dimensions={0,2,3} | broadcast | bytes 1966080 | tf_op jit(solution)/shard_map/broadcast_in_dim | solution.py:225
  38.0 12.8 %day_one_inside.1 = (f32[8,512,256]{2,1,0:T(8,128)}, f32[4,64,256]{2,1,0:T(8,128)S(1)}) custom-call(f32[2,512,256]{2,1,0:T(8,128)S(1)} %get-tuple-element.95.refs_0_.first, f32[2,512,256]{2,1,0:T(8,128)S(1)} %get-tuple-element.103.refs_1_, f32[2,512,256]{2,1,0:T(8,128)} %get-tuple-element.102.refs_2_, f32[2,512,256]{2,1,0:T(8,128)S(1)} %get-tuple-element.94.refs_3_.last, ...), custom_call_target="tpu_custom_call" | custom-call | flops 1000 | bytes 1000 | tf_op jit(solution)/shard_map/day_one_inside/pallas_call | solution.py:289
  50.8 6.5 %collective-permute-done.9.after = f32[4,16,256]{2,1,0:T(8,128)} collective-permute-done((f32[4,16,256]{2,1,0:T(8,128)}, f32[4,16,256]{2,1,0:T(8,128)}, u32[]{:S(2)}, u32[]{:S(2)}) %collective-permute-start.9) | collective-permute-done | bytes 65568 | tf_op jit(solution)/shard_map/ppermute | solution.py:605
  57.6 4.5 %collective-permute-start.11 = (f32[2,512,256]{2,1,0:T(8,128)S(1)}, f32[2,512,256]{2,1,0:T(8,128)}, u32[]{:S(2)}, u32[]{:S(2)}) collective-permute-start(f32[2,512,256]{2,1,0:T(8,128)S(1)} %get-tuple-element.103.refs_1_), channel_id=1, source_target_pairs={{4,0},{8,4},{12,8},{16,12},{20,16},{24,20},{28,24},{0,28},{5,1},{9... | collective-permute-start | bytes 3145736 | tf_op jit(solution)/shard_map/ppermute | solution.py:605
  63.3 1.4 %slice.55 = f32[2,16,256]{2,1,0:T(8,128)} slice(f32[4,16,256]{2,1,0:T(8,128)} %collective-permute-done.8.before), slice={[0:2], [0:16], [0:256]} | slice | bytes 65536 | tf_op jit(solution)/shard_map/slice | solution.py:687
  64.6 1.4 %slice.56 = f32[2,16,256]{2,1,0:T(8,128)} slice(f32[4,16,256]{2,1,0:T(8,128)} %collective-permute-done.9.after), slice={[2:4], [0:16], [0:256]} | slice | bytes 65536 | tf_op jit(solution)/shard_map/slice | solution.py:687
  66.1 18.4 %conditional.1 = (f32[4,512,256]{2,1,0:T(8,128)}, f32[40,8,256]{2,1,0:T(8,128)}, f32[12,8,256]{2,1,0:T(8,128)}, f32[14,8,256]{2,1,0:T(8,128)}, f32[8,16,256]{2,1,0:T(8,128)S(1)}) conditional(s32[]{:T(128)} %bitcast.6, () %tuple.18, (f32[2,512,256]{2,1,0:T(8,128)}, f32[2,512,256]{2,1,0:T(8,128)}, f32[8,512,256]{2,1,0:T(8,128)}, ...), branch_computations={%region_2.0_spmd, %region_3.0_spmd} | conditional | flops 116688 | bytes 4130928 | solution.py:664
  66.1 6.0 %day_one_rim.1 = (f32[4,512,256]{2,1,0:T(8,128)}, f32[28,8,256]{2,1,0:T(8,128)S(1)}, f32[28,8,256]{2,1,0:T(8,128)S(1)}) custom-call(f32[2,512,256]{2,1,0:T(8,128)} %get-tuple-element.38.low, f32[2,512,256]{2,1,0:T(8,128)} %get-tuple-element.39.high, f32[8,512,256]{2,1,0:T(8,128)} %get-tuple-element.40.first.last, ...), custom_call_target="tpu_custom_call" | custom-call | flops 1000 | bytes 1000 | tf_op jit(solution)/shard_map/cond/branch_1_fun/day_one_rim/pallas_call | solution.py:346
  72.1 1.5 %collective-permute-done = f32[28,8,256]{2,1,0:T(8,128)S(1)} collective-permute-done((f32[28,8,256]{2,1,0:T(8,128)S(1)}, f32[28,8,256]{2,1,0:T(8,128)S(1)}, u32[]{:S(2)}, u32[]{:S(2)}) %collective-permute-start) | collective-permute-done | bytes 229408 | tf_op jit(solution)/shard_map/cond/branch_1_fun/ppermute | solution.py:569
  73.6 1.6 %collective-permute-start.1 = (f32[28,8,256]{2,1,0:T(8,128)S(1)}, f32[28,8,256]{2,1,0:T(8,128)S(1)}, u32[]{:S(2)}, u32[]{:S(2)}) collective-permute-start(f32[28,8,256]{2,1,0:T(8,128)S(1)} %add.66), channel_id=1, source_target_pairs={{0,2},{1,3},{2,0},{3,1},{4,6},{5,7},{6,4},{7,5},{8,10},{9,11},{10,... | collective-permute-start | bytes 688136 | tf_op jit(solution)/shard_map/cond/branch_1_fun/ppermute | solution.py:569
  75.2 6.1 %collective-permute-done.1 = f32[28,8,256]{2,1,0:T(8,128)S(1)} collective-permute-done((f32[28,8,256]{2,1,0:T(8,128)S(1)}, f32[28,8,256]{2,1,0:T(8,128)S(1)}, u32[]{:S(2)}, u32[]{:S(2)}) %collective-permute-start.1) | collective-permute-done | bytes 229408 | tf_op jit(solution)/shard_map/cond/branch_1_fun/ppermute | solution.py:569
  81.4 1.5 %collective-permute-done.2.refs_1_ = f32[28,8,256]{2,1,0:T(8,128)S(1)} collective-permute-done((f32[28,8,256]{2,1,0:T(8,128)S(1)}, f32[28,8,256]{2,1,0:T(8,128)S(1)}, u32[]{:S(2)}, u32[]{:S(2)}) %collective-permute-start.2) | collective-permute-done | bytes 229408 | tf_op jit(solution)/shard_map/cond/branch_1_fun/ppermute | solution.py:569
  82.9 1.6 %cell_update.2 = (f32[40,8,256]{2,1,0:T(8,128)}, f32[12,8,256]{2,1,0:T(8,128)}, f32[14,8,256]{2,1,0:T(8,128)}, f32[8,16,256]{2,1,0:T(8,128)S(1)}) custom-call(f32[28,8,256]{2,1,0:T(8,128)S(1)} %add.67.refs_0_, f32[28,8,256]{2,1,0:T(8,128)S(1)} %collective-permute-done.2.refs_1_, f32[40,8,256]{2,1,0:T(8,128)S(1)} %get-tuple-element.52.refs_2_, ...), custom_call_target="tpu_custom_call" | custom-call | flops 1000 | bytes 1000 | tf_op jit(solution)/shard_map/cond/branch_1_fun/cell_update/pallas_call | solution.py:189
  84.6 4.7 %collective-permute-start.13 = (f32[2,16,256]{2,1,0:T(8,128)S(1)}, f32[2,16,256]{2,1,0:T(8,128)S(1)}, u32[]{:S(2)}, u32[]{:S(2)}) collective-permute-start(f32[2,16,256]{2,1,0:T(8,128)S(1)} %get-tuple-element.130), channel_id=1, source_target_pairs={{4,0},{8,4},{12,8},{16,12},{20,16},{24,20},{28,24},{0,28},{5,1},{9... | collective-permute-start | bytes 98312 | tf_op jit(solution)/shard_map/ppermute | solution.py:605
  90.1 4.9 %day_one_beyond.1.near_low.near_high = f32[4,512,256]{2,1,0:T(8,128)S(1)} custom-call(f32[2,512,256]{2,1,0:T(8,128)} %collective-permute-done.3.low, f32[2,512,256]{2,1,0:T(8,128)} %collective-permute-done.4.high, f32[2,512,256]{2,1,0:T(8,128)S(1)} %get-tuple-element.95.refs_0_.first, f32[2,512,256]{2,1,0:T(8,128)S(1)} %get-tuple-element.94.refs_3_.last, ...), custom_call_target="tpu_custom_call" | custom-call | flops 1000 | bytes 1000 | tf_op jit(solution)/shard_map/day_one_beyond/pallas_call | solution.py:395
  95.0 8.0 %day_two.1 = (f32[512,8,256]{2,1,0:T(8,128)}, f32[4,512,256]{2,1,0:T(8,128)S(1)}) custom-call(f32[8,512,256]{2,1,0:T(8,128)} %get-tuple-element.108.refs_0_.refs_1_, f32[8,512,256]{2,1,0:T(8,128)} %get-tuple-element.108.refs_0_.refs_1_, f32[4,512,256]{2,1,0:T(8,128)S(1)} %copy-done.6, f32[8,16,256]{2,1,0:T(8,128)S(1)} %copy-done.12, ...), custom_call_target="tpu_custom_call" | custom-call | flops 1000 | bytes 1000 | tf_op jit(solution)/shard_map/day_two/pallas_call | solution.py:464
  103.2 3.8 %collective-permute-done.13 = f32[2,16,256]{2,1,0:T(8,128)S(1)} collective-permute-done((f32[2,16,256]{2,1,0:T(8,128)S(1)}, f32[2,16,256]{2,1,0:T(8,128)S(1)}, u32[]{:S(2)}, u32[]{:S(2)}) %collective-permute-start.13) | collective-permute-done | bytes 32800 | tf_op jit(solution)/shard_map/ppermute | solution.py:605
  107.1 4.9 %edges.1 = f32[512,8,256]{2,1,0:T(8,128)} custom-call(f32[2,512,256]{2,1,0:T(8,128)} %collective-permute-done.10.low, f32[2,512,256]{2,1,0:T(8,128)} %collective-permute-done.11.high, f32[4,512,256]{2,1,0:T(8,128)S(1)} %day_one_beyond.1.near_low.near_high, f32[4,512,256]{2,1,0:T(8,128)S(1)} %day_one_beyond.1.near_low.near_high, ...), custom_call_target="tpu_custom_call", output_to_operand_aliasing={{}: (10, {})} | custom-call | flops 1000 | bytes 1000 | tf_op jit(solution)/shard_map/edges/pallas_call | solution.py:536
  (112 shorter events, 8.1 us)
Async XLA Ops:
  4.3 53.0 %collective-permute-start.3 = (f32[2,512,256]{2,1,0:T(8,128)S(1)}, f32[2,512,256]{2,1,0:T(8,128)}, u32[]{:S(2)}, u32[]{:S(2)}) collective-permute-start(f32[2,512,256]{2,1,0:T(8,128)S(1)} %get-tuple-element.94.refs_3_.last), channel_id=1, source_target_pairs={{0,4},{4,8},{8,12},{12,16},{16,20},{20,24},{24,28},{28,0},{1,5},{5... | collective-permute-start | bytes 3145736 | tf_op jit(solution)/shard_map/ppermute | solution.py:602
  7.3 50.0 %collective-permute-start.4 = (f32[2,512,256]{2,1,0:T(8,128)S(1)}, f32[2,512,256]{2,1,0:T(8,128)}, u32[]{:S(2)}, u32[]{:S(2)}) collective-permute-start(f32[2,512,256]{2,1,0:T(8,128)S(1)} %get-tuple-element.95.refs_0_.first), channel_id=1, source_target_pairs={{4,0},{8,4},{12,8},{16,12},{20,16},{24,20},{28,24},{0,28},{5,1},{9... | collective-permute-start | bytes 3145736 | tf_op jit(solution)/shard_map/ppermute | solution.py:605
  14.9 2.5 %collective-permute-start.5 = (f32[28,8,256]{2,1,0:T(8,128)S(1)}, f32[28,8,256]{2,1,0:T(8,128)S(1)}, u32[]{:S(2)}, u32[]{:S(2)}) collective-permute-start(f32[28,8,256]{2,1,0:T(8,128)S(1)} %get-tuple-element.99), channel_id=1, source_target_pairs={{0,1},{1,0},{2,3},{3,2},{4,5},{5,4},{6,7},{7,6},{8,9},{9,8},{10,11... | collective-permute-start | bytes 688136 | tf_op jit(solution)/shard_map/ppermute | solution.py:569
  17.4 11.7 %copy-start.2 = (f32[14,8,256]{2,1,0:T(8,128)S(1)}, f32[14,8,256]{2,1,0:T(8,128)}, u32[]{:S(2)}) copy-start(f32[14,8,256]{2,1,0:T(8,128)} %refs_4_.1) | copy-start | bytes 344068
  17.4 11.7 %copy-start.3 = (f32[12,8,256]{2,1,0:T(8,128)S(1)}, f32[12,8,256]{2,1,0:T(8,128)}, u32[]{:S(2)}) copy-start(f32[12,8,256]{2,1,0:T(8,128)} %refs_3_.1) | copy-start | bytes 294916
  17.4 11.7 %copy-start.20 = (f32[40]{0:T(128)S(1)}, f32[40]{0:T(128)}, u32[]{:S(2)}) copy-start(f32[40]{0:T(128)} %refs_6_.1) | copy-start | bytes 484
  17.4 11.7 %copy-start.21 = (f32[40]{0:T(128)S(1)}, f32[40]{0:T(128)}, u32[]{:S(2)}) copy-start(f32[40]{0:T(128)} %refs_7_.1) | copy-start | bytes 484
  17.5 11.7 %copy-start.22 = (f32[40]{0:T(128)S(1)}, f32[40]{0:T(128)}, u32[]{:S(2)}) copy-start(f32[40]{0:T(128)} %refs_8_.1) | copy-start | bytes 484
  17.5 11.7 %copy-start.23 = (f32[14]{0:T(128)S(1)}, f32[14]{0:T(128)}, u32[]{:S(2)}) copy-start(f32[14]{0:T(128)} %refs_9_.1) | copy-start | bytes 172
  17.5 11.7 %copy-start.25 = (s32[40]{0:T(128)S(1)}, s32[40]{0:T(128)}, u32[]{:S(2)}) copy-start(s32[40]{0:T(128)} %refs_10_.1) | copy-start | bytes 484
  18.2 8.0 %collective-permute-start.6 = (f32[28,8,256]{2,1,0:T(8,128)}, f32[28,8,256]{2,1,0:T(8,128)}, u32[]{:S(2)}, u32[]{:S(2)}) collective-permute-start(f32[28,8,256]{2,1,0:T(8,128)} %add.80), channel_id=1, source_target_pairs={{0,2},{1,3},{2,0},{3,1},{4,6},{5,7},{6,4},{7,5},{8,10},{9,11},{10,... | collective-permute-start | bytes 688136 | tf_op jit(solution)/shard_map/ppermute | solution.py:569
  21.7 12.8 %copy-start.27 = (f32[512]{0:T(512)S(1)}, f32[512]{0:T(512)}, u32[]{:S(2)}) copy-start(f32[512]{0:T(512)} %param.28) | copy-start | bytes 6148
  27.3 1.9 %collective-permute-start.7 = (f32[28,8,256]{2,1,0:T(8,128)S(1)}, f32[28,8,256]{2,1,0:T(8,128)S(1)}, u32[]{:S(2)}, u32[]{:S(2)}) collective-permute-start(f32[28,8,256]{2,1,0:T(8,128)S(1)} %add.81.refs_0_), channel_id=1, source_target_pairs={{0,1},{1,0},{2,3},{3,2},{4,5},{5,4},{6,7},{7,6},{8,9},{9,8},{10,11... | collective-permute-start | bytes 688136 | tf_op jit(solution)/shard_map/ppermute | solution.py:569
  32.5 24.8 %collective-permute-start.9 = (f32[4,16,256]{2,1,0:T(8,128)}, f32[4,16,256]{2,1,0:T(8,128)}, u32[]{:S(2)}, u32[]{:S(2)}) collective-permute-start(f32[4,16,256]{2,1,0:T(8,128)} %get-tuple-element.131), channel_id=1, source_target_pairs={{4,0},{8,4},{12,8},{16,12},{20,16},{24,20},{28,24},{0,28},{5,1},{9... | collective-permute-start | bytes 196616 | tf_op jit(solution)/shard_map/ppermute | solution.py:605
  34.4 22.9 %collective-permute-start.8 = (f32[4,16,256]{2,1,0:T(8,128)}, f32[4,16,256]{2,1,0:T(8,128)}, u32[]{:S(2)}, u32[]{:S(2)}) collective-permute-start(f32[4,16,256]{2,1,0:T(8,128)} %get-tuple-element.132), channel_id=1, source_target_pairs={{0,4},{4,8},{8,12},{12,16},{16,20},{20,24},{24,28},{28,0},{1,5},{5... | collective-permute-start | bytes 196616 | tf_op jit(solution)/shard_map/ppermute | solution.py:602
  37.9 28.1 %copy-start.4 = (bf16[5,2,256,256]{3,2,1,0:T(8,128)(2,1)}, bf16[5,2,256,256]{3,2,1,0:T(8,128)(2,1)S(1)}, u32[]{:S(2)}) copy-start(bf16[5,2,256,256]{3,2,1,0:T(8,128)(2,1)S(1)} %broadcast_in_dim.14) | copy-start | bytes 3932164
  38.0 24.1 %copy-start.30 = (s32[8,2]{0,1:T(2,128)S(1)}, s32[8,2]{0,1:T(2,128)}, u32[]{:S(2)}) copy-start(s32[8,2]{0,1:T(2,128)} %param.33) | copy-start | bytes 196
  38.0 28.0 %copy-start.13 = (f32[40,8,256]{2,1,0:T(8,128)S(1)}, f32[40,8,256]{2,1,0:T(8,128)}, u32[]{:S(2)}) copy-start(f32[40,8,256]{2,1,0:T(8,128)} %get-tuple-element.110) | copy-start | bytes 983044
  38.0 28.0 %copy-start.14 = (f32[14,8,256]{2,1,0:T(8,128)S(1)}, f32[14,8,256]{2,1,0:T(8,128)}, u32[]{:S(2)}) copy-start(f32[14,8,256]{2,1,0:T(8,128)} %get-tuple-element.112) | copy-start | bytes 344068
  38.0 28.0 %copy-start.15 = (f32[12,8,256]{2,1,0:T(8,128)S(1)}, f32[12,8,256]{2,1,0:T(8,128)}, u32[]{:S(2)}) copy-start(f32[12,8,256]{2,1,0:T(8,128)} %get-tuple-element.111) | copy-start | bytes 294916
  38.0 28.0 %copy-start.24 = (f32[14]{0:T(128)S(1)}, f32[14]{0:T(128)}, u32[]{:S(2)}) copy-start(f32[14]{0:T(128)} %refs_9_.1) | copy-start | bytes 172
  38.0 28.0 %copy-start.26 = (s32[40]{0:T(128)S(1)}, s32[40]{0:T(128)}, u32[]{:S(2)}) copy-start(s32[40]{0:T(128)} %refs_10_.1) | copy-start | bytes 484
  57.3 49.7 %collective-permute-start.10 = (f32[2,512,256]{2,1,0:T(8,128)}, f32[2,512,256]{2,1,0:T(8,128)}, u32[]{:S(2)}, u32[]{:S(2)}) collective-permute-start(f32[2,512,256]{2,1,0:T(8,128)} %get-tuple-element.102.refs_2_), channel_id=1, source_target_pairs={{0,4},{4,8},{8,12},{12,16},{16,20},{20,24},{24,28},{28,0},{1,5},{5... | collective-permute-start | bytes 3145736 | tf_op jit(solution)/shard_map/ppermute | solution.py:602
  57.6 49.5 %collective-permute-start.11 = (f32[2,512,256]{2,1,0:T(8,128)S(1)}, f32[2,512,256]{2,1,0:T(8,128)}, u32[]{:S(2)}, u32[]{:S(2)}) collective-permute-start(f32[2,512,256]{2,1,0:T(8,128)S(1)} %get-tuple-element.103.refs_1_), channel_id=1, source_target_pairs={{4,0},{8,4},{12,8},{16,12},{20,16},{24,20},{28,24},{0,28},{5,1},{9... | collective-permute-start | bytes 3145736 | tf_op jit(solution)/shard_map/ppermute | solution.py:605
  72.1 1.5 %collective-permute-start = (f32[28,8,256]{2,1,0:T(8,128)S(1)}, f32[28,8,256]{2,1,0:T(8,128)S(1)}, u32[]{:S(2)}, u32[]{:S(2)}) collective-permute-start(f32[28,8,256]{2,1,0:T(8,128)S(1)} %get-tuple-element.51), channel_id=1, source_target_pairs={{0,1},{1,0},{2,3},{3,2},{4,5},{5,4},{6,7},{7,6},{8,9},{9,8},{10,11... | collective-permute-start | bytes 688136 | tf_op jit(solution)/shard_map/cond/branch_1_fun/ppermute | solution.py:569
  73.6 7.7 %collective-permute-start.1 = (f32[28,8,256]{2,1,0:T(8,128)S(1)}, f32[28,8,256]{2,1,0:T(8,128)S(1)}, u32[]{:S(2)}, u32[]{:S(2)}) collective-permute-start(f32[28,8,256]{2,1,0:T(8,128)S(1)} %add.66), channel_id=1, source_target_pairs={{0,2},{1,3},{2,0},{3,1},{4,6},{5,7},{6,4},{7,5},{8,10},{9,11},{10,... | collective-permute-start | bytes 688136 | tf_op jit(solution)/shard_map/cond/branch_1_fun/ppermute | solution.py:569
  81.3 1.6 %collective-permute-start.2 = (f32[28,8,256]{2,1,0:T(8,128)S(1)}, f32[28,8,256]{2,1,0:T(8,128)S(1)}, u32[]{:S(2)}, u32[]{:S(2)}) collective-permute-start(f32[28,8,256]{2,1,0:T(8,128)S(1)} %add.67.refs_0_), channel_id=1, source_target_pairs={{0,1},{1,0},{2,3},{3,2},{4,5},{5,4},{6,7},{7,6},{8,9},{9,8},{10,11... | collective-permute-start | bytes 688136 | tf_op jit(solution)/shard_map/cond/branch_1_fun/ppermute | solution.py:569
  84.5 18.7 %collective-permute-start.12 = (f32[2,16,256]{2,1,0:T(8,128)S(1)}, f32[2,16,256]{2,1,0:T(8,128)S(1)}, u32[]{:S(2)}, u32[]{:S(2)}) collective-permute-start(f32[2,16,256]{2,1,0:T(8,128)S(1)} %get-tuple-element.129), channel_id=1, source_target_pairs={{0,4},{4,8},{8,12},{12,16},{16,20},{20,24},{24,28},{28,0},{1,5},{5... | collective-permute-start | bytes 98312 | tf_op jit(solution)/shard_map/ppermute | solution.py:602
  84.6 22.5 %collective-permute-start.13 = (f32[2,16,256]{2,1,0:T(8,128)S(1)}, f32[2,16,256]{2,1,0:T(8,128)S(1)}, u32[]{:S(2)}, u32[]{:S(2)}) collective-permute-start(f32[2,16,256]{2,1,0:T(8,128)S(1)} %get-tuple-element.130), channel_id=1, source_target_pairs={{4,0},{8,4},{12,8},{16,12},{20,16},{24,20},{28,24},{0,28},{5,1},{9... | collective-permute-start | bytes 98312 | tf_op jit(solution)/shard_map/ppermute | solution.py:605
  90.1 4.9 %copy-start.6 = (f32[4,512,256]{2,1,0:T(8,128)S(1)}, f32[4,512,256]{2,1,0:T(8,128)}, u32[]{:S(2)}) copy-start(f32[4,512,256]{2,1,0:T(8,128)} %get-tuple-element.113.refs_2_) | copy-start | bytes 6291460
  90.1 4.9 %copy-start.8 = (bf16[512,96]{1,0:T(8,128)(2,1)S(1)}, bf16[512,96]{1,0:T(8,128)(2,1)}, u32[]{:S(2)}) copy-start(bf16[512,96]{1,0:T(8,128)(2,1)} %concatenate.21.refs_5_.gain_w.refs_4_) | copy-start | bytes 294916
  90.1 4.9 %copy-start.12 = (f32[8,16,256]{2,1,0:T(8,128)S(1)}, f32[8,16,256]{2,1,0:T(8,128)}, u32[]{:S(2)}) copy-start(f32[8,16,256]{2,1,0:T(8,128)} %copy-done.11) | copy-start | bytes 393220
  (13 other events, 29.9 us)

commit v3 on v2

--- a/solution.py
+++ b/solution.py
@@ -26,16 +26,7 @@
     return pl.CostEstimate(flops=flops, bytes_accessed=moved, transcendentals=0)
 
 
-def pieces_outside(x, count):
-    out = []
-    for _ in range(count):
-        part = lax.reduce_precision(x, 8, 7)
-        out.append(part.astype(BF16))
-        x = x - part
-    return out
-
-
-def pieces_inside(x, count):
+def split(x, count):
     out = []
     for _ in range(count):
         part = x.astype(BF16)
@@ -45,48 +36,55 @@
 
 
 def share_operand(share):
-    high, mid, low = pieces_inside(share, 3)
+    high, mid, low = split(share, 3)
     return jnp.concatenate([high, mid, low, high, mid, high], 0)
-
-
-def trait_operand(matrix):
-    high, mid, low = pieces_outside(matrix, 3)
-    return jnp.concatenate([high, high, high, mid, mid, low], 1)
 
 
 def matmul(a, b):
     return jnp.dot(a, b, preferred_element_type=F32)
 
 
-def take_rows(biomass, rows):
-    count, _, width = biomass.shape
+def take_first(biomass, rows, pieces):
+    count, height, width = biomass.shape
     pairs = len(rows) // 2
+    step = count // pieces
 
     def kernel(source, *refs):
-        outs, sem = refs[:-1], refs[-1]
-        copies = [
-            pltpu.make_async_copy(source.at[:, row, :], outs[i // 2].at[i % 2], sem.at[i])
-            for i, row in enumerate(rows)
-        ]
-        for copy in copies:
-            copy.start()
-        for copy in copies:
+        outs, held, arrived, left = refs[:pairs], refs[pairs], refs[pairs + 1], refs[pairs + 2]
+        loads, stores = [], []
+        for p in range(pieces):
+            taxa = pl.ds(p * step, step)
+            loads.append(pltpu.make_async_copy(source.at[taxa], held.at[taxa], arrived.at[p]))
+            loads[-1].start()
+        for p in range(pieces):
+            taxa = pl.ds(p * step, step)
+            loads[p].wait()
+            for i, row in enumerate(rows):
+                stores.append(
+                    pltpu.make_async_copy(held.at[taxa, row, :], outs[i // 2].at[i % 2, taxa], left.at[p, i])
+                )
+                stores[-1].start()
+        for copy in stores:
             copy.wait()
 
     return pl.pallas_call(
         kernel,
-        name="take_rows",
+        name="take_first",
         out_shape=[jax.ShapeDtypeStruct((2, count, width), F32)] * pairs,
         in_specs=[ANY],
         out_specs=[ANY] * pairs,
-        scratch_shapes=[pltpu.SemaphoreType.DMA((len(rows),))],
-        compiler_params=params(),
-        cost_estimate=cost(0, 8 * len(rows) * count * width),
+        scratch_shapes=[
+            pltpu.VMEM((count, height, width), F32),
+            pltpu.SemaphoreType.DMA((pieces,)),
+            pltpu.SemaphoreType.DMA((pieces, len(rows))),
+        ],
+        compiler_params=pltpu.CompilerParams(vmem_limit_bytes=60 << 20),
+        cost_estimate=cost(1000, 1000),
     )(biomass)
 
 
 def add_sums(total, row, x, weights):
-    high, low = pieces_inside(x, 2)
+    high, low = split(x, 2)
     first = matmul(weights, high)
     second = matmul(weights[:PADDED], low)
     total[row] += first[:PADDED] + first[PADDED:] + second
@@ -107,20 +105,89 @@
         other[...] = low
 
 
-def taxa_sums(row_pairs, weights, odd, block):
-    _, count, width = row_pairs[0].shape
-    rows = 2 * len(row_pairs)
-
-    def kernel(*refs):
-        pairs = refs[: len(row_pairs)]
-        weight, side, mine, other, total = refs[len(row_pairs) :]
+def sum_weights(enz_traits, mono_traits, prod_rate, uptake_rate):
+    n_enz, count = enz_traits.shape
+    used = n_enz + mono_traits.shape[0]
+
+    def kernel(enz, mono, prod, uptake, out, held):
+        held[:n_enz] = enz[...].astype(F32) * prod[...]
+        held[n_enz:used] = mono[...].astype(F32) * uptake[...]
+        held[used:] = jnp.zeros((PADDED - used, count), F32)
+        high, low = split(held[...], 2)
+        out[:PADDED] = high
+        out[PADDED:] = low
+
+    return pl.pallas_call(
+        kernel,
+        name="sum_weights",
+        out_shape=jax.ShapeDtypeStruct((2 * PADDED, count), BF16),
+        scratch_shapes=[pltpu.VMEM((PADDED, count), F32)],
+        compiler_params=params(),
+        cost_estimate=cost(1000, 1000),
+    )(enz_traits, mono_traits, prod_rate, uptake_rate)
+
+
+def spread_operands(enz_traits, mono_traits, prod_rate, uptake_rate, mortality, disperse, offsets, width):
+    count = enz_traits.shape[1]
+    n_mono = mono_traits.shape[0]
+
+    def kernel(enz, mono, prod, uptake, mort, disp, offs, gain, fraction, circulant, held, stacked):
+        held[...] = jnp.zeros_like(held)
+        held[:n_mono] = (YIELD * uptake[...]) * mono[...].astype(F32)
+        made = jnp.sum(enz[...].astype(F32), axis=0, keepdims=True)
+        held[n_mono : n_mono + 1] = 1.0 - mort[...] - prod[...] * made
+        high, mid, low = (part.astype(F32) for part in split(held[...], 3))
+        stacked[...] = jnp.zeros_like(stacked)
+        for i, part in enumerate((high, high, high, mid, mid, low)):
+            stacked[SLOTS * i : SLOTS * (i + 1)] = part
+        gain[...] = stacked[...].T[:, : 6 * SLOTS].astype(BF16)
+        fraction[...] = jnp.broadcast_to(disp[...] * (1.0 / KOFF), (HALF, count)).T
+        source = lax.broadcasted_iota(jnp.int32, (width, width), 0)
+        target = lax.broadcasted_iota(jnp.int32, (width, width), 1)
+        apart = (target - source + width + 2) & (width - 1)
+        for i in range(5):
+            total = jnp.zeros((width, width), F32)
+            for j in range(5):
+                number = jnp.int32(-KOFF if i == 2 and j == 2 else 0)
+                for k in range(KOFF):
+                    hit = (offs[k, 0] == 2 - i) & (offs[k, 1] == j - 2)
+                    number = number + hit.astype(jnp.int32)
+                total = jnp.where(apart == j, number.astype(F32), total)
+            circulant[width * i : width * (i + 1)] = total.astype(BF16)
+
+    vmem = pl.BlockSpec(memory_space=pltpu.VMEM)
+    return pl.pallas_call(
+        kernel,
+        name="spread_operands",
+        out_shape=[
+            jax.ShapeDtypeStruct((count, 6 * SLOTS), BF16),
+            jax.ShapeDtypeStruct((count, HALF), F32),
+            jax.ShapeDtypeStruct((5 * width, width), BF16),
+        ],
+        in_specs=[vmem] * 6 + [SMEM],
+        out_specs=[vmem] * 3,
+        scratch_shapes=[pltpu.VMEM((SLOTS, count), F32), pltpu.VMEM((HALF, count), F32)],
+        compiler_params=params(),
+        cost_estimate=cost(1000, 1000),
+    )(enz_traits, mono_traits, prod_rate, uptake_rate, mortality, disperse, offsets)
+
+
+def first_sums(biomass, weights, odd, block):
+    count, rows, width = biomass.shape
+    inner = rows // 2 - 2
+
+    def kernel(source, weight, side, *refs):
+        pairs, (mine, other, total) = refs[:inner], refs[inner:]
 
         @pl.when(pl.program_id(0) == 0)
         def _():
             total[...] = jnp.zeros_like(total)
 
+        x = jnp.swapaxes(source[...], 0, 1)
         for row in range(rows):
-            add_sums(total, row, pairs[row // 2][row % 2], weight[...])
+            if 2 <= row < rows - 2:
+                pairs[row // 2 - 1][row % 2] = x[row]
+            add_sums(total, row, x[row], weight[...])
 
         @pl.when(pl.program_id(0) == pl.num_programs(0) - 1)
         def _():
@@ -129,16 +196,19 @@
     half = (CHAN // 2, rows, width)
     return pl.pallas_call(
         kernel,
-        name="taxa_sums",
+        name="first_sums",
         grid=(count // block,),
-        out_shape=[jax.ShapeDtypeStruct(half, F32)] * 2,
-        in_specs=[pl.BlockSpec((2, block, width), lambda i: (0, i, 0))] * len(row_pairs)
-        + [pl.BlockSpec((2 * PADDED, block), lambda i: (0, i)), SMEM],
-        out_specs=[whole(half)] * 2,
+        out_shape=[jax.ShapeDtypeStruct((2, count, width), F32)] * inner + [jax.ShapeDtypeStruct(half, F32)] * 2,
+        in_specs=[
+            pl.BlockSpec((block, rows, width), lambda i: (i, 0, 0)),
+            pl.BlockSpec((2 * PADDED, block), lambda i: (0, i)),
+            SMEM,
+        ],
+        out_specs=[pair_spec(block, width)] * inner + [whole(half)] * 2,
         scratch_shapes=[pltpu.VMEM((rows, PADDED, width), F32)],
         compiler_params=params(),
         cost_estimate=cost(1000, 1000),
-    )(*row_pairs, weights, odd)
+    )(biomass, weights, odd)
 
 
 def cell_update(mine, rest, odd, enz, sub, mono, enz_loss, vmax, kmich, khalf, enz_target):
@@ -208,38 +278,22 @@
     )(mine, rest, enz, sub, mono, odd, enz_loss, vmax, kmich, khalf, enz_target)
 
 
-def circulants(offsets, width):
-    row_offset = 2 - lax.iota(jnp.int32, 5)
-    col_offset = lax.iota(jnp.int32, 5) - 2
-    row_hit = (offsets[:, 0, None] == row_offset[None, :]).astype(F32)
-    col_hit = (offsets[:, 1, None] == col_offset[None, :]).astype(F32)
-    number = jnp.sum(row_hit[:, :, None] * col_hit[:, None, :], axis=0)
-    still = (row_offset[:, None] == 0) & (col_offset[None, :] == 0)
-    number = number - KOFF * still.astype(F32)
-    source = lax.broadcasted_iota(jnp.int32, (width, width), 0)
-    target = lax.broadcasted_iota(jnp.int32, (width, width), 1)
-    apart = lax.rem(target - source + width + 2, width)
-    total = jnp.zeros((5, width, width), F32)
-    for i in range(5):
-        total = total + number[:, i, None, None] * (apart == i).astype(F32)
-    total = jnp.broadcast_to(total.astype(BF16)[:, None], (5, 2, width, width))
-    return total.reshape(10 * width, width)
-
-
 def store_pieces(pieces, index, value):
-    width = value.shape[1]
-    at = 2 * width * index
-    high, low = pieces_inside(value, 2)
-    pieces[:, at : at + width] = high
-    pieces[:, at + width : at + 2 * width] = low
+    count, width = value.shape
+    columns = slice(width * index, width * (index + 1))
+    high, low = split(value, 2)
+    pieces[:count, columns] = high
+    pieces[count:, columns] = low
 
 
 def stencil(pieces, circulant, first, count, offset):
-    span = circulant.shape[1] * 2
-    return matmul(
-        pieces[:, span * first : span * (first + count)],
-        circulant[span * offset : span * (offset + count), :],
-    )
+    width = circulant.shape[1]
+    both = matmul(
+        pieces[:, width * first : width * (first + count)],
+        circulant[width * offset : width * (offset + count), :],
+    )
+    half = both.shape[0] // 2
+    return both[:half] + both[half:]
 
 
 def window(target, rows):
@@ -270,7 +324,7 @@
 
     def kernel(*refs):
         pairs = refs[: len(row_pairs)]
-        own, gain_w, frac, circ, weight, out, total, pieces = refs[len(row_pairs) :]
+        own, gain_w, frac, circ, weight, out, to_next, to_previous, total, pieces = refs[len(row_pairs) :]
 
         @pl.when(pl.program_id(0) == 0)
         def _():
@@ -285,6 +339,10 @@
             out[row] = value
             if 2 <= row < rows - 2:
                 add_sums(total, row - 2, value, weight[...])
+        for i, (source, number, offset) in enumerate(TERMS):
+            source += rows - 4 if i < 2 else 0
+            value = spread(0.0, frac[...], stencil(pieces, circ, source, number, offset))
+            (to_next if i < 2 else to_previous)[i % 2] = value
 
     return pl.pallas_call(
         kernel,
@@ -292,6 +350,7 @@
         grid=(count // block,),
         out_shape=[
             jax.ShapeDtypeStruct((rows, count, width), F32),
+            *[jax.ShapeDtypeStruct((2, count, width), F32)] * 2,
             jax.ShapeDtypeStruct((inner, PADDED, width), F32),
         ],
         in_specs=[pair_spec(block, width)] * len(row_pairs)
@@ -304,9 +363,11 @@
         ],
         out_specs=[
             pl.BlockSpec((rows, block, width), lambda i: (0, i, 0)),
+            pair_spec(block, width),
+            pair_spec(block, width),
             whole((inner, PADDED, width)),
         ],
-        scratch_shapes=[pltpu.VMEM((block, rows * 2 * width), BF16)],
+        scratch_shapes=[pltpu.VMEM((2 * block, rows * width), BF16)],
         compiler_params=params(),
         cost_estimate=cost(1000, 1000),
     )(*row_pairs, share, gain, fraction, circulant, weights)
@@ -330,7 +391,7 @@
 
         for i in range(4):
             x = low[i] if i < 2 else high[i - 2]
-            s = before[2 + i] if i < 2 else after[i - 2]
+            s = before[i] if i < 2 else after[i - 2]
             store_pieces(far, i, x * matmul(gain_w[...], share_operand(s)))
         for i in range(4):
             x = first[i] if i < 2 else last[i - 2]
@@ -364,7 +425,7 @@
         ],
         out_specs=[pl.BlockSpec((4, block, width), lambda i: (0, i, 0))] + [whole(half)] * 2,
         scratch_shapes=[
-            pltpu.VMEM((block, 8 * width), BF16),
+            pltpu.VMEM((2 * block, 4 * width), BF16),
             pltpu.VMEM((rows, PADDED, width), F32),
         ],
         compiler_params=params(),
@@ -381,7 +442,7 @@
             for i in range(4):
                 if side == 0:
                     x = low[i] if i < 2 else first[i - 2]
-                    s = before[2 + i] if i < 2 else own[i - 2]
+                    s = before[i] if i < 2 else own[i - 2]
                 else:
                     x = last[i] if i < 2 else high[i - 2]
                     s = own[rows - 2 + i] if i < 2 else after[i - 2]
@@ -407,7 +468,7 @@
             whole(circulant.shape),
         ],
         out_specs=pl.BlockSpec((4, block, width), lambda i: (0, i, 0)),
-        scratch_shapes=[pltpu.VMEM((block, 8 * width), BF16)],
+        scratch_shapes=[pltpu.VMEM((2 * block, 4 * width), BF16)],
         compiler_params=params(),
         cost_estimate=cost(1000, 1000),
     )(low, high, row_pairs[0], row_pairs[-1], share, share_low, share_high, gain, fraction, circulant)
@@ -479,7 +540,7 @@
         ],
         out_specs=[ANY, ANY],
         scratch_shapes=[
-            pltpu.VMEM((block, rows * 2 * width), BF16),
+            pltpu.VMEM((2 * block, rows * width), BF16),
             pltpu.VMEM((2, rows, block, width), F32),
             pltpu.SemaphoreType.DMA((2, rows)),
         ],
@@ -488,12 +549,14 @@
     )(*[inside] * middle, rim, share, gain, fraction, circulant)
 
 
-def edges(outer_low, outer_high, beyond, edge, biomass_out, share_one, share_two, gain, fraction, circulant, block):
-    _, count, width = outer_low.shape
+def edges(early_low, late_low, from_high, beyond, edge, biomass_out, share_low, share_high, gain, fraction, circulant, block):
+    _, count, width = from_high.shape
     rows = biomass_out.shape[1]
     steps = count // block
 
-    def kernel(low, high, near_low, near_high, own, s1, s2, gain_w, frac, circ, unused, out, far, near, result, sem):
+    def kernel(
+        early, late, high, near_low, near_high, own, before, after, gain_w, frac, circ, unused, out, near, result, sem
+    ):
         step = pl.program_id(0)
         slot = lax.rem(step, 2)
 
@@ -514,12 +577,12 @@
                 copy.wait()
 
         for i in range(4):
-            x = low[i] if i < 2 else high[i - 2]
-            store_pieces(far, i, x * matmul(gain_w[...], share_operand(s1[i])))
-        for i in range(4):
-            x = near_low[i] if i < 2 else near_high[i - 2]
-            value = spread(x, frac[...], stencil(far, circ, *TERMS[i]))
-            store_pieces(near, i, value * matmul(gain_w[...], share_operand(s2[i])))
+            if i < 2:
+                value = near_low[i] + jnp.where(step == 0, early[i], late[i])
+            else:
+                value = near_high[i - 2] + high[i - 2]
+            s = before[i] if i < 2 else after[i - 2]
+            store_pieces(near, i, value * matmul(gain_w[...], share_operand(s)))
         for i in range(4):
             result[slot, i] = spread(own[i], frac[...], stencil(near, circ, *TERMS[i]))
         for copy in copies(step, slot):
@@ -539,11 +602,14 @@
         grid=(steps,),
         out_shape=jax.ShapeDtypeStruct(biomass_out.shape, F32),
         in_specs=[
-            *[pair_spec(block, width)] * 3,
-            pair_spec(block, width, 1),
+            whole(early_low.shape),
+            whole(late_low.shape),
+            pair_spec(block, width),
+            pl.BlockSpec((2, block, width), lambda i: (0, i, 0)),
+            pl.BlockSpec((2, block, width), lambda i: (1, i, 0)),
             pl.BlockSpec((4, block, width), lambda i: (0, i, 0)),
-            whole(share_one.shape),
-            whole(share_two.shape),
+            whole(share_low.shape),
+            whole(share_high.shape),
             pl.BlockSpec((block, gain.shape[1]), lambda i: (i, 0)),
             pl.BlockSpec((block, HALF), lambda i: (i, 0)),
             whole(circulant.shape),
@@ -551,15 +617,27 @@
         ],
         out_specs=ANY,
         scratch_shapes=[
-            pltpu.VMEM((block, 8 * width), BF16),
-            pltpu.VMEM((block, 8 * width), BF16),
+            pltpu.VMEM((2 * block, 4 * width), BF16),
             pltpu.VMEM((2, 4, block, width), F32),
             pltpu.SemaphoreType.DMA((2, 4)),
         ],
-        input_output_aliases={10: 0},
-        compiler_params=params(),
-        cost_estimate=cost(1000, 1000),
-    )(outer_low, outer_high, beyond, beyond, edge, share_one, share_two, gain, fraction, circulant, biomass_out)
+        input_output_aliases={11: 0},
+        compiler_params=params(),
+        cost_estimate=cost(1000, 1000),
+    )(
+        early_low,
+        late_low,
+        from_high,
+        beyond,
+        beyond,
+        edge,
+        share_low,
+        share_high,
+        gain,
+        fraction,
+        circulant,
+        biomass_out,
+    )
 
 
 def over_taxa(mine, other):
@@ -574,6 +652,13 @@
         mine = mine + exchange(mine, step)
         step *= 2
     return mine, exchange(mine, 1)
+
+
+def as_branch(offsets, run, *operands):
+    def unused(*operands):
+        return jax.tree.map(lambda x: jnp.zeros(x.shape, x.dtype), jax.eval_shape(run, *operands))
+
+    return lax.cond(offsets[0, 0] < 3, run, unused, *operands)
 
 
 def body(
@@ -607,48 +692,33 @@
     count, rows, width = biomass.shape
     block = min(count, 256)
 
-    first, last = take_rows(biomass, (0, 1, rows - 2, rows - 1))
+    first, last = take_first(biomass, (0, 1, rows - 2, rows - 1), 4)
     inner_low, inner_high = down(last), up(first)
-    middle = take_rows(biomass, tuple(range(2, rows - 2)))
+    odd = lax.rem(lax.axis_index("taxa"), 2).reshape(1).astype(jnp.int32)
+    traits = (enz_traits.T, mono_traits.T, prod_rate.reshape(1, count), uptake_rate.reshape(1, count))
+    cells = (enz_loss, vmax, kmich, khalf, enz_target)
+
+    def sums_and_cells(biomass, enzymes, substrates, monomers):
+        weights = sum_weights(*traits)
+        *middle, mine, other = first_sums(biomass, weights, odd, block)
+        sums = over_taxa(mine, other)
+        return *middle, weights, *cell_update(*sums, odd, enzymes, substrates, monomers, *cells)
+
+    *middle, weights, enzymes, substrates, monomers, share_one = as_branch(
+        offsets, sums_and_cells, biomass, enzymes, substrates, monomers
+    )
     row_pairs = [first, *middle, last]
-
-    enz_f = enz_traits.astype(F32)
-    mono_f = mono_traits.astype(F32)
-    weight = jnp.concatenate(
-        [
-            enz_f * prod_rate[:, None],
-            mono_f * uptake_rate[:, None],
-            jnp.zeros((count, PADDED - enz_f.shape[1] - mono_f.shape[1]), F32),
-        ],
-        1,
-    ).T
-    weights = jnp.concatenate(pieces_outside(weight, 2), 0)
-    keep = 1.0 - mortality - prod_rate * jnp.sum(enz_f, axis=1)
-    gain = jnp.concatenate(
-        [
-            (YIELD * uptake_rate)[:, None] * mono_f,
-            keep[:, None],
-            jnp.zeros((count, SLOTS - 1 - mono_f.shape[1]), F32),
-        ],
-        1,
-    )
-    gain = trait_operand(gain)
-    fraction = jnp.broadcast_to((disperse / KOFF)[:, None], (count, HALF))
-    circulant = circulants(offsets, width)
-    cells = (enz_loss, vmax, kmich, khalf, enz_target)
-
-    odd = lax.rem(lax.axis_index("taxa"), 2).reshape(1).astype(jnp.int32)
-
-    sums = over_taxa(*taxa_sums(row_pairs, weights, odd, block))
-    enzymes, substrates, monomers, share_one = cell_update(*sums, odd, enzymes, substrates, monomers, *cells)
-    share_low, share_high = down(share_one[rows - 4 :]), up(share_one[:4])
-    spreading = (gain, fraction, circulant)
-    inside, inside_sums = day_one_inside(row_pairs, share_one, *spreading, weights, block)
-
-    inner_low, inner_high, share_low, share_high, inside, outer_first, outer_last = lax.optimization_barrier(
-        (inner_low, inner_high, share_low, share_high, inside, middle[0], middle[-1])
-    )
-    outer_low, outer_high = down(outer_last), up(outer_first)
+    spreading = spread_operands(
+        *traits, mortality.reshape(1, count), disperse.reshape(1, count), offsets, width
+    )
+    share_low, share_high = down(share_one[rows - 2 :]), up(share_one[:2])
+    inside, to_next, to_previous, inside_sums = day_one_inside(row_pairs, share_one, *spreading, weights, block)
+
+    early = count // 2
+    inner_low, inner_high, share_low, share_high, inside, next_early, to_previous = lax.optimization_barrier(
+        (inner_low, inner_high, share_low, share_high, inside, to_next[:, :early], to_previous)
+    )
+    from_low, from_high = down(next_early), up(to_previous)
 
     def rest_of_day_one(low, high, share_low, share_high, enzymes, substrates, monomers):
         rim, *sums = day_one_rim(
@@ -657,14 +727,9 @@
         sums = over_taxa(*sums)
         return rim, *cell_update(*sums, odd, enzymes, substrates, monomers, *cells)
 
-    def unused(*operands):
-        shapes = jax.eval_shape(rest_of_day_one, *operands)
-        return jax.tree.map(lambda x: jnp.zeros(x.shape, x.dtype), shapes)
-
-    rim, enzymes, substrates, monomers, share_two = lax.cond(
-        offsets[0, 0] < 3,
+    rim, enzymes, substrates, monomers, share_two = as_branch(
+        offsets,
         rest_of_day_one,
-        unused,
         inner_low,
         inner_high,
         share_low,
@@ -674,22 +739,15 @@
         monomers,
     )
     near_low, near_high = down(share_two[rows - 2 :]), up(share_two[:2])
+    inner_low, inner_high, share_two = lax.optimization_barrier((inner_low, inner_high, share_two))
     beyond = day_one_beyond(
         row_pairs, inner_low, inner_high, share_one, share_low, share_high, *spreading, block
     )
+    beyond, next_late = lax.optimization_barrier((beyond, to_next[:, early:]))
+    late_low = down(next_late)
     biomass_out, edge = day_two(inside, rim, share_two, *spreading, block)
     biomass_out = edges(
-        outer_low,
-        outer_high,
-        beyond,
-        edge,
-        biomass_out,
-        jnp.concatenate([share_low[:2], share_high[2:]], 0),
-        jnp.concatenate([near_low, near_high], 0),
-        gain,
-        fraction,
-        circulant,
-        block,
+        from_low, late_low, from_high, beyond, edge, biomass_out, near_low, near_high, *spreading, early
     )
     return (biomass_out, enzymes, substrates, monomers)
 

time: 113 us -> 108 us (0.956)
  waiting for transfers between devices: 24 us -> 36.4 us
  local copies, waits for them, and re-layouts: 13 us -> 2.44 us
  other arithmetic: 6.49 us -> 0.12 us
  Pallas kernels: 45.4 us -> 47 us
  starting transfers between devices: 21.1 us -> 19.7 us
    ppermute x4, waiting for transfers between devices: 10.3 us -> 18.3 us  [up(): return lax.ppermute(x, 'space', backward)]
    ppermute x6, waiting for transfers between devices: 13.6 us -> 18 us  [exchange(): return lax.ppermute(x, 'taxa', [(i, i ^ step) for i in range(count)])]
    pallas_call x3 -> x4, Pallas kernels: 5.63 us -> 9.66 us  [the longest x1 4.65 us: first_sums(): pl.pallas_call(kernel, name='first_sums', grid=(count // block,), out_sha...]
    convert_element_type x9 -> x0, other arithmetic: 3.53 us -> none  [the longest x3 1.88 us: pieces_outside(): out.append(part.astype(BF16))]
    unnamed x62 -> x63, local copies, waits for them, and re-layouts: 3.64 us -> 0.24 us
    concatenate x4 -> x0, local copies, waits for them, and re-layouts: 2.96 us -> none  [the longest x1 1.97 us: trait_operand(): return jnp.concatenate([high, high, high, mid, mid, low], 1)]
    slice x6 -> x3, local copies, waits for them, and re-layouts: 4.15 us -> 2.18 us  [the longest x1 1.01 us: body(): beyond, next_late = lax.optimization_barrier((beyond, to_next[:, early:]))]
    broadcast_in_dim x3 -> x0, local copies, waits for them, and re-layouts: 1.31 us -> none  [the longest x1 1.19 us: circulants(): total = jnp.broadcast_to(total.astype(BF16)[:, None], (5, 2, width, width))]
  transfers between devices with their start and end apart: 14 -> 15, of which waited for: 7 -> 8; matrix products, arithmetic and copies ran while one was open for 14% -> 2% of each run, Pallas kernels for 35% -> 37%
where the time goes in v3:
time: 108 us
  Pallas kernels  47 us (44%)
  waiting for transfers between devices  36.4 us (34%)
  starting transfers between devices  19.7 us (18%)
  local copies, waits for them, and re-layouts  2.44 us (2%)
  between operations  1.91 us (2%)
    ppermute x4, waiting for transfers between devices, up(): return lax.ppermute(x, 'space', backward)  18.3 us
    ppermute x6, waiting for transfers between devices, exchange(): return lax.ppermute(x, 'taxa', [(i, i ^ step) for i in range(count)])  18 us
    ppermute x4, starting transfers between devices, up(): return lax.ppermute(x, 'space', backward)  13.1 us
    pallas_call x1, Pallas kernels, day_one_inside(): pl.pallas_call(kernel, name='day_one_inside', grid=(count // block,), out...  13 us
    pallas_call x1, Pallas kernels, day_two(): pl.pallas_call(kernel, name='day_two', grid=(steps,), out_shape=[jax.Shap...  7.16 us
    pallas_call x1, Pallas kernels, day_one_rim(): pl.pallas_call(kernel, name='day_one_rim', grid=(count // block,), out_sh...  5.44 us
    pallas_call x1, Pallas kernels, day_one_beyond(): pl.pallas_call(kernel, name='day_one_beyond', grid=(count // block,), out...  4.69 us
    pallas_call x1, Pallas kernels, first_sums(): pl.pallas_call(kernel, name='first_sums', grid=(count // block,), out_sha...  4.65 us
  transfers between devices with their start and end apart: 15, of which 8 were waited for; matrix products, arithmetic and copies ran while one was open for 2% of the time, Pallas kernels for 37%

profile of v3, /device:TPU:0, one launch (start us, length us, event | category | flops | bytes accessed | tf_op | source)
XLA Modules:
  0.0 107.7 jit_solution(6424084948400532842)
XLA Ops:
  0.8 3.3 %take_first.1 = (f32[2,512,256]{2,1,0:T(8,128)}, f32[2,512,256]{2,1,0:T(8,128)}) custom-call(f32[512,8,256]{2,1,0:T(8,128)} %source.1), custom_call_target="tpu_custom_call" | custom-call | flops 1000 | bytes 1000 | tf_op jit(solution)/shard_map/take_first/pallas_call | solution.py:70
  4.0 3.0 %collective-permute-start.6 = (f32[2,512,256]{2,1,0:T(8,128)}, f32[2,512,256]{2,1,0:T(8,128)}, u32[]{:S(2)}, u32[]{:S(2)}) collective-permute-start(f32[2,512,256]{2,1,0:T(8,128)} %get-tuple-element.153.refs_3_.last), channel_id=1, source_target_pairs={{0,4},{4,8},{8,12},{12,16},{16,20},{20,24},{24,28},{28,0},{1,5},{5... | collective-permute-start | bytes 3145736 | tf_op jit(solution)/shard_map/ppermute | solution.py:687
  7.0 3.1 %collective-permute-start.7 = (f32[2,512,256]{2,1,0:T(8,128)}, f32[2,512,256]{2,1,0:T(8,128)}, u32[]{:S(2)}, u32[]{:S(2)}) collective-permute-start(f32[2,512,256]{2,1,0:T(8,128)} %get-tuple-element.154.refs_0_.first), channel_id=1, source_target_pairs={{4,0},{8,4},{12,8},{16,12},{20,16},{24,20},{28,24},{0,28},{5,1},{9... | collective-permute-start | bytes 3145736 | tf_op jit(solution)/shard_map/ppermute | solution.py:690
  10.1 0.5 slice.22
  11.4 17.2 %conditional.2 = (f32[2,512,256]{2,1,0:T(8,128)}, f32[2,512,256]{2,1,0:T(8,128)S(1)}, bf16[128,512]{1,0:T(8,128)(2,1)}, f32[40,8,256]{2,1,0:T(8,128)}, f32[12,8,...) conditional(s32[]{:T(128)} %bitcast, () %tuple.27, (s32[40,512]{1,0:T(8,128)S(1)}, ...), branch_computations={%region_0.0_spmd, %region_1.0_spmd} | conditional | flops 117688 | bytes 6360252 | solution.py:661
  11.5 4.6 %first_sums.1 = (f32[2,512,256]{2,1,0:T(8,128)}, f32[2,512,256]{2,1,0:T(8,128)S(1)}, f32[28,8,256]{2,1,0:T(8,128)S(1)}, f32[28,8,256]{2,1,0:T(8,128)S(1)}) custom-call(f32[512,8,256]{2,1,0:T(8,128)} %get-tuple-element.66.source, bf16[128,512]{1,0:T(8,128)(2,1)S(1)} %sum_weights.1.weight, s32[1]{0:T(128)} %get-tuple-element.71.side.refs_5_), custom_call_target="tpu_custom_call" | custom-call | flops 1000 | bytes 1000 | tf_op jit(solution)/shard_map/cond/branch_1_fun/first_sums/pallas_call | solution.py:197
  16.2 1.5 %collective-permute-done = f32[28,8,256]{2,1,0:T(8,128)S(1)} collective-permute-done((f32[28,8,256]{2,1,0:T(8,128)S(1)}, f32[28,8,256]{2,1,0:T(8,128)S(1)}, u32[]{:S(2)}, u32[]{:S(2)}) %collective-permute-start) | collective-permute-done | bytes 229408 | tf_op jit(solution)/shard_map/cond/branch_1_fun/ppermute | solution.py:647
  17.7 1.7 %collective-permute-start.1 = (f32[28,8,256]{2,1,0:T(8,128)S(1)}, f32[28,8,256]{2,1,0:T(8,128)S(1)}, u32[]{:S(2)}, u32[]{:S(2)}) collective-permute-start(f32[28,8,256]{2,1,0:T(8,128)S(1)} %add.8), channel_id=1, source_target_pairs={{0,2},{1,3},{2,0},{3,1},{4,6},{5,7},{6,4},{7,5},{8,10},{9,11},{10,... | collective-permute-start | bytes 688136 | tf_op jit(solution)/shard_map/cond/branch_1_fun/ppermute | solution.py:647
  19.4 6.0 %collective-permute-done.1 = f32[28,8,256]{2,1,0:T(8,128)S(1)} collective-permute-done((f32[28,8,256]{2,1,0:T(8,128)S(1)}, f32[28,8,256]{2,1,0:T(8,128)S(1)}, u32[]{:S(2)}, u32[]{:S(2)}) %collective-permute-start.1) | collective-permute-done | bytes 229408 | tf_op jit(solution)/shard_map/cond/branch_1_fun/ppermute | solution.py:647
  25.5 0.1 collective-permute-start.2
  25.5 1.5 %collective-permute-done.2.refs_1_ = f32[28,8,256]{2,1,0:T(8,128)S(1)} collective-permute-done((f32[28,8,256]{2,1,0:T(8,128)S(1)}, f32[28,8,256]{2,1,0:T(8,128)S(1)}, u32[]{:S(2)}, u32[]{:S(2)}) %collective-permute-start.2) | collective-permute-done | bytes 229408 | tf_op jit(solution)/shard_map/cond/branch_1_fun/ppermute | solution.py:647
  27.0 1.6 %cell_update.2 = (f32[40,8,256]{2,1,0:T(8,128)}, f32[12,8,256]{2,1,0:T(8,128)}, f32[14,8,256]{2,1,0:T(8,128)}, f32[8,16,256]{2,1,0:T(8,128)S(1)}) custom-call(f32[28,8,256]{2,1,0:T(8,128)S(1)} %add.9.refs_0_, f32[28,8,256]{2,1,0:T(8,128)S(1)} %collective-permute-done.2.refs_1_, f32[40,8,256]{2,1,0:T(8,128)S(1)} %copy-done.16, f32[12,8,256]{2,1,0:T(8,128)S(1)} %copy-done.20, ...), custom_call_target="tpu_custom_call" | custom-call | flops 1000 | bytes 1000 | tf_op jit(solution)/shard_map/cond/branch_1_fun/cell_update/pallas_call | solution.py:259
  28.6 0.7 fusion.2
  29.3 2.0 %collective-permute-start.9 = (f32[2,16,256]{2,1,0:T(8,128)}, f32[2,16,256]{2,1,0:T(8,128)}, u32[]{:S(2)}, u32[]{:S(2)}) collective-permute-start(f32[2,16,256]{2,1,0:T(8,128)} %get-tuple-element.198), channel_id=1, source_target_pairs={{4,0},{8,4},{12,8},{16,12},{20,16},{24,20},{28,24},{0,28},{5,1},{9... | collective-permute-start | bytes 98312 | tf_op jit(solution)/shard_map/ppermute | solution.py:690
  31.3 0.1 copy.24.offs
  31.4 1.7 %spread_operands.1 = (bf16[512,96]{1,0:T(8,128)(2,1)S(1)}, f32[512,128]{1,0:T(8,128)S(1)}, bf16[1280,256]{1,0:T(8,128)(2,1)S(1)}) custom-call(s32[40,512]{1,0:T(8,128)} %bitcast.10, s32[14,512]{1,0:T(8,128)} %bitcast.12, f32[1,512]{1,0:T(1,128)S(1)} %bitcast.15, f32[1,512]{1,0:T(1,128)} %bitcast.16, f32[1,512]{1,0:T(1,128)S(1)} %bitcast.8, ...), custom_call_target="tpu_custom_call" | custom-call | flops 1000 | bytes 1000 | tf_op jit(solution)/shard_map/spread_operands/pallas_call | solution.py:159
  33.2 13.0 %day_one_inside.1 = (f32[8,512,256]{2,1,0:T(8,128)S(1)}, f32[2,512,256]{2,1,0:T(8,128)S(1)}, f32[2,512,256]{2,1,0:T(8,128)}, f32[4,64,256]{2,1,0:T(8,128)S(1)}) custom-call(f32[2,512,256]{2,1,0:T(8,128)S(1)} %copy-done, f32[2,512,256]{2,1,0:T(8,128)} %get-tuple-element.156.refs_1_, f32[2,512,256]{2,1,0:T(8,128)S(1)} %get-tuple-element.157.refs_2_, ...), custom_call_target="tpu_custom_call" | custom-call | flops 1000 | bytes 1000 | tf_op jit(solution)/shard_map/day_one_inside/pallas_call | solution.py:347
  46.3 1.0 fusion
  47.3 8.6 %collective-permute-done.9.after = f32[2,16,256]{2,1,0:T(8,128)} collective-permute-done((f32[2,16,256]{2,1,0:T(8,128)}, f32[2,16,256]{2,1,0:T(8,128)}, u32[]{:S(2)}, u32[]{:S(2)}) %collective-permute-start.9) | collective-permute-done | bytes 32800 | tf_op jit(solution)/shard_map/ppermute | solution.py:690
  55.9 3.3 %collective-permute-start.12 = (f32[2,512,256]{2,1,0:T(8,128)}, f32[2,512,256]{2,1,0:T(8,128)S(1)}, u32[]{:S(2)}, u32[]{:S(2)}) collective-permute-start(f32[2,512,256]{2,1,0:T(8,128)} %get-tuple-element.179), channel_id=1, source_target_pairs={{4,0},{8,4},{12,8},{16,12},{20,16},{24,20},{28,24},{0,28},{5,1},{9... | collective-permute-start | bytes 3145736 | tf_op jit(solution)/shard_map/ppermute | solution.py:690
  59.3 17.9 %conditional.3 = (f32[4,512,256]{2,1,0:T(8,128)}, f32[40,8,256]{2,1,0:T(8,128)}, f32[12,8,256]{2,1,0:T(8,128)}, f32[14,8,256]{2,1,0:T(8,128)}, f32[8,16,256]{2,1,0:T(8,128)}) conditional(s32[]{:T(128)} %bitcast, () %tuple.30, (f32[2,512,256]{2,1,0:T(8,128)}, f32[2,512,256]{2,1,0:T(8,128)}, f32[8,512,256]{2,1,0:T(8,128)S(1)}, ...), branch_computations={%region_2.0_spmd, %region_3.0_spmd} | conditional | flops 116688 | bytes 4130928 | solution.py:661
  59.3 5.4 %day_one_rim.1 = (f32[4,512,256]{2,1,0:T(8,128)}, f32[28,8,256]{2,1,0:T(8,128)S(1)}, f32[28,8,256]{2,1,0:T(8,128)S(1)}) custom-call(f32[2,512,256]{2,1,0:T(8,128)} %get-tuple-element.88.low, f32[2,512,256]{2,1,0:T(8,128)} %get-tuple-element.89.high, f32[8,512,256]{2,1,0:T(8,128)S(1)} %get-tuple-element.90.first.last, ...), custom_call_target="tpu_custom_call" | custom-call | flops 1000 | bytes 1000 | tf_op jit(solution)/shard_map/cond/branch_1_fun/day_one_rim/pallas_call | solution.py:407
  64.7 1.5 %collective-permute-done.3 = f32[28,8,256]{2,1,0:T(8,128)S(1)} collective-permute-done((f32[28,8,256]{2,1,0:T(8,128)S(1)}, f32[28,8,256]{2,1,0:T(8,128)S(1)}, u32[]{:S(2)}, u32[]{:S(2)}) %collective-permute-start.3) | collective-permute-done | bytes 229408 | tf_op jit(solution)/shard_map/cond/branch_1_fun/ppermute | solution.py:647
  66.3 1.6 %collective-permute-start.4 = (f32[28,8,256]{2,1,0:T(8,128)S(1)}, f32[28,8,256]{2,1,0:T(8,128)S(1)}, u32[]{:S(2)}, u32[]{:S(2)}) collective-permute-start(f32[28,8,256]{2,1,0:T(8,128)S(1)} %add.10), channel_id=1, source_target_pairs={{0,2},{1,3},{2,0},{3,1},{4,6},{5,7},{6,4},{7,5},{8,10},{9,11},{10,... | collective-permute-start | bytes 688136 | tf_op jit(solution)/shard_map/cond/branch_1_fun/ppermute | solution.py:647
  67.8 6.1 %collective-permute-done.4 = f32[28,8,256]{2,1,0:T(8,128)S(1)} collective-permute-done((f32[28,8,256]{2,1,0:T(8,128)S(1)}, f32[28,8,256]{2,1,0:T(8,128)S(1)}, u32[]{:S(2)}, u32[]{:S(2)}) %collective-permute-start.4) | collective-permute-done | bytes 229408 | tf_op jit(solution)/shard_map/cond/branch_1_fun/ppermute | solution.py:647
  74.1 1.5 %collective-permute-done.5.refs_1_ = f32[28,8,256]{2,1,0:T(8,128)S(1)} collective-permute-done((f32[28,8,256]{2,1,0:T(8,128)S(1)}, f32[28,8,256]{2,1,0:T(8,128)S(1)}, u32[]{:S(2)}, u32[]{:S(2)}) %collective-permute-start.5) | collective-permute-done | bytes 229408 | tf_op jit(solution)/shard_map/cond/branch_1_fun/ppermute | solution.py:647
  75.5 1.7 %cell_update.3 = (f32[40,8,256]{2,1,0:T(8,128)}, f32[12,8,256]{2,1,0:T(8,128)}, f32[14,8,256]{2,1,0:T(8,128)}, f32[8,16,256]{2,1,0:T(8,128)}) custom-call(f32[28,8,256]{2,1,0:T(8,128)S(1)} %add.11.refs_0_, f32[28,8,256]{2,1,0:T(8,128)S(1)} %collective-permute-done.5.refs_1_, f32[40,8,256]{2,1,0:T(8,128)S(1)} %get-tuple-element.102.refs_2_, ...), custom_call_target="tpu_custom_call" | custom-call | flops 1000 | bytes 1000 | tf_op jit(solution)/shard_map/cond/branch_1_fun/cell_update/pallas_call | solution.py:259
  77.2 4.7 %day_one_beyond.1.near_low.near_high = f32[4,512,256]{2,1,0:T(8,128)S(1)} custom-call(f32[2,512,256]{2,1,0:T(8,128)} %collective-permute-done.6.low, f32[2,512,256]{2,1,0:T(8,128)} %collective-permute-done.7.high, f32[2,512,256]{2,1,0:T(8,128)S(1)} %copy-done, f32[2,512,256]{2,1,0:T(8,128)S(1)} %copy-done.1, f32[8,16,256]{2,1,0:T(8,128)} %copy-done.11, ...), custom_call_target="tpu_custom_call" | custom-call | flops 1000 | bytes 1000 | tf_op jit(solution)/shard_map/day_one_beyond/pallas_call | solution.py:456
  82.0 4.8 %collective-permute-start.14 = (f32[2,16,256]{2,1,0:T(8,128)S(1)}, f32[2,16,256]{2,1,0:T(8,128)S(1)}, u32[]{:S(2)}, u32[]{:S(2)}) collective-permute-start(f32[2,16,256]{2,1,0:T(8,128)S(1)} %get-tuple-element.196), channel_id=1, source_target_pairs={{4,0},{8,4},{12,8},{16,12},{20,16},{24,20},{28,24},{0,28},{5,1},{9... | collective-permute-start | bytes 98312 | tf_op jit(solution)/shard_map/ppermute | solution.py:690
  86.8 7.2 %day_two.1 = (f32[512,8,256]{2,1,0:T(8,128)}, f32[4,512,256]{2,1,0:T(8,128)S(1)}) custom-call(f32[8,512,256]{2,1,0:T(8,128)S(1)} %copy-done.5, f32[8,512,256]{2,1,0:T(8,128)S(1)} %copy-done.5, f32[4,512,256]{2,1,0:T(8,128)S(1)} %copy-done.8, f32[8,16,256]{2,1,0:T(8,128)S(1)} %copy-done.13, bf16[512,96]{1,0:T(8,128)(2,1)S(1)} %get-tuple-element.158.refs_5_.gain_w.refs_4_, ...), custom_call_target="tpu_custom_call" | custom-call | flops 1000 | bytes 1000 | tf_op jit(solution)/shard_map/day_two/pallas_call | solution.py:525
  94.0 9.7 %collective-permute-done.14.after = f32[2,16,256]{2,1,0:T(8,128)S(1)} collective-permute-done((f32[2,16,256]{2,1,0:T(8,128)S(1)}, f32[2,16,256]{2,1,0:T(8,128)S(1)}, u32[]{:S(2)}, u32[]{:S(2)}) %collective-permute-start.14) | collective-permute-done | bytes 32800 | tf_op jit(solution)/shard_map/ppermute | solution.py:690
  103.7 3.8 %edges.1 = f32[512,8,256]{2,1,0:T(8,128)} custom-call(f32[2,256,256]{2,1,0:T(8,128)} %collective-permute-done.10.early, f32[2,256,256]{2,1,0:T(8,128)S(1)} %collective-permute-done.11.late, f32[2,512,256]{2,1,0:T(8,128)S(1)} %collective-permute-done.12.high, f32[4,512,256]{2,1,0:T(8,128)S(1)} %day_one_beyond.1.near_low.near_high, ...), custom_call_target="tpu_custom_call", output_to_operand_aliasing={{}: (11, {})} | custom-call | flops 1000 | bytes 1000 | tf_op jit(solution)/shard_map/edges/pallas_call | solution.py:599
  (88 shorter events, 0.6 us)
Async XLA Ops:
  4.0 51.8 %collective-permute-start.6 = (f32[2,512,256]{2,1,0:T(8,128)}, f32[2,512,256]{2,1,0:T(8,128)}, u32[]{:S(2)}, u32[]{:S(2)}) collective-permute-start(f32[2,512,256]{2,1,0:T(8,128)} %get-tuple-element.153.refs_3_.last), channel_id=1, source_target_pairs={{0,4},{4,8},{8,12},{12,16},{16,20},{20,24},{24,28},{28,0},{1,5},{5... | collective-permute-start | bytes 3145736 | tf_op jit(solution)/shard_map/ppermute | solution.py:687
  7.0 48.8 %collective-permute-start.7 = (f32[2,512,256]{2,1,0:T(8,128)}, f32[2,512,256]{2,1,0:T(8,128)}, u32[]{:S(2)}, u32[]{:S(2)}) collective-permute-start(f32[2,512,256]{2,1,0:T(8,128)} %get-tuple-element.154.refs_0_.first), channel_id=1, source_target_pairs={{4,0},{8,4},{12,8},{16,12},{20,16},{24,20},{28,24},{0,28},{5,1},{9... | collective-permute-start | bytes 3145736 | tf_op jit(solution)/shard_map/ppermute | solution.py:690
  11.4 20.0 %copy-start.2 = (f32[512]{0:T(512)S(1)}, f32[512]{0:T(512)}, u32[]{:S(2)}) copy-start(f32[512]{0:T(512)} %param.29) | copy-start | bytes 6148
  11.4 20.0 %copy-start.3 = (f32[512]{0:T(512)S(1)}, f32[512]{0:T(512)}, u32[]{:S(2)}) copy-start(f32[512]{0:T(512)} %param.30) | copy-start | bytes 6148
  11.4 21.7 %copy-start = (f32[2,512,256]{2,1,0:T(8,128)S(1)}, f32[2,512,256]{2,1,0:T(8,128)}, u32[]{:S(2)}) copy-start(f32[2,512,256]{2,1,0:T(8,128)} %get-tuple-element.154.refs_0_.first) | copy-start | bytes 3145732
  11.4 21.7 %copy-start.1 = (f32[2,512,256]{2,1,0:T(8,128)S(1)}, f32[2,512,256]{2,1,0:T(8,128)}, u32[]{:S(2)}) copy-start(f32[2,512,256]{2,1,0:T(8,128)} %get-tuple-element.153.refs_3_.last) | copy-start | bytes 3145732
  11.5 15.5 %copy-start.16 = (f32[40,8,256]{2,1,0:T(8,128)S(1)}, f32[40,8,256]{2,1,0:T(8,128)}, u32[]{:S(2)}) copy-start(f32[40,8,256]{2,1,0:T(8,128)} %get-tuple-element.191.refs_2_) | copy-start | bytes 983044 | tf_op jit(solution)/shard_map/cond
  11.5 15.5 %copy-start.20 = (f32[12,8,256]{2,1,0:T(8,128)S(1)}, f32[12,8,256]{2,1,0:T(8,128)}, u32[]{:S(2)}) copy-start(f32[12,8,256]{2,1,0:T(8,128)} %get-tuple-element.192.refs_3_) | copy-start | bytes 294916 | tf_op jit(solution)/shard_map/cond
  16.2 1.5 %collective-permute-start = (f32[28,8,256]{2,1,0:T(8,128)S(1)}, f32[28,8,256]{2,1,0:T(8,128)S(1)}, u32[]{:S(2)}, u32[]{:S(2)}) collective-permute-start(f32[28,8,256]{2,1,0:T(8,128)S(1)} %get-tuple-element.75), channel_id=1, source_target_pairs={{0,1},{1,0},{2,3},{3,2},{4,5},{5,4},{6,7},{7,6},{8,9},{9,8},{10,11... | collective-permute-start | bytes 688136 | tf_op jit(solution)/shard_map/cond/branch_1_fun/ppermute | solution.py:647
  17.7 7.7 %collective-permute-start.1 = (f32[28,8,256]{2,1,0:T(8,128)S(1)}, f32[28,8,256]{2,1,0:T(8,128)S(1)}, u32[]{:S(2)}, u32[]{:S(2)}) collective-permute-start(f32[28,8,256]{2,1,0:T(8,128)S(1)} %add.8), channel_id=1, source_target_pairs={{0,2},{1,3},{2,0},{3,1},{4,6},{5,7},{6,4},{7,5},{8,10},{9,11},{10,... | collective-permute-start | bytes 688136 | tf_op jit(solution)/shard_map/cond/branch_1_fun/ppermute | solution.py:647
  25.5 1.6 %collective-permute-start.2 = (f32[28,8,256]{2,1,0:T(8,128)S(1)}, f32[28,8,256]{2,1,0:T(8,128)S(1)}, u32[]{:S(2)}, u32[]{:S(2)}) collective-permute-start(f32[28,8,256]{2,1,0:T(8,128)S(1)} %add.9.refs_0_), channel_id=1, source_target_pairs={{0,1},{1,0},{2,3},{3,2},{4,5},{5,4},{6,7},{7,6},{8,9},{9,8},{10,11... | collective-permute-start | bytes 688136 | tf_op jit(solution)/shard_map/cond/branch_1_fun/ppermute | solution.py:647
  29.3 26.5 %collective-permute-start.9 = (f32[2,16,256]{2,1,0:T(8,128)}, f32[2,16,256]{2,1,0:T(8,128)}, u32[]{:S(2)}, u32[]{:S(2)}) collective-permute-start(f32[2,16,256]{2,1,0:T(8,128)} %get-tuple-element.198), channel_id=1, source_target_pairs={{4,0},{8,4},{12,8},{16,12},{20,16},{24,20},{28,24},{0,28},{5,1},{9... | collective-permute-start | bytes 98312 | tf_op jit(solution)/shard_map/ppermute | solution.py:690
  31.3 24.6 %collective-permute-start.8 = (f32[2,16,256]{2,1,0:T(8,128)}, f32[2,16,256]{2,1,0:T(8,128)}, u32[]{:S(2)}, u32[]{:S(2)}) collective-permute-start(f32[2,16,256]{2,1,0:T(8,128)} %get-tuple-element.199), channel_id=1, source_target_pairs={{0,4},{4,8},{8,12},{12,16},{16,20},{20,24},{24,28},{28,0},{1,5},{5... | collective-permute-start | bytes 98312 | tf_op jit(solution)/shard_map/ppermute | solution.py:687
  33.1 26.1 %copy-start.6 = (bf16[1280,256]{1,0:T(8,128)(2,1)}, bf16[1280,256]{1,0:T(8,128)(2,1)S(1)}, u32[]{:S(2)}) copy-start(bf16[1280,256]{1,0:T(8,128)(2,1)S(1)} %get-tuple-element.160.refs_7_.circ.refs_6_) | copy-start | bytes 1966084
  46.2 13.1 %copy-start.4 = (f32[8,512,256]{2,1,0:T(8,128)}, f32[8,512,256]{2,1,0:T(8,128)S(1)}, u32[]{:S(2)}) copy-start(f32[8,512,256]{2,1,0:T(8,128)S(1)} %get-tuple-element.168.refs_0_.refs_1_) | copy-start | bytes 12582916
  46.2 13.0 %copy-start.10 = (bf16[128,512]{1,0:T(8,128)(2,1)S(1)}, bf16[128,512]{1,0:T(8,128)(2,1)}, u32[]{:S(2)}) copy-start(bf16[128,512]{1,0:T(8,128)(2,1)} %get-tuple-element.161.refs_8_) | copy-start | bytes 393220
  46.2 13.0 %copy-start.12 = (f32[40,8,256]{2,1,0:T(8,128)S(1)}, f32[40,8,256]{2,1,0:T(8,128)}, u32[]{:S(2)}) copy-start(f32[40,8,256]{2,1,0:T(8,128)} %get-tuple-element.172) | copy-start | bytes 983044
  46.2 13.0 %copy-start.14 = (f32[14,8,256]{2,1,0:T(8,128)S(1)}, f32[14,8,256]{2,1,0:T(8,128)}, u32[]{:S(2)}) copy-start(f32[14,8,256]{2,1,0:T(8,128)} %get-tuple-element.174) | copy-start | bytes 344068
  46.2 13.0 %copy-start.15 = (f32[12,8,256]{2,1,0:T(8,128)S(1)}, f32[12,8,256]{2,1,0:T(8,128)}, u32[]{:S(2)}) copy-start(f32[12,8,256]{2,1,0:T(8,128)} %get-tuple-element.173) | copy-start | bytes 294916
  46.2 13.0 %copy-start.24 = (f32[40]{0:T(128)S(1)}, f32[40]{0:T(128)}, u32[]{:S(2)}) copy-start(f32[40]{0:T(128)} %param.31) | copy-start | bytes 484
  46.2 13.0 %copy-start.26 = (f32[40]{0:T(128)S(1)}, f32[40]{0:T(128)}, u32[]{:S(2)}) copy-start(f32[40]{0:T(128)} %param.32) | copy-start | bytes 484
  46.2 13.0 %copy-start.28 = (f32[40]{0:T(128)S(1)}, f32[40]{0:T(128)}, u32[]{:S(2)}) copy-start(f32[40]{0:T(128)} %param.33) | copy-start | bytes 484
  46.2 13.0 %copy-start.30 = (f32[14]{0:T(128)S(1)}, f32[14]{0:T(128)}, u32[]{:S(2)}) copy-start(f32[14]{0:T(128)} %param.34) | copy-start | bytes 172
  46.2 13.0 %copy-start.32 = (s32[40]{0:T(128)S(1)}, s32[40]{0:T(128)}, u32[]{:S(2)}) copy-start(s32[40]{0:T(128)} %param.26) | copy-start | bytes 484
  55.9 47.9 %collective-permute-start.12 = (f32[2,512,256]{2,1,0:T(8,128)}, f32[2,512,256]{2,1,0:T(8,128)S(1)}, u32[]{:S(2)}, u32[]{:S(2)}) collective-permute-start(f32[2,512,256]{2,1,0:T(8,128)} %get-tuple-element.179), channel_id=1, source_target_pairs={{4,0},{8,4},{12,8},{16,12},{20,16},{24,20},{28,24},{0,28},{5,1},{9... | collective-permute-start | bytes 3145736 | tf_op jit(solution)/shard_map/ppermute | solution.py:690
  59.2 44.5 %collective-permute-start.10 = (f32[2,256,256]{2,1,0:T(8,128)}, f32[2,256,256]{2,1,0:T(8,128)}, u32[]{:S(2)}, u32[]{:S(2)}) collective-permute-start(f32[2,256,256]{2,1,0:T(8,128)} %get-tuple-element.165), channel_id=1, source_target_pairs={{0,4},{4,8},{8,12},{12,16},{16,20},{20,24},{24,28},{28,0},{1,5},{5... | collective-permute-start | bytes 1572872 | tf_op jit(solution)/shard_map/ppermute | solution.py:687
  64.7 1.5 %collective-permute-start.3 = (f32[28,8,256]{2,1,0:T(8,128)S(1)}, f32[28,8,256]{2,1,0:T(8,128)S(1)}, u32[]{:S(2)}, u32[]{:S(2)}) collective-permute-start(f32[28,8,256]{2,1,0:T(8,128)S(1)} %get-tuple-element.101), channel_id=1, source_target_pairs={{0,1},{1,0},{2,3},{3,2},{4,5},{5,4},{6,7},{7,6},{8,9},{9,8},{10,11... | collective-permute-start | bytes 688136 | tf_op jit(solution)/shard_map/cond/branch_1_fun/ppermute | solution.py:647
  66.3 7.7 %collective-permute-start.4 = (f32[28,8,256]{2,1,0:T(8,128)S(1)}, f32[28,8,256]{2,1,0:T(8,128)S(1)}, u32[]{:S(2)}, u32[]{:S(2)}) collective-permute-start(f32[28,8,256]{2,1,0:T(8,128)S(1)} %add.10), channel_id=1, source_target_pairs={{0,2},{1,3},{2,0},{3,1},{4,6},{5,7},{6,4},{7,5},{8,10},{9,11},{10,... | collective-permute-start | bytes 688136 | tf_op jit(solution)/shard_map/cond/branch_1_fun/ppermute | solution.py:647
  74.0 1.6 %collective-permute-start.5 = (f32[28,8,256]{2,1,0:T(8,128)S(1)}, f32[28,8,256]{2,1,0:T(8,128)S(1)}, u32[]{:S(2)}, u32[]{:S(2)}) collective-permute-start(f32[28,8,256]{2,1,0:T(8,128)S(1)} %add.11.refs_0_), channel_id=1, source_target_pairs={{0,1},{1,0},{2,3},{3,2},{4,5},{5,4},{6,7},{7,6},{8,9},{9,8},{10,11... | collective-permute-start | bytes 688136 | tf_op jit(solution)/shard_map/cond/branch_1_fun/ppermute | solution.py:647
  81.9 21.8 %collective-permute-start.11 = (f32[2,256,256]{2,1,0:T(8,128)}, f32[2,256,256]{2,1,0:T(8,128)S(1)}, u32[]{:S(2)}, u32[]{:S(2)}) collective-permute-start(f32[2,256,256]{2,1,0:T(8,128)} %get-tuple-element.178), channel_id=1, source_target_pairs={{0,4},{4,8},{8,12},{12,16},{16,20},{20,24},{24,28},{28,0},{1,5},{5... | collective-permute-start | bytes 1572872 | tf_op jit(solution)/shard_map/ppermute | solution.py:687
  82.0 21.7 %collective-permute-start.14 = (f32[2,16,256]{2,1,0:T(8,128)S(1)}, f32[2,16,256]{2,1,0:T(8,128)S(1)}, u32[]{:S(2)}, u32[]{:S(2)}) collective-permute-start(f32[2,16,256]{2,1,0:T(8,128)S(1)} %get-tuple-element.196), channel_id=1, source_target_pairs={{4,0},{8,4},{12,8},{16,12},{20,16},{24,20},{28,24},{0,28},{5,1},{9... | collective-permute-start | bytes 98312 | tf_op jit(solution)/shard_map/ppermute | solution.py:690
  86.8 16.9 %collective-permute-start.13 = (f32[2,16,256]{2,1,0:T(8,128)S(1)}, f32[2,16,256]{2,1,0:T(8,128)S(1)}, u32[]{:S(2)}, u32[]{:S(2)}) collective-permute-start(f32[2,16,256]{2,1,0:T(8,128)S(1)} %get-tuple-element.197), channel_id=1, source_target_pairs={{0,4},{4,8},{8,12},{12,16},{16,20},{20,24},{24,28},{28,0},{1,5},{5... | collective-permute-start | bytes 98312 | tf_op jit(solution)/shard_map/ppermute | solution.py:687
  (17 other events, 157.0 us)

commit v4 on v3

--- a/solution.py
+++ b/solution.py
@@ -44,25 +44,23 @@
     return jnp.dot(a, b, preferred_element_type=F32)
 
 
-def take_first(biomass, rows, pieces):
+def take_first(biomass, pieces):
     count, height, width = biomass.shape
-    pairs = len(rows) // 2
-    step = count // pieces
-
-    def kernel(source, *refs):
-        outs, held, arrived, left = refs[:pairs], refs[pairs], refs[pairs + 1], refs[pairs + 2]
+    half, step = count // 2, count // pieces
+
+    def kernel(source, first, early, late, held, arrived, left):
         loads, stores = [], []
         for p in range(pieces):
             taxa = pl.ds(p * step, step)
             loads.append(pltpu.make_async_copy(source.at[taxa], held.at[taxa], arrived.at[p]))
             loads[-1].start()
         for p in range(pieces):
-            taxa = pl.ds(p * step, step)
             loads[p].wait()
-            for i, row in enumerate(rows):
-                stores.append(
-                    pltpu.make_async_copy(held.at[taxa, row, :], outs[i // 2].at[i % 2, taxa], left.at[p, i])
-                )
+            at = p * step
+            last = early if at < half else late
+            for i, row in enumerate((0, 1, height - 2, height - 1)):
+                target = first.at[i, pl.ds(at, step)] if i < 2 else last.at[i - 2, pl.ds(at % half, step)]
+                stores.append(pltpu.make_async_copy(held.at[pl.ds(at, step), row, :], target, left.at[p, i]))
                 stores[-1].start()
         for copy in stores:
             copy.wait()
@@ -70,13 +68,13 @@
     return pl.pallas_call(
         kernel,
         name="take_first",
-        out_shape=[jax.ShapeDtypeStruct((2, count, width), F32)] * pairs,
+        out_shape=[jax.ShapeDtypeStruct((2, n, width), F32) for n in (count, half, half)],
         in_specs=[ANY],
-        out_specs=[ANY] * pairs,
+        out_specs=[ANY] * 3,
         scratch_shapes=[
             pltpu.VMEM((count, height, width), F32),
             pltpu.SemaphoreType.DMA((pieces,)),
-            pltpu.SemaphoreType.DMA((pieces, len(rows))),
+            pltpu.SemaphoreType.DMA((pieces, 4)),
         ],
         compiler_params=pltpu.CompilerParams(vmem_limit_bytes=60 << 20),
         cost_estimate=cost(1000, 1000),
@@ -174,7 +172,7 @@
 
 def first_sums(biomass, weights, odd, block):
     count, rows, width = biomass.shape
-    inner = rows // 2 - 2
+    inner = rows // 2 - 1
 
     def kernel(source, weight, side, *refs):
         pairs, (mine, other, total) = refs[:inner], refs[inner:]
@@ -185,7 +183,7 @@
 
         x = jnp.swapaxes(source[...], 0, 1)
         for row in range(rows):
-            if 2 <= row < rows - 2:
+            if row >= 2:
                 pairs[row // 2 - 1][row % 2] = x[row]
             add_sums(total, row, x[row], weight[...])
 
@@ -376,12 +374,16 @@
 TERMS = ((0, 2, 0), (1, 1, 0), (2, 1, 4), (2, 2, 3))
 
 
-def day_one_rim(low, high, inside, sums, share_low, share_high, gain, fraction, circulant, weights, odd, block):
-    _, count, width = low.shape
+def chosen(early, late):
+    return jnp.where(pl.program_id(0) == 0, early, late)
+
+
+def day_one_rim(early_low, late_low, high, inside, sums, share_low, share_high, gain, fraction, circulant, weights, odd, block):
+    _, count, width = high.shape
     rows = inside.shape[0]
 
     def kernel(
-        low, high, first, last, part, before, after, gain_w, frac, circ, weight, side, out, mine, other, far, total
+        early, late, high, first, last, part, before, after, gain_w, frac, circ, weight, side, out, mine, other, far, total
     ):
         @pl.when(pl.program_id(0) == 0)
         def _():
@@ -390,7 +392,7 @@
                 total[row] = jnp.zeros((PADDED, width), F32)
 
         for i in range(4):
-            x = low[i] if i < 2 else high[i - 2]
+            x = chosen(early[i], late[i]) if i < 2 else high[i - 2]
             s = before[i] if i < 2 else after[i - 2]
             store_pieces(far, i, x * matmul(gain_w[...], share_operand(s)))
         for i in range(4):
@@ -410,7 +412,8 @@
         grid=(count // block,),
         out_shape=[jax.ShapeDtypeStruct((4, count, width), F32)] + [jax.ShapeDtypeStruct(half, F32)] * 2,
         in_specs=[
-            pair_spec(block, width),
+            whole(early_low.shape),
+            whole(late_low.shape),
             pair_spec(block, width),
             pair_spec(block, width),
             pair_spec(block, width, rows // 2 - 1),
@@ -430,18 +433,18 @@
         ],
         compiler_params=params(),
         cost_estimate=cost(1000, 1000),
-    )(low, high, inside, inside, sums, share_low, share_high, gain, fraction, circulant, weights, odd)
-
-
-def day_one_beyond(row_pairs, low, high, share, share_low, share_high, gain, fraction, circulant, block):
-    _, count, width = low.shape
+    )(early_low, late_low, high, inside, inside, sums, share_low, share_high, gain, fraction, circulant, weights, odd)
+
+
+def day_one_beyond(row_pairs, early_low, late_low, high, share, share_low, share_high, gain, fraction, circulant, block):
+    _, count, width = high.shape
     rows = 2 * len(row_pairs)
 
-    def kernel(low, high, first, last, own, before, after, gain_w, frac, circ, out, pieces):
+    def kernel(early, late, high, first, last, own, before, after, gain_w, frac, circ, out, pieces):
         for side in range(2):
             for i in range(4):
                 if side == 0:
-                    x = low[i] if i < 2 else first[i - 2]
+                    x = chosen(early[i], late[i]) if i < 2 else first[i - 2]
                     s = before[i] if i < 2 else own[i - 2]
                 else:
                     x = last[i] if i < 2 else high[i - 2]
@@ -458,7 +461,8 @@
         name="day_one_beyond",
         grid=(count // block,),
         out_shape=jax.ShapeDtypeStruct((4, count, width), F32),
-        in_specs=[pair_spec(block, width)] * 4
+        in_specs=[whole(early_low.shape), whole(late_low.shape)]
+        + [pair_spec(block, width)] * 3
         + [
             whole(share.shape),
             whole(share_low.shape),
@@ -471,7 +475,7 @@
         scratch_shapes=[pltpu.VMEM((2 * block, 4 * width), BF16)],
         compiler_params=params(),
         cost_estimate=cost(1000, 1000),
-    )(low, high, row_pairs[0], row_pairs[-1], share, share_low, share_high, gain, fraction, circulant)
+    )(early_low, late_low, high, row_pairs[0], row_pairs[-1], share, share_low, share_high, gain, fraction, circulant)
 
 
 def day_two(inside, rim, share, gain, fraction, circulant, block):
@@ -578,7 +582,7 @@
 
         for i in range(4):
             if i < 2:
-                value = near_low[i] + jnp.where(step == 0, early[i], late[i])
+                value = near_low[i] + chosen(early[i], late[i])
             else:
                 value = near_high[i - 2] + high[i - 2]
             s = before[i] if i < 2 else after[i - 2]
@@ -690,39 +694,40 @@
         return lax.ppermute(x, "space", backward)
 
     count, rows, width = biomass.shape
-    block = min(count, 256)
-
-    first, last = take_first(biomass, (0, 1, rows - 2, rows - 1), 4)
-    inner_low, inner_high = down(last), up(first)
+    block = early = count // 2
+
+    first, last_early, last_late = take_first(biomass, 4)
+    inner_early, inner_high = down(last_early), up(first)
     odd = lax.rem(lax.axis_index("taxa"), 2).reshape(1).astype(jnp.int32)
     traits = (enz_traits.T, mono_traits.T, prod_rate.reshape(1, count), uptake_rate.reshape(1, count))
     cells = (enz_loss, vmax, kmich, khalf, enz_target)
 
     def sums_and_cells(biomass, enzymes, substrates, monomers):
         weights = sum_weights(*traits)
-        *middle, mine, other = first_sums(biomass, weights, odd, block)
+        *others, mine, other = first_sums(biomass, weights, odd, block)
         sums = over_taxa(mine, other)
-        return *middle, weights, *cell_update(*sums, odd, enzymes, substrates, monomers, *cells)
-
-    *middle, weights, enzymes, substrates, monomers, share_one = as_branch(
+        return *others, weights, *cell_update(*sums, odd, enzymes, substrates, monomers, *cells)
+
+    *others, weights, enzymes, substrates, monomers, share_one = as_branch(
         offsets, sums_and_cells, biomass, enzymes, substrates, monomers
     )
-    row_pairs = [first, *middle, last]
+    row_pairs = [first, *others]
     spreading = spread_operands(
         *traits, mortality.reshape(1, count), disperse.reshape(1, count), offsets, width
     )
+    share_one, last_late = lax.optimization_barrier((share_one, last_late))
     share_low, share_high = down(share_one[rows - 2 :]), up(share_one[:2])
+    inner_late = down(last_late)
     inside, to_next, to_previous, inside_sums = day_one_inside(row_pairs, share_one, *spreading, weights, block)
 
-    early = count // 2
-    inner_low, inner_high, share_low, share_high, inside, next_early, to_previous = lax.optimization_barrier(
-        (inner_low, inner_high, share_low, share_high, inside, to_next[:, :early], to_previous)
+    inner_early, inner_late, inner_high, share_low, share_high, inside, next_early, to_previous = lax.optimization_barrier(
+        (inner_early, inner_late, inner_high, share_low, share_high, inside, to_next[:, :early], to_previous)
     )
     from_low, from_high = down(next_early), up(to_previous)
 
-    def rest_of_day_one(low, high, share_low, share_high, enzymes, substrates, monomers):
+    def rest_of_day_one(low_early, low_late, high, share_low, share_high, enzymes, substrates, monomers):
         rim, *sums = day_one_rim(
-            low, high, inside, inside_sums, share_low, share_high, *spreading, weights, odd, block
+            low_early, low_late, high, inside, inside_sums, share_low, share_high, *spreading, weights, odd, block
         )
         sums = over_taxa(*sums)
         return rim, *cell_update(*sums, odd, enzymes, substrates, monomers, *cells)
@@ -730,7 +735,8 @@
     rim, enzymes, substrates, monomers, share_two = as_branch(
         offsets,
         rest_of_day_one,
-        inner_low,
+        inner_early,
+        inner_late,
         inner_high,
         share_low,
         share_high,
@@ -739,9 +745,9 @@
         monomers,
     )
     near_low, near_high = down(share_two[rows - 2 :]), up(share_two[:2])
-    inner_low, inner_high, share_two = lax.optimization_barrier((inner_low, inner_high, share_two))
+    inner_early, inner_high, share_two = lax.optimization_barrier((inner_early, inner_high, share_two))
     beyond = day_one_beyond(
-        row_pairs, inner_low, inner_high, share_one, share_low, share_high, *spreading, block
+        row_pairs, inner_early, inner_late, inner_high, share_one, share_low, share_high, *spreading, block
     )
     beyond, next_late = lax.optimization_barrier((beyond, to_next[:, early:]))
     late_low = down(next_late)

time: 108 us -> 108 us (level)
  waiting for transfers between devices: 36.4 us -> 32.1 us
  starting transfers between devices: 19.7 us -> 23.8 us
    ppermute x4, starting transfers between devices: 13.1 us -> 20 us  [up(): return lax.ppermute(x, 'space', backward)]
    ppermute x4, waiting for transfers between devices: 18.3 us -> 13.6 us  [up(): return lax.ppermute(x, 'space', backward)]
    ppermute x5 -> x6, starting transfers between devices: 3.12 us -> 0.58 us  [down(): return lax.ppermute(x, 'space', forward)]
  transfers between devices with their start and end apart: 15 -> 16, of which waited for: 8 -> 10; matrix products, arithmetic and copies ran while one was open for 2% -> 2% of each run, Pallas kernels for 37% -> 38%
where the time goes in v4:
time: 108 us
  Pallas kernels  47.3 us (44%)
  waiting for transfers between devices  32.1 us (30%)
  starting transfers between devices  23.8 us (22%)
  local copies, waits for them, and re-layouts  2.48 us (2%)
  between operations  1.91 us (2%)
    ppermute x4, starting transfers between devices, up(): return lax.ppermute(x, 'space', backward)  20 us
    ppermute x6, waiting for transfers between devices, exchange(): return lax.ppermute(x, 'taxa', [(i, i ^ step) for i in range(count)])  18.2 us
    ppermute x4, waiting for transfers between devices, up(): return lax.ppermute(x, 'space', backward)  13.6 us
    pallas_call x1, Pallas kernels, day_one_inside(): pl.pallas_call(kernel, name='day_one_inside', grid=(count // block,), out...  13 us
    pallas_call x1, Pallas kernels, day_two(): pl.pallas_call(kernel, name='day_two', grid=(steps,), out_shape=[jax.Shap...  7.14 us
    pallas_call x1, Pallas kernels, day_one_rim(): pl.pallas_call(kernel, name='day_one_rim', grid=(count // block,), out_sh...  5.66 us
    pallas_call x1, Pallas kernels, day_one_beyond(): pl.pallas_call(kernel, name='day_one_beyond', grid=(count // block,), out...  4.82 us
    pallas_call x1, Pallas kernels, first_sums(): pl.pallas_call(kernel, name='first_sums', grid=(count // block,), out_sha...  4.73 us
  transfers between devices with their start and end apart: 16, of which 10 were waited for; matrix products, arithmetic and copies ran while one was open for 2% of the time, Pallas kernels for 38%

profile of v4, /device:TPU:0, one launch (start us, length us, event | category | flops | bytes accessed | tf_op | source)
XLA Modules:
  0.0 107.8 jit_solution(9419775564593485708)
XLA Ops:
  0.8 3.3 %take_first.1 = (f32[2,512,256]{2,1,0:T(8,128)}, f32[2,256,256]{2,1,0:T(8,128)}, f32[2,256,256]{2,1,0:T(8,128)}) custom-call(f32[512,8,256]{2,1,0:T(8,128)} %source.1), custom_call_target="tpu_custom_call" | custom-call | flops 1000 | bytes 1000 | tf_op jit(solution)/shard_map/take_first/pallas_call | solution.py:68
  4.1 6.0 %collective-permute-start.8 = (f32[2,512,256]{2,1,0:T(8,128)}, f32[2,512,256]{2,1,0:T(8,128)}, u32[]{:S(2)}, u32[]{:S(2)}) collective-permute-start(f32[2,512,256]{2,1,0:T(8,128)} %get-tuple-element.166.refs_0_.first), channel_id=1, source_target_pairs={{4,0},{8,4},{12,8},{16,12},{20,16},{24,20},{28,24},{0,28},{5,1},{9... | collective-permute-start | bytes 3145736 | tf_op jit(solution)/shard_map/ppermute | solution.py:694
  10.2 0.5 slice.22
  11.5 17.9 %conditional.2 = (f32[2,512,256]{2,1,0:T(8,128)}, f32[2,512,256]{2,1,0:T(8,128)}, f32[2,512,256]{2,1,0:T(8,128)S(1)}, bf16[128,512]{1,0:T(8,128)(2,1)}, f32[40,8...) conditional(s32[]{:T(128)} %bitcast, () %tuple.28, ...), branch_computations={%region_0.0_spmd, %region_1.0_spmd} | conditional | flops 117688 | bytes 4525196 | solution.py:665
  11.5 0.7 sum_weights.1.weight
  12.2 4.7 %first_sums.1 = (f32[2,512,256]{2,1,0:T(8,128)}, f32[2,512,256]{2,1,0:T(8,128)}, f32[2,512,256]{2,1,0:T(8,128)S(1)}, f32[28,8,256]{2,1,0:T(8,128)S(1)}, f32[28,8,256]{2,1,0:T(8,128)S(1)}) custom-call(f32[512,8,256]{2,1,0:T(8,128)} %get-tuple-element.68.source, bf16[128,512]{1,0:T(8,128)(2,1)} %sum_weights.1.weight, s32[1]{0:T(128)} %get-tuple-element.73.side.refs_5_), custom_call_target="tpu_custom_call" | custom-call | flops 1000 | bytes 1000 | tf_op jit(solution)/shard_map/cond/branch_1_fun/first_sums/pallas_call | solution.py:195
  16.9 1.5 %collective-permute-done = f32[28,8,256]{2,1,0:T(8,128)S(1)} collective-permute-done((f32[28,8,256]{2,1,0:T(8,128)S(1)}, f32[28,8,256]{2,1,0:T(8,128)S(1)}, u32[]{:S(2)}, u32[]{:S(2)}) %collective-permute-start) | collective-permute-done | bytes 229408 | tf_op jit(solution)/shard_map/cond/branch_1_fun/ppermute | solution.py:651
  18.4 1.6 %collective-permute-start.1 = (f32[28,8,256]{2,1,0:T(8,128)S(1)}, f32[28,8,256]{2,1,0:T(8,128)S(1)}, u32[]{:S(2)}, u32[]{:S(2)}) collective-permute-start(f32[28,8,256]{2,1,0:T(8,128)S(1)} %add.8), channel_id=1, source_target_pairs={{0,2},{1,3},{2,0},{3,1},{4,6},{5,7},{6,4},{7,5},{8,10},{9,11},{10,... | collective-permute-start | bytes 688136 | tf_op jit(solution)/shard_map/cond/branch_1_fun/ppermute | solution.py:651
  20.0 6.1 %collective-permute-done.1 = f32[28,8,256]{2,1,0:T(8,128)S(1)} collective-permute-done((f32[28,8,256]{2,1,0:T(8,128)S(1)}, f32[28,8,256]{2,1,0:T(8,128)S(1)}, u32[]{:S(2)}, u32[]{:S(2)}) %collective-permute-start.1) | collective-permute-done | bytes 229408 | tf_op jit(solution)/shard_map/cond/branch_1_fun/ppermute | solution.py:651
  26.3 1.5 %collective-permute-done.2.refs_1_ = f32[28,8,256]{2,1,0:T(8,128)S(1)} collective-permute-done((f32[28,8,256]{2,1,0:T(8,128)S(1)}, f32[28,8,256]{2,1,0:T(8,128)S(1)}, u32[]{:S(2)}, u32[]{:S(2)}) %collective-permute-start.2) | collective-permute-done | bytes 229408 | tf_op jit(solution)/shard_map/cond/branch_1_fun/ppermute | solution.py:651
  27.7 1.6 %cell_update.2 = (f32[40,8,256]{2,1,0:T(8,128)}, f32[12,8,256]{2,1,0:T(8,128)}, f32[14,8,256]{2,1,0:T(8,128)}, f32[8,16,256]{2,1,0:T(8,128)S(1)}) custom-call(f32[28,8,256]{2,1,0:T(8,128)S(1)} %add.9.refs_0_, f32[28,8,256]{2,1,0:T(8,128)S(1)} %collective-permute-done.2.refs_1_, f32[40,8,256]{2,1,0:T(8,128)S(1)} %get-tuple-element.205.refs_2_, ...), custom_call_target="tpu_custom_call" | custom-call | flops 1000 | bytes 1000 | tf_op jit(solution)/shard_map/cond/branch_1_fun/cell_update/pallas_call | solution.py:257
  29.4 0.7 fusion.2
  30.1 4.7 %collective-permute-start.10 = (f32[2,16,256]{2,1,0:T(8,128)}, f32[2,16,256]{2,1,0:T(8,128)}, u32[]{:S(2)}, u32[]{:S(2)}) collective-permute-start(f32[2,16,256]{2,1,0:T(8,128)} %get-tuple-element.212), channel_id=1, source_target_pairs={{4,0},{8,4},{12,8},{16,12},{20,16},{24,20},{28,24},{0,28},{5,1},{9... | collective-permute-start | bytes 98312 | tf_op jit(solution)/shard_map/ppermute | solution.py:694
  34.9 1.7 %spread_operands.1 = (bf16[512,96]{1,0:T(8,128)(2,1)S(1)}, f32[512,128]{1,0:T(8,128)S(1)}, bf16[1280,256]{1,0:T(8,128)(2,1)S(1)}) custom-call(s32[40,512]{1,0:T(8,128)} %bitcast.10, s32[14,512]{1,0:T(8,128)} %bitcast.12, f32[1,512]{1,0:T(1,128)S(1)} %bitcast.15, f32[1,512]{1,0:T(1,128)} %bitcast.16, f32[1,512]{1,0:T(1,128)S(1)} %bitcast.8, ...), custom_call_target="tpu_custom_call" | custom-call | flops 1000 | bytes 1000 | tf_op jit(solution)/shard_map/spread_operands/pallas_call | solution.py:157
  36.6 13.0 %day_one_inside.1 = (f32[8,512,256]{2,1,0:T(8,128)S(1)}, f32[2,512,256]{2,1,0:T(8,128)S(1)}, f32[2,512,256]{2,1,0:T(8,128)}, f32[4,64,256]{2,1,0:T(8,128)S(1)}) custom-call(f32[2,512,256]{2,1,0:T(8,128)S(1)} %copy-done, f32[2,512,256]{2,1,0:T(8,128)} %get-tuple-element.168.refs_1_, f32[2,512,256]{2,1,0:T(8,128)} %get-tuple-element.169.refs_2_, ...), custom_call_target="tpu_custom_call" | custom-call | flops 1000 | bytes 1000 | tf_op jit(solution)/shard_map/day_one_inside/pallas_call | solution.py:345
  49.7 1.0 fusion
  50.7 3.7 %collective-permute-done.10.after = f32[2,16,256]{2,1,0:T(8,128)} collective-permute-done((f32[2,16,256]{2,1,0:T(8,128)}, f32[2,16,256]{2,1,0:T(8,128)}, u32[]{:S(2)}, u32[]{:S(2)}) %collective-permute-start.10) | collective-permute-done | bytes 32800 | tf_op jit(solution)/shard_map/ppermute | solution.py:694
  54.6 4.9 %collective-permute-start.13 = (f32[2,512,256]{2,1,0:T(8,128)}, f32[2,512,256]{2,1,0:T(8,128)S(1)}, u32[]{:S(2)}, u32[]{:S(2)}) collective-permute-start(f32[2,512,256]{2,1,0:T(8,128)} %get-tuple-element.193), channel_id=1, source_target_pairs={{4,0},{8,4},{12,8},{16,12},{20,16},{24,20},{28,24},{0,28},{5,1},{9... | collective-permute-start | bytes 3145736 | tf_op jit(solution)/shard_map/ppermute | solution.py:694
  59.7 18.2 %conditional.3 = (f32[4,512,256]{2,1,0:T(8,128)}, f32[40,8,256]{2,1,0:T(8,128)}, f32[12,8,256]{2,1,0:T(8,128)}, f32[14,8,256]{2,1,0:T(8,128)}, f32[8,16,256]{2,1,0:T(8,128)}) conditional(s32[]{:T(128)} %bitcast, () %tuple.32, (f32[2,256,256]{2,1,0:T(8,128)}, f32[2,256,256]{2,1,0:T(8,128)}, f32[2,512,256]{2,1,0:T(8,128)}, ...), branch_computations={%region_2.0_spmd, %region_3.0_spmd} | conditional | flops 116688 | bytes 4130928 | solution.py:665
  59.7 5.7 %day_one_rim.1 = (f32[4,512,256]{2,1,0:T(8,128)}, f32[28,8,256]{2,1,0:T(8,128)S(1)}, f32[28,8,256]{2,1,0:T(8,128)S(1)}) custom-call(f32[2,256,256]{2,1,0:T(8,128)} %get-tuple-element.91.early, f32[2,256,256]{2,1,0:T(8,128)} %get-tuple-element.92.late, f32[2,512,256]{2,1,0:T(8,128)} %get-tuple-element.93.high, ...), custom_call_target="tpu_custom_call" | custom-call | flops 1000 | bytes 1000 | tf_op jit(solution)/shard_map/cond/branch_1_fun/day_one_rim/pallas_call | solution.py:409
  65.4 1.5 %collective-permute-done.3 = f32[28,8,256]{2,1,0:T(8,128)S(1)} collective-permute-done((f32[28,8,256]{2,1,0:T(8,128)S(1)}, f32[28,8,256]{2,1,0:T(8,128)S(1)}, u32[]{:S(2)}, u32[]{:S(2)}) %collective-permute-start.3) | collective-permute-done | bytes 229408 | tf_op jit(solution)/shard_map/cond/branch_1_fun/ppermute | solution.py:651
  66.9 1.6 %collective-permute-start.4 = (f32[28,8,256]{2,1,0:T(8,128)S(1)}, f32[28,8,256]{2,1,0:T(8,128)S(1)}, u32[]{:S(2)}, u32[]{:S(2)}) collective-permute-start(f32[28,8,256]{2,1,0:T(8,128)S(1)} %add.10), channel_id=1, source_target_pairs={{0,2},{1,3},{2,0},{3,1},{4,6},{5,7},{6,4},{7,5},{8,10},{9,11},{10,... | collective-permute-start | bytes 688136 | tf_op jit(solution)/shard_map/cond/branch_1_fun/ppermute | solution.py:651
  68.4 6.1 %collective-permute-done.4 = f32[28,8,256]{2,1,0:T(8,128)S(1)} collective-permute-done((f32[28,8,256]{2,1,0:T(8,128)S(1)}, f32[28,8,256]{2,1,0:T(8,128)S(1)}, u32[]{:S(2)}, u32[]{:S(2)}) %collective-permute-start.4) | collective-permute-done | bytes 229408 | tf_op jit(solution)/shard_map/cond/branch_1_fun/ppermute | solution.py:651
  74.7 1.5 %collective-permute-done.5.refs_1_ = f32[28,8,256]{2,1,0:T(8,128)S(1)} collective-permute-done((f32[28,8,256]{2,1,0:T(8,128)S(1)}, f32[28,8,256]{2,1,0:T(8,128)S(1)}, u32[]{:S(2)}, u32[]{:S(2)}) %collective-permute-start.5) | collective-permute-done | bytes 229408 | tf_op jit(solution)/shard_map/cond/branch_1_fun/ppermute | solution.py:651
  76.2 1.7 %cell_update.3 = (f32[40,8,256]{2,1,0:T(8,128)}, f32[12,8,256]{2,1,0:T(8,128)}, f32[14,8,256]{2,1,0:T(8,128)}, f32[8,16,256]{2,1,0:T(8,128)}) custom-call(f32[28,8,256]{2,1,0:T(8,128)S(1)} %add.11.refs_0_, f32[28,8,256]{2,1,0:T(8,128)S(1)} %collective-permute-done.5.refs_1_, f32[40,8,256]{2,1,0:T(8,128)S(1)} %get-tuple-element.106.refs_2_, ...), custom_call_target="tpu_custom_call" | custom-call | flops 1000 | bytes 1000 | tf_op jit(solution)/shard_map/cond/branch_1_fun/cell_update/pallas_call | solution.py:257
  77.9 4.8 %day_one_beyond.1.near_low.near_high = f32[4,512,256]{2,1,0:T(8,128)S(1)} custom-call(f32[2,256,256]{2,1,0:T(8,128)} %copy-done.9, f32[2,256,256]{2,1,0:T(8,128)} %collective-permute-done.7.late, f32[2,512,256]{2,1,0:T(8,128)} %collective-permute-done.8.high, f32[2,512,256]{2,1,0:T(8,128)S(1)} %copy-done, f32[2,512,256]{2,1,0:T(8,128)} %copy-done.5, ...), custom_call_target="tpu_custom_call" | custom-call | flops 1000 | bytes 1000 | tf_op jit(solution)/shard_map/day_one_beyond/pallas_call | solution.py:459
  82.7 0.6 collective-permute-start.12
  83.3 4.3 %collective-permute-start.15 = (f32[2,16,256]{2,1,0:T(8,128)S(1)}, f32[2,16,256]{2,1,0:T(8,128)S(1)}, u32[]{:S(2)}, u32[]{:S(2)}) collective-permute-start(f32[2,16,256]{2,1,0:T(8,128)S(1)} %get-tuple-element.210), channel_id=1, source_target_pairs={{4,0},{8,4},{12,8},{16,12},{20,16},{24,20},{28,24},{0,28},{5,1},{9... | collective-permute-start | bytes 98312 | tf_op jit(solution)/shard_map/ppermute | solution.py:694
  87.6 7.1 %day_two.1 = (f32[512,8,256]{2,1,0:T(8,128)}, f32[4,512,256]{2,1,0:T(8,128)S(1)}) custom-call(f32[8,512,256]{2,1,0:T(8,128)S(1)} %copy-done.4, f32[8,512,256]{2,1,0:T(8,128)S(1)} %copy-done.4, f32[4,512,256]{2,1,0:T(8,128)S(1)} %copy-done.6, f32[8,16,256]{2,1,0:T(8,128)S(1)} %copy-done.12, bf16[512,96]{1,0:T(8,128)(2,1)S(1)} %copy-done.8, ...), custom_call_target="tpu_custom_call" | custom-call | flops 1000 | bytes 1000 | tf_op jit(solution)/shard_map/day_two/pallas_call | solution.py:529
  94.7 9.9 %collective-permute-done.15.after = f32[2,16,256]{2,1,0:T(8,128)S(1)} collective-permute-done((f32[2,16,256]{2,1,0:T(8,128)S(1)}, f32[2,16,256]{2,1,0:T(8,128)S(1)}, u32[]{:S(2)}, u32[]{:S(2)}) %collective-permute-start.15) | collective-permute-done | bytes 32800 | tf_op jit(solution)/shard_map/ppermute | solution.py:694
  104.6 0.2 collective-permute-done.14.before
  104.8 2.9 %edges.1 = f32[512,8,256]{2,1,0:T(8,128)} custom-call(f32[2,256,256]{2,1,0:T(8,128)S(1)} %collective-permute-done.11.early, f32[2,256,256]{2,1,0:T(8,128)S(1)} %collective-permute-done.12.late, f32[2,512,256]{2,1,0:T(8,128)S(1)} %collective-permute-done.13.high, ...), custom_call_target="tpu_custom_call", output_to_operand_aliasing={{}: (11, {})} | custom-call | flops 1000 | bytes 1000 | tf_op jit(solution)/shard_map/edges/pallas_call | solution.py:603
  (90 shorter events, 0.7 us)
Async XLA Ops:
  0.6 10.7 %copy-start.29 = (f32[14]{0:T(128)S(1)}, f32[14]{0:T(128)}, u32[]{:S(2)}) copy-start(f32[14]{0:T(128)} %param.34) | copy-start | bytes 172
  0.7 10.7 %copy-start.27 = (f32[40]{0:T(128)S(1)}, f32[40]{0:T(128)}, u32[]{:S(2)}) copy-start(f32[40]{0:T(128)} %param.33) | copy-start | bytes 484
  0.7 10.7 %copy-start.25 = (f32[40]{0:T(128)S(1)}, f32[40]{0:T(128)}, u32[]{:S(2)}) copy-start(f32[40]{0:T(128)} %param.32) | copy-start | bytes 484
  0.7 10.7 %copy-start.23 = (f32[40]{0:T(128)S(1)}, f32[40]{0:T(128)}, u32[]{:S(2)}) copy-start(f32[40]{0:T(128)} %param.31) | copy-start | bytes 484
  0.7 10.7 %copy-start.31 = (s32[40]{0:T(128)S(1)}, s32[40]{0:T(128)}, u32[]{:S(2)}) copy-start(s32[40]{0:T(128)} %param.26) | copy-start | bytes 484
  0.7 10.7 %copy-start.22 = (f32[512]{0:T(512)S(1)}, f32[512]{0:T(512)}, u32[]{:S(2)}) copy-start(f32[512]{0:T(512)} %param.28) | copy-start | bytes 6148
  0.7 10.7 %copy-start.21 = (f32[512]{0:T(512)S(1)}, f32[512]{0:T(512)}, u32[]{:S(2)}) copy-start(f32[512]{0:T(512)} %param.27) | copy-start | bytes 6148
  0.7 10.7 %copy-start.18 = (s32[512,14]{0,1:T(8,128)S(1)}, s32[512,14]{0,1:T(8,128)}, u32[]{:S(2)}) copy-start(s32[512,14]{0,1:T(8,128)} %param.25) | copy-start | bytes 86020
  0.7 10.7 %copy-start.17 = (s32[512,40]{0,1:T(8,128)S(1)}, s32[512,40]{0,1:T(8,128)}, u32[]{:S(2)}) copy-start(s32[512,40]{0,1:T(8,128)} %param.24) | copy-start | bytes 245764
  0.7 10.7 %copy-start.19 = (f32[14,8,256]{2,1,0:T(8,128)S(1)}, f32[14,8,256]{2,1,0:T(8,128)}, u32[]{:S(2)}) copy-start(f32[14,8,256]{2,1,0:T(8,128)} %param.23) | copy-start | bytes 344068
  4.1 50.5 %collective-permute-start.8 = (f32[2,512,256]{2,1,0:T(8,128)}, f32[2,512,256]{2,1,0:T(8,128)}, u32[]{:S(2)}, u32[]{:S(2)}) collective-permute-start(f32[2,512,256]{2,1,0:T(8,128)} %get-tuple-element.166.refs_0_.first), channel_id=1, source_target_pairs={{4,0},{8,4},{12,8},{16,12},{20,16},{24,20},{28,24},{0,28},{5,1},{9... | collective-permute-start | bytes 3145736 | tf_op jit(solution)/shard_map/ppermute | solution.py:694
  10.1 44.5 %collective-permute-start.6 = (f32[2,256,256]{2,1,0:T(8,128)}, f32[2,256,256]{2,1,0:T(8,128)S(1)}, u32[]{:S(2)}, u32[]{:S(2)}) collective-permute-start(f32[2,256,256]{2,1,0:T(8,128)} %get-tuple-element.162), channel_id=1, source_target_pairs={{0,4},{4,8},{8,12},{12,16},{16,20},{20,24},{24,28},{28,0},{1,5},{5... | collective-permute-start | bytes 1572872 | tf_op jit(solution)/shard_map/ppermute | solution.py:691
  11.4 23.5 %copy-start.1 = (f32[512]{0:T(512)S(1)}, f32[512]{0:T(512)}, u32[]{:S(2)}) copy-start(f32[512]{0:T(512)} %param.29) | copy-start | bytes 6148
  11.4 23.5 %copy-start.2 = (f32[512]{0:T(512)S(1)}, f32[512]{0:T(512)}, u32[]{:S(2)}) copy-start(f32[512]{0:T(512)} %param.30) | copy-start | bytes 6148
  11.5 25.2 %copy-start = (f32[2,512,256]{2,1,0:T(8,128)S(1)}, f32[2,512,256]{2,1,0:T(8,128)}, u32[]{:S(2)}) copy-start(f32[2,512,256]{2,1,0:T(8,128)} %get-tuple-element.166.refs_0_.first) | copy-start | bytes 3145732
  12.2 15.6 %copy-start.20 = (f32[12,8,256]{2,1,0:T(8,128)S(1)}, f32[12,8,256]{2,1,0:T(8,128)}, u32[]{:S(2)}) copy-start(f32[12,8,256]{2,1,0:T(8,128)} %get-tuple-element.206.refs_3_) | copy-start | bytes 294916 | tf_op jit(solution)/shard_map/cond
  16.9 1.5 %collective-permute-start = (f32[28,8,256]{2,1,0:T(8,128)S(1)}, f32[28,8,256]{2,1,0:T(8,128)S(1)}, u32[]{:S(2)}, u32[]{:S(2)}) collective-permute-start(f32[28,8,256]{2,1,0:T(8,128)S(1)} %get-tuple-element.78), channel_id=1, source_target_pairs={{0,1},{1,0},{2,3},{3,2},{4,5},{5,4},{6,7},{7,6},{8,9},{9,8},{10,11... | collective-permute-start | bytes 688136 | tf_op jit(solution)/shard_map/cond/branch_1_fun/ppermute | solution.py:651
  18.4 7.7 %collective-permute-start.1 = (f32[28,8,256]{2,1,0:T(8,128)S(1)}, f32[28,8,256]{2,1,0:T(8,128)S(1)}, u32[]{:S(2)}, u32[]{:S(2)}) collective-permute-start(f32[28,8,256]{2,1,0:T(8,128)S(1)} %add.8), channel_id=1, source_target_pairs={{0,2},{1,3},{2,0},{3,1},{4,6},{5,7},{6,4},{7,5},{8,10},{9,11},{10,... | collective-permute-start | bytes 688136 | tf_op jit(solution)/shard_map/cond/branch_1_fun/ppermute | solution.py:651
  26.2 1.6 %collective-permute-start.2 = (f32[28,8,256]{2,1,0:T(8,128)S(1)}, f32[28,8,256]{2,1,0:T(8,128)S(1)}, u32[]{:S(2)}, u32[]{:S(2)}) collective-permute-start(f32[28,8,256]{2,1,0:T(8,128)S(1)} %add.9.refs_0_), channel_id=1, source_target_pairs={{0,1},{1,0},{2,3},{3,2},{4,5},{5,4},{6,7},{7,6},{8,9},{9,8},{10,11... | collective-permute-start | bytes 688136 | tf_op jit(solution)/shard_map/cond/branch_1_fun/ppermute | solution.py:651
  29.4 20.3 %copy-start.5 = (f32[2,512,256]{2,1,0:T(8,128)}, f32[2,512,256]{2,1,0:T(8,128)S(1)}, u32[]{:S(2)}) copy-start(f32[2,512,256]{2,1,0:T(8,128)S(1)} %get-tuple-element.170.refs_3_.last) | copy-start | bytes 3145732
  29.4 25.3 %collective-permute-start.7 = (f32[2,256,256]{2,1,0:T(8,128)}, f32[2,256,256]{2,1,0:T(8,128)}, u32[]{:S(2)}, u32[]{:S(2)}) collective-permute-start(f32[2,256,256]{2,1,0:T(8,128)} %get-tuple-element.165), channel_id=1, source_target_pairs={{0,4},{4,8},{8,12},{12,16},{16,20},{20,24},{24,28},{28,0},{1,5},{5... | collective-permute-start | bytes 1572872 | tf_op jit(solution)/shard_map/ppermute | solution.py:691
  30.1 24.4 %collective-permute-start.10 = (f32[2,16,256]{2,1,0:T(8,128)}, f32[2,16,256]{2,1,0:T(8,128)}, u32[]{:S(2)}, u32[]{:S(2)}) collective-permute-start(f32[2,16,256]{2,1,0:T(8,128)} %get-tuple-element.212), channel_id=1, source_target_pairs={{4,0},{8,4},{12,8},{16,12},{20,16},{24,20},{28,24},{0,28},{5,1},{9... | collective-permute-start | bytes 98312 | tf_op jit(solution)/shard_map/ppermute | solution.py:694
  34.8 19.8 %collective-permute-start.9 = (f32[2,16,256]{2,1,0:T(8,128)}, f32[2,16,256]{2,1,0:T(8,128)}, u32[]{:S(2)}, u32[]{:S(2)}) collective-permute-start(f32[2,16,256]{2,1,0:T(8,128)} %get-tuple-element.213), channel_id=1, source_target_pairs={{0,4},{4,8},{8,12},{12,16},{16,20},{20,24},{24,28},{28,0},{1,5},{5... | collective-permute-start | bytes 98312 | tf_op jit(solution)/shard_map/ppermute | solution.py:691
  36.6 23.0 %copy-start.7 = (bf16[512,96]{1,0:T(8,128)(2,1)}, bf16[512,96]{1,0:T(8,128)(2,1)S(1)}, u32[]{:S(2)}) copy-start(bf16[512,96]{1,0:T(8,128)(2,1)S(1)} %get-tuple-element.171.refs_5_.gain_w.refs_4_) | copy-start | bytes 294916
  54.6 50.1 %collective-permute-start.13 = (f32[2,512,256]{2,1,0:T(8,128)}, f32[2,512,256]{2,1,0:T(8,128)S(1)}, u32[]{:S(2)}, u32[]{:S(2)}) collective-permute-start(f32[2,512,256]{2,1,0:T(8,128)} %get-tuple-element.193), channel_id=1, source_target_pairs={{4,0},{8,4},{12,8},{16,12},{20,16},{24,20},{28,24},{0,28},{5,1},{9... | collective-permute-start | bytes 3145736 | tf_op jit(solution)/shard_map/ppermute | solution.py:694
  59.6 45.2 %collective-permute-start.11 = (f32[2,256,256]{2,1,0:T(8,128)}, f32[2,256,256]{2,1,0:T(8,128)S(1)}, u32[]{:S(2)}, u32[]{:S(2)}) collective-permute-start(f32[2,256,256]{2,1,0:T(8,128)} %get-tuple-element.178), channel_id=1, source_target_pairs={{0,4},{4,8},{8,12},{12,16},{16,20},{20,24},{24,28},{28,0},{1,5},{5... | collective-permute-start | bytes 1572872 | tf_op jit(solution)/shard_map/ppermute | solution.py:691
  65.3 1.5 %collective-permute-start.3 = (f32[28,8,256]{2,1,0:T(8,128)S(1)}, f32[28,8,256]{2,1,0:T(8,128)S(1)}, u32[]{:S(2)}, u32[]{:S(2)}) collective-permute-start(f32[28,8,256]{2,1,0:T(8,128)S(1)} %get-tuple-element.105), channel_id=1, source_target_pairs={{0,1},{1,0},{2,3},{3,2},{4,5},{5,4},{6,7},{7,6},{8,9},{9,8},{10,11... | collective-permute-start | bytes 688136 | tf_op jit(solution)/shard_map/cond/branch_1_fun/ppermute | solution.py:651
  66.9 7.7 %collective-permute-start.4 = (f32[28,8,256]{2,1,0:T(8,128)S(1)}, f32[28,8,256]{2,1,0:T(8,128)S(1)}, u32[]{:S(2)}, u32[]{:S(2)}) collective-permute-start(f32[28,8,256]{2,1,0:T(8,128)S(1)} %add.10), channel_id=1, source_target_pairs={{0,2},{1,3},{2,0},{3,1},{4,6},{5,7},{6,4},{7,5},{8,10},{9,11},{10,... | collective-permute-start | bytes 688136 | tf_op jit(solution)/shard_map/cond/branch_1_fun/ppermute | solution.py:651
  74.6 1.6 %collective-permute-start.5 = (f32[28,8,256]{2,1,0:T(8,128)S(1)}, f32[28,8,256]{2,1,0:T(8,128)S(1)}, u32[]{:S(2)}, u32[]{:S(2)}) collective-permute-start(f32[28,8,256]{2,1,0:T(8,128)S(1)} %add.11.refs_0_), channel_id=1, source_target_pairs={{0,1},{1,0},{2,3},{3,2},{4,5},{5,4},{6,7},{7,6},{8,9},{9,8},{10,11... | collective-permute-start | bytes 688136 | tf_op jit(solution)/shard_map/cond/branch_1_fun/ppermute | solution.py:651
  82.7 22.0 %collective-permute-start.12 = (f32[2,256,256]{2,1,0:T(8,128)S(1)}, f32[2,256,256]{2,1,0:T(8,128)S(1)}, u32[]{:S(2)}, u32[]{:S(2)}) collective-permute-start(f32[2,256,256]{2,1,0:T(8,128)S(1)} %copy-done.13), channel_id=1, source_target_pairs={{0,4},{4,8},{8,12},{12,16},{16,20},{20,24},{24,28},{28,0},{1,5},{5... | collective-permute-start | bytes 1572872 | tf_op jit(solution)/shard_map/ppermute | solution.py:691
  83.3 21.3 %collective-permute-start.15 = (f32[2,16,256]{2,1,0:T(8,128)S(1)}, f32[2,16,256]{2,1,0:T(8,128)S(1)}, u32[]{:S(2)}, u32[]{:S(2)}) collective-permute-start(f32[2,16,256]{2,1,0:T(8,128)S(1)} %get-tuple-element.210), channel_id=1, source_target_pairs={{4,0},{8,4},{12,8},{16,12},{20,16},{24,20},{28,24},{0,28},{5,1},{9... | collective-permute-start | bytes 98312 | tf_op jit(solution)/shard_map/ppermute | solution.py:694
  87.6 17.2 %collective-permute-start.14 = (f32[2,16,256]{2,1,0:T(8,128)S(1)}, f32[2,16,256]{2,1,0:T(8,128)S(1)}, u32[]{:S(2)}, u32[]{:S(2)}) collective-permute-start(f32[2,16,256]{2,1,0:T(8,128)S(1)} %get-tuple-element.211), channel_id=1, source_target_pairs={{0,4},{4,8},{8,12},{12,16},{16,20},{20,24},{24,28},{28,0},{1,5},{5... | collective-permute-start | bytes 98312 | tf_op jit(solution)/shard_map/ppermute | solution.py:691
  (18 other events, 159.6 us)

commit v5 on v3

--- a/solution.py
+++ b/solution.py
@@ -576,17 +576,19 @@
             for copy in copies(step - 2, slot):
                 copy.wait()
 
-        for i in range(4):
-            if i < 2:
-                value = near_low[i] + jnp.where(step == 0, early[i], late[i])
-            else:
-                value = near_high[i - 2] + high[i - 2]
-            s = before[i] if i < 2 else after[i - 2]
-            store_pieces(near, i, value * matmul(gain_w[...], share_operand(s)))
-        for i in range(4):
-            result[slot, i] = spread(own[i], frac[...], stencil(near, circ, *TERMS[i]))
-        for copy in copies(step, slot):
-            copy.start()
+        started = copies(step, slot)
+        for side in ((0, 1), (2, 3)):
+            for i in side:
+                if i < 2:
+                    value = near_low[i] + jnp.where(step == 0, early[i], late[i])
+                else:
+                    value = near_high[i - 2] + high[i - 2]
+                s = before[i] if i < 2 else after[i - 2]
+                store_pieces(near, i, value * matmul(gain_w[...], share_operand(s)))
+            for i in side:
+                result[slot, i] = spread(own[i], frac[...], stencil(near, circ, *TERMS[i]))
+            for i in side:
+                started[i].start()
 
         @pl.when(step == steps - 1)
         def _():

time: 108 us -> 109 us (level)
  no operation moved by 1% of the time
where the time goes in v5:
time: 109 us; the launch traced here: 108 us
  Pallas kernels  47.7 us (44%)
  waiting for transfers between devices  36.4 us (33%)
  starting transfers between devices  19.7 us (18%)
  local copies, waits for them, and re-layouts  2.44 us (2%)
  between operations  1.91 us (2%)
    ppermute x4, waiting for transfers between devices, up(): return lax.ppermute(x, 'space', backward)  18.3 us
    ppermute x6, waiting for transfers between devices, exchange(): return lax.ppermute(x, 'taxa', [(i, i ^ step) for i in range(count)])  18 us
    ppermute x4, starting transfers between devices, up(): return lax.ppermute(x, 'space', backward)  13.1 us
    pallas_call x1, Pallas kernels, day_one_inside(): pl.pallas_call(kernel, name='day_one_inside', grid=(count // block,), out...  13 us
    pallas_call x1, Pallas kernels, day_two(): pl.pallas_call(kernel, name='day_two', grid=(steps,), out_shape=[jax.Shap...  7.16 us
    pallas_call x1, Pallas kernels, day_one_rim(): pl.pallas_call(kernel, name='day_one_rim', grid=(count // block,), out_sh...  5.44 us
    pallas_call x1, Pallas kernels, day_one_beyond(): pl.pallas_call(kernel, name='day_one_beyond', grid=(count // block,), out...  4.69 us
    pallas_call x1, Pallas kernels, first_sums(): pl.pallas_call(kernel, name='first_sums', grid=(count // block,), out_sha...  4.65 us
  transfers between devices with their start and end apart: 15, of which 8 were waited for; matrix products, arithmetic and copies ran while one was open for 2% of the time, Pallas kernels for 37%

profile of v5, /device:TPU:0, one launch (start us, length us, event | category | flops | bytes accessed | tf_op | source)
XLA Modules:
  0.0 108.4 jit_solution(4594882656874916147)
XLA Ops:
  0.8 3.3 %take_first.1 = (f32[2,512,256]{2,1,0:T(8,128)}, f32[2,512,256]{2,1,0:T(8,128)}) custom-call(f32[512,8,256]{2,1,0:T(8,128)} %source.1), custom_call_target="tpu_custom_call" | custom-call | flops 1000 | bytes 1000 | tf_op jit(solution)/shard_map/take_first/pallas_call | solution.py:70
  4.0 3.0 %collective-permute-start.6 = (f32[2,512,256]{2,1,0:T(8,128)}, f32[2,512,256]{2,1,0:T(8,128)}, u32[]{:S(2)}, u32[]{:S(2)}) collective-permute-start(f32[2,512,256]{2,1,0:T(8,128)} %get-tuple-element.153.refs_3_.last), channel_id=1, source_target_pairs={{0,4},{4,8},{8,12},{12,16},{16,20},{20,24},{24,28},{28,0},{1,5},{5... | collective-permute-start | bytes 3145736 | tf_op jit(solution)/shard_map/ppermute | solution.py:689
  7.0 3.1 %collective-permute-start.7 = (f32[2,512,256]{2,1,0:T(8,128)}, f32[2,512,256]{2,1,0:T(8,128)}, u32[]{:S(2)}, u32[]{:S(2)}) collective-permute-start(f32[2,512,256]{2,1,0:T(8,128)} %get-tuple-element.154.refs_0_.first), channel_id=1, source_target_pairs={{4,0},{8,4},{12,8},{16,12},{20,16},{24,20},{28,24},{0,28},{5,1},{9... | collective-permute-start | bytes 3145736 | tf_op jit(solution)/shard_map/ppermute | solution.py:692
  10.1 0.5 slice.22
  11.4 17.2 %conditional.2 = (f32[2,512,256]{2,1,0:T(8,128)}, f32[2,512,256]{2,1,0:T(8,128)S(1)}, bf16[128,512]{1,0:T(8,128)(2,1)}, f32[40,8,256]{2,1,0:T(8,128)}, f32[12,8,...) conditional(s32[]{:T(128)} %bitcast, () %tuple.27, (s32[40,512]{1,0:T(8,128)S(1)}, ...), branch_computations={%region_0.0_spmd, %region_1.0_spmd} | conditional | flops 117688 | bytes 6360252 | solution.py:663
  11.5 4.6 %first_sums.1 = (f32[2,512,256]{2,1,0:T(8,128)}, f32[2,512,256]{2,1,0:T(8,128)S(1)}, f32[28,8,256]{2,1,0:T(8,128)S(1)}, f32[28,8,256]{2,1,0:T(8,128)S(1)}) custom-call(f32[512,8,256]{2,1,0:T(8,128)} %get-tuple-element.66.source, bf16[128,512]{1,0:T(8,128)(2,1)S(1)} %sum_weights.1.weight, s32[1]{0:T(128)} %get-tuple-element.71.side.refs_5_), custom_call_target="tpu_custom_call" | custom-call | flops 1000 | bytes 1000 | tf_op jit(solution)/shard_map/cond/branch_1_fun/first_sums/pallas_call | solution.py:197
  16.2 1.5 %collective-permute-done = f32[28,8,256]{2,1,0:T(8,128)S(1)} collective-permute-done((f32[28,8,256]{2,1,0:T(8,128)S(1)}, f32[28,8,256]{2,1,0:T(8,128)S(1)}, u32[]{:S(2)}, u32[]{:S(2)}) %collective-permute-start) | collective-permute-done | bytes 229408 | tf_op jit(solution)/shard_map/cond/branch_1_fun/ppermute | solution.py:649
  17.7 1.7 %collective-permute-start.1 = (f32[28,8,256]{2,1,0:T(8,128)S(1)}, f32[28,8,256]{2,1,0:T(8,128)S(1)}, u32[]{:S(2)}, u32[]{:S(2)}) collective-permute-start(f32[28,8,256]{2,1,0:T(8,128)S(1)} %add.8), channel_id=1, source_target_pairs={{0,2},{1,3},{2,0},{3,1},{4,6},{5,7},{6,4},{7,5},{8,10},{9,11},{10,... | collective-permute-start | bytes 688136 | tf_op jit(solution)/shard_map/cond/branch_1_fun/ppermute | solution.py:649
  19.4 6.0 %collective-permute-done.1 = f32[28,8,256]{2,1,0:T(8,128)S(1)} collective-permute-done((f32[28,8,256]{2,1,0:T(8,128)S(1)}, f32[28,8,256]{2,1,0:T(8,128)S(1)}, u32[]{:S(2)}, u32[]{:S(2)}) %collective-permute-start.1) | collective-permute-done | bytes 229408 | tf_op jit(solution)/shard_map/cond/branch_1_fun/ppermute | solution.py:649
  25.5 0.1 collective-permute-start.2
  25.5 1.5 %collective-permute-done.2.refs_1_ = f32[28,8,256]{2,1,0:T(8,128)S(1)} collective-permute-done((f32[28,8,256]{2,1,0:T(8,128)S(1)}, f32[28,8,256]{2,1,0:T(8,128)S(1)}, u32[]{:S(2)}, u32[]{:S(2)}) %collective-permute-start.2) | collective-permute-done | bytes 229408 | tf_op jit(solution)/shard_map/cond/branch_1_fun/ppermute | solution.py:649
  27.0 1.6 %cell_update.2 = (f32[40,8,256]{2,1,0:T(8,128)}, f32[12,8,256]{2,1,0:T(8,128)}, f32[14,8,256]{2,1,0:T(8,128)}, f32[8,16,256]{2,1,0:T(8,128)S(1)}) custom-call(f32[28,8,256]{2,1,0:T(8,128)S(1)} %add.9.refs_0_, f32[28,8,256]{2,1,0:T(8,128)S(1)} %collective-permute-done.2.refs_1_, f32[40,8,256]{2,1,0:T(8,128)S(1)} %copy-done.16, f32[12,8,256]{2,1,0:T(8,128)S(1)} %copy-done.20, ...), custom_call_target="tpu_custom_call" | custom-call | flops 1000 | bytes 1000 | tf_op jit(solution)/shard_map/cond/branch_1_fun/cell_update/pallas_call | solution.py:259
  28.6 0.7 fusion.2
  29.3 2.0 %collective-permute-start.9 = (f32[2,16,256]{2,1,0:T(8,128)}, f32[2,16,256]{2,1,0:T(8,128)}, u32[]{:S(2)}, u32[]{:S(2)}) collective-permute-start(f32[2,16,256]{2,1,0:T(8,128)} %get-tuple-element.198), channel_id=1, source_target_pairs={{4,0},{8,4},{12,8},{16,12},{20,16},{24,20},{28,24},{0,28},{5,1},{9... | collective-permute-start | bytes 98312 | tf_op jit(solution)/shard_map/ppermute | solution.py:692
  31.3 0.1 copy.24.offs
  31.4 1.7 %spread_operands.1 = (bf16[512,96]{1,0:T(8,128)(2,1)S(1)}, f32[512,128]{1,0:T(8,128)S(1)}, bf16[1280,256]{1,0:T(8,128)(2,1)S(1)}) custom-call(s32[40,512]{1,0:T(8,128)} %bitcast.10, s32[14,512]{1,0:T(8,128)} %bitcast.12, f32[1,512]{1,0:T(1,128)S(1)} %bitcast.15, f32[1,512]{1,0:T(1,128)} %bitcast.16, f32[1,512]{1,0:T(1,128)S(1)} %bitcast.8, ...), custom_call_target="tpu_custom_call" | custom-call | flops 1000 | bytes 1000 | tf_op jit(solution)/shard_map/spread_operands/pallas_call | solution.py:159
  33.2 13.0 %day_one_inside.1 = (f32[8,512,256]{2,1,0:T(8,128)S(1)}, f32[2,512,256]{2,1,0:T(8,128)S(1)}, f32[2,512,256]{2,1,0:T(8,128)}, f32[4,64,256]{2,1,0:T(8,128)S(1)}) custom-call(f32[2,512,256]{2,1,0:T(8,128)S(1)} %copy-done, f32[2,512,256]{2,1,0:T(8,128)} %get-tuple-element.156.refs_1_, f32[2,512,256]{2,1,0:T(8,128)S(1)} %get-tuple-element.157.refs_2_, ...), custom_call_target="tpu_custom_call" | custom-call | flops 1000 | bytes 1000 | tf_op jit(solution)/shard_map/day_one_inside/pallas_call | solution.py:347
  46.2 1.0 fusion
  47.2 8.6 %collective-permute-done.9.after = f32[2,16,256]{2,1,0:T(8,128)} collective-permute-done((f32[2,16,256]{2,1,0:T(8,128)}, f32[2,16,256]{2,1,0:T(8,128)}, u32[]{:S(2)}, u32[]{:S(2)}) %collective-permute-start.9) | collective-permute-done | bytes 32800 | tf_op jit(solution)/shard_map/ppermute | solution.py:692
  55.9 3.3 %collective-permute-start.12 = (f32[2,512,256]{2,1,0:T(8,128)}, f32[2,512,256]{2,1,0:T(8,128)S(1)}, u32[]{:S(2)}, u32[]{:S(2)}) collective-permute-start(f32[2,512,256]{2,1,0:T(8,128)} %get-tuple-element.179), channel_id=1, source_target_pairs={{4,0},{8,4},{12,8},{16,12},{20,16},{24,20},{28,24},{0,28},{5,1},{9... | collective-permute-start | bytes 3145736 | tf_op jit(solution)/shard_map/ppermute | solution.py:692
  59.3 17.9 %conditional.3 = (f32[4,512,256]{2,1,0:T(8,128)}, f32[40,8,256]{2,1,0:T(8,128)}, f32[12,8,256]{2,1,0:T(8,128)}, f32[14,8,256]{2,1,0:T(8,128)}, f32[8,16,256]{2,1,0:T(8,128)}) conditional(s32[]{:T(128)} %bitcast, () %tuple.30, (f32[2,512,256]{2,1,0:T(8,128)}, f32[2,512,256]{2,1,0:T(8,128)}, f32[8,512,256]{2,1,0:T(8,128)S(1)}, ...), branch_computations={%region_2.0_spmd, %region_3.0_spmd} | conditional | flops 116688 | bytes 4130928 | solution.py:663
  59.3 5.4 %day_one_rim.1 = (f32[4,512,256]{2,1,0:T(8,128)}, f32[28,8,256]{2,1,0:T(8,128)S(1)}, f32[28,8,256]{2,1,0:T(8,128)S(1)}) custom-call(f32[2,512,256]{2,1,0:T(8,128)} %get-tuple-element.88.low, f32[2,512,256]{2,1,0:T(8,128)} %get-tuple-element.89.high, f32[8,512,256]{2,1,0:T(8,128)S(1)} %get-tuple-element.90.first.last, ...), custom_call_target="tpu_custom_call" | custom-call | flops 1000 | bytes 1000 | tf_op jit(solution)/shard_map/cond/branch_1_fun/day_one_rim/pallas_call | solution.py:407
  64.7 1.5 %collective-permute-done.3 = f32[28,8,256]{2,1,0:T(8,128)S(1)} collective-permute-done((f32[28,8,256]{2,1,0:T(8,128)S(1)}, f32[28,8,256]{2,1,0:T(8,128)S(1)}, u32[]{:S(2)}, u32[]{:S(2)}) %collective-permute-start.3) | collective-permute-done | bytes 229408 | tf_op jit(solution)/shard_map/cond/branch_1_fun/ppermute | solution.py:649
  66.3 1.6 %collective-permute-start.4 = (f32[28,8,256]{2,1,0:T(8,128)S(1)}, f32[28,8,256]{2,1,0:T(8,128)S(1)}, u32[]{:S(2)}, u32[]{:S(2)}) collective-permute-start(f32[28,8,256]{2,1,0:T(8,128)S(1)} %add.10), channel_id=1, source_target_pairs={{0,2},{1,3},{2,0},{3,1},{4,6},{5,7},{6,4},{7,5},{8,10},{9,11},{10,... | collective-permute-start | bytes 688136 | tf_op jit(solution)/shard_map/cond/branch_1_fun/ppermute | solution.py:649
  67.8 6.1 %collective-permute-done.4 = f32[28,8,256]{2,1,0:T(8,128)S(1)} collective-permute-done((f32[28,8,256]{2,1,0:T(8,128)S(1)}, f32[28,8,256]{2,1,0:T(8,128)S(1)}, u32[]{:S(2)}, u32[]{:S(2)}) %collective-permute-start.4) | collective-permute-done | bytes 229408 | tf_op jit(solution)/shard_map/cond/branch_1_fun/ppermute | solution.py:649
  74.1 1.5 %collective-permute-done.5.refs_1_ = f32[28,8,256]{2,1,0:T(8,128)S(1)} collective-permute-done((f32[28,8,256]{2,1,0:T(8,128)S(1)}, f32[28,8,256]{2,1,0:T(8,128)S(1)}, u32[]{:S(2)}, u32[]{:S(2)}) %collective-permute-start.5) | collective-permute-done | bytes 229408 | tf_op jit(solution)/shard_map/cond/branch_1_fun/ppermute | solution.py:649
  75.5 1.7 %cell_update.3 = (f32[40,8,256]{2,1,0:T(8,128)}, f32[12,8,256]{2,1,0:T(8,128)}, f32[14,8,256]{2,1,0:T(8,128)}, f32[8,16,256]{2,1,0:T(8,128)}) custom-call(f32[28,8,256]{2,1,0:T(8,128)S(1)} %add.11.refs_0_, f32[28,8,256]{2,1,0:T(8,128)S(1)} %collective-permute-done.5.refs_1_, f32[40,8,256]{2,1,0:T(8,128)S(1)} %get-tuple-element.102.refs_2_, ...), custom_call_target="tpu_custom_call" | custom-call | flops 1000 | bytes 1000 | tf_op jit(solution)/shard_map/cond/branch_1_fun/cell_update/pallas_call | solution.py:259
  77.2 4.7 %day_one_beyond.1.near_low.near_high = f32[4,512,256]{2,1,0:T(8,128)S(1)} custom-call(f32[2,512,256]{2,1,0:T(8,128)} %collective-permute-done.6.low, f32[2,512,256]{2,1,0:T(8,128)} %collective-permute-done.7.high, f32[2,512,256]{2,1,0:T(8,128)S(1)} %copy-done, f32[2,512,256]{2,1,0:T(8,128)S(1)} %copy-done.1, f32[8,16,256]{2,1,0:T(8,128)} %copy-done.11, ...), custom_call_target="tpu_custom_call" | custom-call | flops 1000 | bytes 1000 | tf_op jit(solution)/shard_map/day_one_beyond/pallas_call | solution.py:456
  82.0 4.8 %collective-permute-start.14 = (f32[2,16,256]{2,1,0:T(8,128)S(1)}, f32[2,16,256]{2,1,0:T(8,128)S(1)}, u32[]{:S(2)}, u32[]{:S(2)}) collective-permute-start(f32[2,16,256]{2,1,0:T(8,128)S(1)} %get-tuple-element.196), channel_id=1, source_target_pairs={{4,0},{8,4},{12,8},{16,12},{20,16},{24,20},{28,24},{0,28},{5,1},{9... | collective-permute-start | bytes 98312 | tf_op jit(solution)/shard_map/ppermute | solution.py:692
  86.8 7.2 %day_two.1 = (f32[512,8,256]{2,1,0:T(8,128)}, f32[4,512,256]{2,1,0:T(8,128)S(1)}) custom-call(f32[8,512,256]{2,1,0:T(8,128)S(1)} %copy-done.5, f32[8,512,256]{2,1,0:T(8,128)S(1)} %copy-done.5, f32[4,512,256]{2,1,0:T(8,128)S(1)} %copy-done.8, f32[8,16,256]{2,1,0:T(8,128)S(1)} %copy-done.13, bf16[512,96]{1,0:T(8,128)(2,1)S(1)} %get-tuple-element.158.refs_5_.gain_w.refs_4_, ...), custom_call_target="tpu_custom_call" | custom-call | flops 1000 | bytes 1000 | tf_op jit(solution)/shard_map/day_two/pallas_call | solution.py:525
  94.0 9.7 %collective-permute-done.14.after = f32[2,16,256]{2,1,0:T(8,128)S(1)} collective-permute-done((f32[2,16,256]{2,1,0:T(8,128)S(1)}, f32[2,16,256]{2,1,0:T(8,128)S(1)}, u32[]{:S(2)}, u32[]{:S(2)}) %collective-permute-start.14) | collective-permute-done | bytes 32800 | tf_op jit(solution)/shard_map/ppermute | solution.py:692
  103.7 4.5 %edges.1 = f32[512,8,256]{2,1,0:T(8,128)} custom-call(f32[2,256,256]{2,1,0:T(8,128)} %collective-permute-done.10.early, f32[2,256,256]{2,1,0:T(8,128)S(1)} %collective-permute-done.11.late, f32[2,512,256]{2,1,0:T(8,128)S(1)} %collective-permute-done.12.high, f32[4,512,256]{2,1,0:T(8,128)S(1)} %day_one_beyond.1.near_low.near_high, ...), custom_call_target="tpu_custom_call", output_to_operand_aliasing={{}: (11, {})} | custom-call | flops 1000 | bytes 1000 | tf_op jit(solution)/shard_map/edges/pallas_call | solution.py:601
  (88 shorter events, 0.6 us)
Async XLA Ops:
  4.0 51.8 %collective-permute-start.6 = (f32[2,512,256]{2,1,0:T(8,128)}, f32[2,512,256]{2,1,0:T(8,128)}, u32[]{:S(2)}, u32[]{:S(2)}) collective-permute-start(f32[2,512,256]{2,1,0:T(8,128)} %get-tuple-element.153.refs_3_.last), channel_id=1, source_target_pairs={{0,4},{4,8},{8,12},{12,16},{16,20},{20,24},{24,28},{28,0},{1,5},{5... | collective-permute-start | bytes 3145736 | tf_op jit(solution)/shard_map/ppermute | solution.py:689
  7.0 48.8 %collective-permute-start.7 = (f32[2,512,256]{2,1,0:T(8,128)}, f32[2,512,256]{2,1,0:T(8,128)}, u32[]{:S(2)}, u32[]{:S(2)}) collective-permute-start(f32[2,512,256]{2,1,0:T(8,128)} %get-tuple-element.154.refs_0_.first), channel_id=1, source_target_pairs={{4,0},{8,4},{12,8},{16,12},{20,16},{24,20},{28,24},{0,28},{5,1},{9... | collective-permute-start | bytes 3145736 | tf_op jit(solution)/shard_map/ppermute | solution.py:692
  11.4 20.0 %copy-start.2 = (f32[512]{0:T(512)S(1)}, f32[512]{0:T(512)}, u32[]{:S(2)}) copy-start(f32[512]{0:T(512)} %param.29) | copy-start | bytes 6148
  11.4 20.0 %copy-start.3 = (f32[512]{0:T(512)S(1)}, f32[512]{0:T(512)}, u32[]{:S(2)}) copy-start(f32[512]{0:T(512)} %param.30) | copy-start | bytes 6148
  11.4 21.7 %copy-start = (f32[2,512,256]{2,1,0:T(8,128)S(1)}, f32[2,512,256]{2,1,0:T(8,128)}, u32[]{:S(2)}) copy-start(f32[2,512,256]{2,1,0:T(8,128)} %get-tuple-element.154.refs_0_.first) | copy-start | bytes 3145732
  11.4 21.7 %copy-start.1 = (f32[2,512,256]{2,1,0:T(8,128)S(1)}, f32[2,512,256]{2,1,0:T(8,128)}, u32[]{:S(2)}) copy-start(f32[2,512,256]{2,1,0:T(8,128)} %get-tuple-element.153.refs_3_.last) | copy-start | bytes 3145732
  11.5 15.5 %copy-start.16 = (f32[40,8,256]{2,1,0:T(8,128)S(1)}, f32[40,8,256]{2,1,0:T(8,128)}, u32[]{:S(2)}) copy-start(f32[40,8,256]{2,1,0:T(8,128)} %get-tuple-element.191.refs_2_) | copy-start | bytes 983044 | tf_op jit(solution)/shard_map/cond
  11.5 15.5 %copy-start.20 = (f32[12,8,256]{2,1,0:T(8,128)S(1)}, f32[12,8,256]{2,1,0:T(8,128)}, u32[]{:S(2)}) copy-start(f32[12,8,256]{2,1,0:T(8,128)} %get-tuple-element.192.refs_3_) | copy-start | bytes 294916 | tf_op jit(solution)/shard_map/cond
  16.2 1.5 %collective-permute-start = (f32[28,8,256]{2,1,0:T(8,128)S(1)}, f32[28,8,256]{2,1,0:T(8,128)S(1)}, u32[]{:S(2)}, u32[]{:S(2)}) collective-permute-start(f32[28,8,256]{2,1,0:T(8,128)S(1)} %get-tuple-element.75), channel_id=1, source_target_pairs={{0,1},{1,0},{2,3},{3,2},{4,5},{5,4},{6,7},{7,6},{8,9},{9,8},{10,11... | collective-permute-start | bytes 688136 | tf_op jit(solution)/shard_map/cond/branch_1_fun/ppermute | solution.py:649
  17.7 7.7 %collective-permute-start.1 = (f32[28,8,256]{2,1,0:T(8,128)S(1)}, f32[28,8,256]{2,1,0:T(8,128)S(1)}, u32[]{:S(2)}, u32[]{:S(2)}) collective-permute-start(f32[28,8,256]{2,1,0:T(8,128)S(1)} %add.8), channel_id=1, source_target_pairs={{0,2},{1,3},{2,0},{3,1},{4,6},{5,7},{6,4},{7,5},{8,10},{9,11},{10,... | collective-permute-start | bytes 688136 | tf_op jit(solution)/shard_map/cond/branch_1_fun/ppermute | solution.py:649
  25.5 1.6 %collective-permute-start.2 = (f32[28,8,256]{2,1,0:T(8,128)S(1)}, f32[28,8,256]{2,1,0:T(8,128)S(1)}, u32[]{:S(2)}, u32[]{:S(2)}) collective-permute-start(f32[28,8,256]{2,1,0:T(8,128)S(1)} %add.9.refs_0_), channel_id=1, source_target_pairs={{0,1},{1,0},{2,3},{3,2},{4,5},{5,4},{6,7},{7,6},{8,9},{9,8},{10,11... | collective-permute-start | bytes 688136 | tf_op jit(solution)/shard_map/cond/branch_1_fun/ppermute | solution.py:649
  29.3 26.5 %collective-permute-start.9 = (f32[2,16,256]{2,1,0:T(8,128)}, f32[2,16,256]{2,1,0:T(8,128)}, u32[]{:S(2)}, u32[]{:S(2)}) collective-permute-start(f32[2,16,256]{2,1,0:T(8,128)} %get-tuple-element.198), channel_id=1, source_target_pairs={{4,0},{8,4},{12,8},{16,12},{20,16},{24,20},{28,24},{0,28},{5,1},{9... | collective-permute-start | bytes 98312 | tf_op jit(solution)/shard_map/ppermute | solution.py:692
  31.3 24.6 %collective-permute-start.8 = (f32[2,16,256]{2,1,0:T(8,128)}, f32[2,16,256]{2,1,0:T(8,128)}, u32[]{:S(2)}, u32[]{:S(2)}) collective-permute-start(f32[2,16,256]{2,1,0:T(8,128)} %get-tuple-element.199), channel_id=1, source_target_pairs={{0,4},{4,8},{8,12},{12,16},{16,20},{20,24},{24,28},{28,0},{1,5},{5... | collective-permute-start | bytes 98312 | tf_op jit(solution)/shard_map/ppermute | solution.py:689
  33.1 26.1 %copy-start.6 = (bf16[1280,256]{1,0:T(8,128)(2,1)}, bf16[1280,256]{1,0:T(8,128)(2,1)S(1)}, u32[]{:S(2)}) copy-start(bf16[1280,256]{1,0:T(8,128)(2,1)S(1)} %get-tuple-element.160.refs_7_.circ.refs_6_) | copy-start | bytes 1966084
  46.1 13.1 %copy-start.4 = (f32[8,512,256]{2,1,0:T(8,128)}, f32[8,512,256]{2,1,0:T(8,128)S(1)}, u32[]{:S(2)}) copy-start(f32[8,512,256]{2,1,0:T(8,128)S(1)} %get-tuple-element.168.refs_0_.refs_1_) | copy-start | bytes 12582916
  46.1 13.0 %copy-start.10 = (bf16[128,512]{1,0:T(8,128)(2,1)S(1)}, bf16[128,512]{1,0:T(8,128)(2,1)}, u32[]{:S(2)}) copy-start(bf16[128,512]{1,0:T(8,128)(2,1)} %get-tuple-element.161.refs_8_) | copy-start | bytes 393220
  46.2 13.0 %copy-start.12 = (f32[40,8,256]{2,1,0:T(8,128)S(1)}, f32[40,8,256]{2,1,0:T(8,128)}, u32[]{:S(2)}) copy-start(f32[40,8,256]{2,1,0:T(8,128)} %get-tuple-element.172) | copy-start | bytes 983044
  46.2 13.0 %copy-start.14 = (f32[14,8,256]{2,1,0:T(8,128)S(1)}, f32[14,8,256]{2,1,0:T(8,128)}, u32[]{:S(2)}) copy-start(f32[14,8,256]{2,1,0:T(8,128)} %get-tuple-element.174) | copy-start | bytes 344068
  46.2 13.0 %copy-start.15 = (f32[12,8,256]{2,1,0:T(8,128)S(1)}, f32[12,8,256]{2,1,0:T(8,128)}, u32[]{:S(2)}) copy-start(f32[12,8,256]{2,1,0:T(8,128)} %get-tuple-element.173) | copy-start | bytes 294916
  46.2 13.0 %copy-start.24 = (f32[40]{0:T(128)S(1)}, f32[40]{0:T(128)}, u32[]{:S(2)}) copy-start(f32[40]{0:T(128)} %param.31) | copy-start | bytes 484
  46.2 13.0 %copy-start.26 = (f32[40]{0:T(128)S(1)}, f32[40]{0:T(128)}, u32[]{:S(2)}) copy-start(f32[40]{0:T(128)} %param.32) | copy-start | bytes 484
  46.2 13.0 %copy-start.28 = (f32[40]{0:T(128)S(1)}, f32[40]{0:T(128)}, u32[]{:S(2)}) copy-start(f32[40]{0:T(128)} %param.33) | copy-start | bytes 484
  46.2 13.0 %copy-start.30 = (f32[14]{0:T(128)S(1)}, f32[14]{0:T(128)}, u32[]{:S(2)}) copy-start(f32[14]{0:T(128)} %param.34) | copy-start | bytes 172
  46.2 13.0 %copy-start.32 = (s32[40]{0:T(128)S(1)}, s32[40]{0:T(128)}, u32[]{:S(2)}) copy-start(s32[40]{0:T(128)} %param.26) | copy-start | bytes 484
  55.9 47.9 %collective-permute-start.12 = (f32[2,512,256]{2,1,0:T(8,128)}, f32[2,512,256]{2,1,0:T(8,128)S(1)}, u32[]{:S(2)}, u32[]{:S(2)}) collective-permute-start(f32[2,512,256]{2,1,0:T(8,128)} %get-tuple-element.179), channel_id=1, source_target_pairs={{4,0},{8,4},{12,8},{16,12},{20,16},{24,20},{28,24},{0,28},{5,1},{9... | collective-permute-start | bytes 3145736 | tf_op jit(solution)/shard_map/ppermute | solution.py:692
  59.2 44.5 %collective-permute-start.10 = (f32[2,256,256]{2,1,0:T(8,128)}, f32[2,256,256]{2,1,0:T(8,128)}, u32[]{:S(2)}, u32[]{:S(2)}) collective-permute-start(f32[2,256,256]{2,1,0:T(8,128)} %get-tuple-element.165), channel_id=1, source_target_pairs={{0,4},{4,8},{8,12},{12,16},{16,20},{20,24},{24,28},{28,0},{1,5},{5... | collective-permute-start | bytes 1572872 | tf_op jit(solution)/shard_map/ppermute | solution.py:689
  64.7 1.5 %collective-permute-start.3 = (f32[28,8,256]{2,1,0:T(8,128)S(1)}, f32[28,8,256]{2,1,0:T(8,128)S(1)}, u32[]{:S(2)}, u32[]{:S(2)}) collective-permute-start(f32[28,8,256]{2,1,0:T(8,128)S(1)} %get-tuple-element.101), channel_id=1, source_target_pairs={{0,1},{1,0},{2,3},{3,2},{4,5},{5,4},{6,7},{7,6},{8,9},{9,8},{10,11... | collective-permute-start | bytes 688136 | tf_op jit(solution)/shard_map/cond/branch_1_fun/ppermute | solution.py:649
  66.3 7.7 %collective-permute-start.4 = (f32[28,8,256]{2,1,0:T(8,128)S(1)}, f32[28,8,256]{2,1,0:T(8,128)S(1)}, u32[]{:S(2)}, u32[]{:S(2)}) collective-permute-start(f32[28,8,256]{2,1,0:T(8,128)S(1)} %add.10), channel_id=1, source_target_pairs={{0,2},{1,3},{2,0},{3,1},{4,6},{5,7},{6,4},{7,5},{8,10},{9,11},{10,... | collective-permute-start | bytes 688136 | tf_op jit(solution)/shard_map/cond/branch_1_fun/ppermute | solution.py:649
  74.0 1.6 %collective-permute-start.5 = (f32[28,8,256]{2,1,0:T(8,128)S(1)}, f32[28,8,256]{2,1,0:T(8,128)S(1)}, u32[]{:S(2)}, u32[]{:S(2)}) collective-permute-start(f32[28,8,256]{2,1,0:T(8,128)S(1)} %add.11.refs_0_), channel_id=1, source_target_pairs={{0,1},{1,0},{2,3},{3,2},{4,5},{5,4},{6,7},{7,6},{8,9},{9,8},{10,11... | collective-permute-start | bytes 688136 | tf_op jit(solution)/shard_map/cond/branch_1_fun/ppermute | solution.py:649
  81.9 21.8 %collective-permute-start.11 = (f32[2,256,256]{2,1,0:T(8,128)}, f32[2,256,256]{2,1,0:T(8,128)S(1)}, u32[]{:S(2)}, u32[]{:S(2)}) collective-permute-start(f32[2,256,256]{2,1,0:T(8,128)} %get-tuple-element.178), channel_id=1, source_target_pairs={{0,4},{4,8},{8,12},{12,16},{16,20},{20,24},{24,28},{28,0},{1,5},{5... | collective-permute-start | bytes 1572872 | tf_op jit(solution)/shard_map/ppermute | solution.py:689
  82.0 21.7 %collective-permute-start.14 = (f32[2,16,256]{2,1,0:T(8,128)S(1)}, f32[2,16,256]{2,1,0:T(8,128)S(1)}, u32[]{:S(2)}, u32[]{:S(2)}) collective-permute-start(f32[2,16,256]{2,1,0:T(8,128)S(1)} %get-tuple-element.196), channel_id=1, source_target_pairs={{4,0},{8,4},{12,8},{16,12},{20,16},{24,20},{28,24},{0,28},{5,1},{9... | collective-permute-start | bytes 98312 | tf_op jit(solution)/shard_map/ppermute | solution.py:692
  86.8 16.9 %collective-permute-start.13 = (f32[2,16,256]{2,1,0:T(8,128)S(1)}, f32[2,16,256]{2,1,0:T(8,128)S(1)}, u32[]{:S(2)}, u32[]{:S(2)}) collective-permute-start(f32[2,16,256]{2,1,0:T(8,128)S(1)} %get-tuple-element.197), channel_id=1, source_target_pairs={{0,4},{4,8},{8,12},{12,16},{16,20},{20,24},{24,28},{28,0},{1,5},{5... | collective-permute-start | bytes 98312 | tf_op jit(solution)/shard_map/ppermute | solution.py:689
  (17 other events, 157.0 us)

commit v6 on v3

--- a/solution.py
+++ b/solution.py
@@ -692,7 +692,7 @@
     count, rows, width = biomass.shape
     block = min(count, 256)
 
-    first, last = take_first(biomass, (0, 1, rows - 2, rows - 1), 4)
+    first, last = take_first(biomass, (0, 1, rows - 2, rows - 1), 2)
     inner_low, inner_high = down(last), up(first)
     odd = lax.rem(lax.axis_index("taxa"), 2).reshape(1).astype(jnp.int32)
     traits = (enz_traits.T, mono_traits.T, prod_rate.reshape(1, count), uptake_rate.reshape(1, count))

time: 108 us -> 108 us (level)
  no operation moved by 1% of the time
where the time goes in v6:
time: 108 us
  Pallas kernels  47.1 us (44%)
  waiting for transfers between devices  36.4 us (34%)
  starting transfers between devices  19.7 us (18%)
  local copies, waits for them, and re-layouts  2.44 us (2%)
  between operations  1.91 us (2%)
    ppermute x4, waiting for transfers between devices, up(): return lax.ppermute(x, 'space', backward)  18.3 us
    ppermute x6, waiting for transfers between devices, exchange(): return lax.ppermute(x, 'taxa', [(i, i ^ step) for i in range(count)])  18 us
    ppermute x4, starting transfers between devices, up(): return lax.ppermute(x, 'space', backward)  13.1 us
    pallas_call x1, Pallas kernels, day_one_inside(): pl.pallas_call(kernel, name='day_one_inside', grid=(count // block,), out...  13 us
    pallas_call x1, Pallas kernels, day_two(): pl.pallas_call(kernel, name='day_two', grid=(steps,), out_shape=[jax.Shap...  7.16 us
    pallas_call x1, Pallas kernels, day_one_rim(): pl.pallas_call(kernel, name='day_one_rim', grid=(count // block,), out_sh...  5.44 us
    pallas_call x1, Pallas kernels, day_one_beyond(): pl.pallas_call(kernel, name='day_one_beyond', grid=(count // block,), out...  4.7 us
    pallas_call x1, Pallas kernels, first_sums(): pl.pallas_call(kernel, name='first_sums', grid=(count // block,), out_sha...  4.65 us
  transfers between devices with their start and end apart: 15, of which 8 were waited for; matrix products, arithmetic and copies ran while one was open for 2% of the time, Pallas kernels for 37%

profile of v6, /device:TPU:0, one launch (start us, length us, event | category | flops | bytes accessed | tf_op | source)
XLA Modules:
  0.0 107.8 jit_solution(17699226380166322027)
XLA Ops:
  0.8 3.4 %take_first.1 = (f32[2,512,256]{2,1,0:T(8,128)}, f32[2,512,256]{2,1,0:T(8,128)}) custom-call(f32[512,8,256]{2,1,0:T(8,128)} %source.1), custom_call_target="tpu_custom_call" | custom-call | flops 1000 | bytes 1000 | tf_op jit(solution)/shard_map/take_first/pallas_call | solution.py:70
  4.1 3.0 %collective-permute-start.6 = (f32[2,512,256]{2,1,0:T(8,128)}, f32[2,512,256]{2,1,0:T(8,128)}, u32[]{:S(2)}, u32[]{:S(2)}) collective-permute-start(f32[2,512,256]{2,1,0:T(8,128)} %get-tuple-element.153.refs_3_.last), channel_id=1, source_target_pairs={{0,4},{4,8},{8,12},{12,16},{16,20},{20,24},{24,28},{28,0},{1,5},{5... | collective-permute-start | bytes 3145736 | tf_op jit(solution)/shard_map/ppermute | solution.py:687
  7.1 3.1 %collective-permute-start.7 = (f32[2,512,256]{2,1,0:T(8,128)}, f32[2,512,256]{2,1,0:T(8,128)}, u32[]{:S(2)}, u32[]{:S(2)}) collective-permute-start(f32[2,512,256]{2,1,0:T(8,128)} %get-tuple-element.154.refs_0_.first), channel_id=1, source_target_pairs={{4,0},{8,4},{12,8},{16,12},{20,16},{24,20},{28,24},{0,28},{5,1},{9... | collective-permute-start | bytes 3145736 | tf_op jit(solution)/shard_map/ppermute | solution.py:690
  10.2 0.5 slice.22
  11.5 17.2 %conditional.2 = (f32[2,512,256]{2,1,0:T(8,128)}, f32[2,512,256]{2,1,0:T(8,128)S(1)}, bf16[128,512]{1,0:T(8,128)(2,1)}, f32[40,8,256]{2,1,0:T(8,128)}, f32[12,8,...) conditional(s32[]{:T(128)} %bitcast, () %tuple.27, (s32[40,512]{1,0:T(8,128)S(1)}, ...), branch_computations={%region_0.0_spmd, %region_1.0_spmd} | conditional | flops 117688 | bytes 6360252 | solution.py:661
  11.6 4.6 %first_sums.1 = (f32[2,512,256]{2,1,0:T(8,128)}, f32[2,512,256]{2,1,0:T(8,128)S(1)}, f32[28,8,256]{2,1,0:T(8,128)S(1)}, f32[28,8,256]{2,1,0:T(8,128)S(1)}) custom-call(f32[512,8,256]{2,1,0:T(8,128)} %get-tuple-element.66.source, bf16[128,512]{1,0:T(8,128)(2,1)S(1)} %sum_weights.1.weight, s32[1]{0:T(128)} %get-tuple-element.71.side.refs_5_), custom_call_target="tpu_custom_call" | custom-call | flops 1000 | bytes 1000 | tf_op jit(solution)/shard_map/cond/branch_1_fun/first_sums/pallas_call | solution.py:197
  16.3 1.5 %collective-permute-done = f32[28,8,256]{2,1,0:T(8,128)S(1)} collective-permute-done((f32[28,8,256]{2,1,0:T(8,128)S(1)}, f32[28,8,256]{2,1,0:T(8,128)S(1)}, u32[]{:S(2)}, u32[]{:S(2)}) %collective-permute-start) | collective-permute-done | bytes 229408 | tf_op jit(solution)/shard_map/cond/branch_1_fun/ppermute | solution.py:647
  17.8 1.7 %collective-permute-start.1 = (f32[28,8,256]{2,1,0:T(8,128)S(1)}, f32[28,8,256]{2,1,0:T(8,128)S(1)}, u32[]{:S(2)}, u32[]{:S(2)}) collective-permute-start(f32[28,8,256]{2,1,0:T(8,128)S(1)} %add.8), channel_id=1, source_target_pairs={{0,2},{1,3},{2,0},{3,1},{4,6},{5,7},{6,4},{7,5},{8,10},{9,11},{10,... | collective-permute-start | bytes 688136 | tf_op jit(solution)/shard_map/cond/branch_1_fun/ppermute | solution.py:647
  19.5 6.0 %collective-permute-done.1 = f32[28,8,256]{2,1,0:T(8,128)S(1)} collective-permute-done((f32[28,8,256]{2,1,0:T(8,128)S(1)}, f32[28,8,256]{2,1,0:T(8,128)S(1)}, u32[]{:S(2)}, u32[]{:S(2)}) %collective-permute-start.1) | collective-permute-done | bytes 229408 | tf_op jit(solution)/shard_map/cond/branch_1_fun/ppermute | solution.py:647
  25.6 0.1 collective-permute-start.2
  25.6 1.5 %collective-permute-done.2.refs_1_ = f32[28,8,256]{2,1,0:T(8,128)S(1)} collective-permute-done((f32[28,8,256]{2,1,0:T(8,128)S(1)}, f32[28,8,256]{2,1,0:T(8,128)S(1)}, u32[]{:S(2)}, u32[]{:S(2)}) %collective-permute-start.2) | collective-permute-done | bytes 229408 | tf_op jit(solution)/shard_map/cond/branch_1_fun/ppermute | solution.py:647
  27.1 1.6 %cell_update.2 = (f32[40,8,256]{2,1,0:T(8,128)}, f32[12,8,256]{2,1,0:T(8,128)}, f32[14,8,256]{2,1,0:T(8,128)}, f32[8,16,256]{2,1,0:T(8,128)S(1)}) custom-call(f32[28,8,256]{2,1,0:T(8,128)S(1)} %add.9.refs_0_, f32[28,8,256]{2,1,0:T(8,128)S(1)} %collective-permute-done.2.refs_1_, f32[40,8,256]{2,1,0:T(8,128)S(1)} %copy-done.16, f32[12,8,256]{2,1,0:T(8,128)S(1)} %copy-done.20, ...), custom_call_target="tpu_custom_call" | custom-call | flops 1000 | bytes 1000 | tf_op jit(solution)/shard_map/cond/branch_1_fun/cell_update/pallas_call | solution.py:259
  28.7 0.7 fusion.2
  29.4 2.0 %collective-permute-start.9 = (f32[2,16,256]{2,1,0:T(8,128)}, f32[2,16,256]{2,1,0:T(8,128)}, u32[]{:S(2)}, u32[]{:S(2)}) collective-permute-start(f32[2,16,256]{2,1,0:T(8,128)} %get-tuple-element.198), channel_id=1, source_target_pairs={{4,0},{8,4},{12,8},{16,12},{20,16},{24,20},{28,24},{0,28},{5,1},{9... | collective-permute-start | bytes 98312 | tf_op jit(solution)/shard_map/ppermute | solution.py:690
  31.4 0.1 copy.24.offs
  31.5 1.7 %spread_operands.1 = (bf16[512,96]{1,0:T(8,128)(2,1)S(1)}, f32[512,128]{1,0:T(8,128)S(1)}, bf16[1280,256]{1,0:T(8,128)(2,1)S(1)}) custom-call(s32[40,512]{1,0:T(8,128)} %bitcast.10, s32[14,512]{1,0:T(8,128)} %bitcast.12, f32[1,512]{1,0:T(1,128)S(1)} %bitcast.15, f32[1,512]{1,0:T(1,128)} %bitcast.16, f32[1,512]{1,0:T(1,128)S(1)} %bitcast.8, ...), custom_call_target="tpu_custom_call" | custom-call | flops 1000 | bytes 1000 | tf_op jit(solution)/shard_map/spread_operands/pallas_call | solution.py:159
  33.3 13.0 %day_one_inside.1 = (f32[8,512,256]{2,1,0:T(8,128)S(1)}, f32[2,512,256]{2,1,0:T(8,128)S(1)}, f32[2,512,256]{2,1,0:T(8,128)}, f32[4,64,256]{2,1,0:T(8,128)S(1)}) custom-call(f32[2,512,256]{2,1,0:T(8,128)S(1)} %copy-done, f32[2,512,256]{2,1,0:T(8,128)} %get-tuple-element.156.refs_1_, f32[2,512,256]{2,1,0:T(8,128)S(1)} %get-tuple-element.157.refs_2_, ...), custom_call_target="tpu_custom_call" | custom-call | flops 1000 | bytes 1000 | tf_op jit(solution)/shard_map/day_one_inside/pallas_call | solution.py:347
  46.3 1.0 fusion
  47.4 8.6 %collective-permute-done.9.after = f32[2,16,256]{2,1,0:T(8,128)} collective-permute-done((f32[2,16,256]{2,1,0:T(8,128)}, f32[2,16,256]{2,1,0:T(8,128)}, u32[]{:S(2)}, u32[]{:S(2)}) %collective-permute-start.9) | collective-permute-done | bytes 32800 | tf_op jit(solution)/shard_map/ppermute | solution.py:690
  56.0 3.3 %collective-permute-start.12 = (f32[2,512,256]{2,1,0:T(8,128)}, f32[2,512,256]{2,1,0:T(8,128)S(1)}, u32[]{:S(2)}, u32[]{:S(2)}) collective-permute-start(f32[2,512,256]{2,1,0:T(8,128)} %get-tuple-element.179), channel_id=1, source_target_pairs={{4,0},{8,4},{12,8},{16,12},{20,16},{24,20},{28,24},{0,28},{5,1},{9... | collective-permute-start | bytes 3145736 | tf_op jit(solution)/shard_map/ppermute | solution.py:690
  59.4 17.9 %conditional.3 = (f32[4,512,256]{2,1,0:T(8,128)}, f32[40,8,256]{2,1,0:T(8,128)}, f32[12,8,256]{2,1,0:T(8,128)}, f32[14,8,256]{2,1,0:T(8,128)}, f32[8,16,256]{2,1,0:T(8,128)}) conditional(s32[]{:T(128)} %bitcast, () %tuple.30, (f32[2,512,256]{2,1,0:T(8,128)}, f32[2,512,256]{2,1,0:T(8,128)}, f32[8,512,256]{2,1,0:T(8,128)S(1)}, ...), branch_computations={%region_2.0_spmd, %region_3.0_spmd} | conditional | flops 116688 | bytes 4130928 | solution.py:661
  59.4 5.4 %day_one_rim.1 = (f32[4,512,256]{2,1,0:T(8,128)}, f32[28,8,256]{2,1,0:T(8,128)S(1)}, f32[28,8,256]{2,1,0:T(8,128)S(1)}) custom-call(f32[2,512,256]{2,1,0:T(8,128)} %get-tuple-element.88.low, f32[2,512,256]{2,1,0:T(8,128)} %get-tuple-element.89.high, f32[8,512,256]{2,1,0:T(8,128)S(1)} %get-tuple-element.90.first.last, ...), custom_call_target="tpu_custom_call" | custom-call | flops 1000 | bytes 1000 | tf_op jit(solution)/shard_map/cond/branch_1_fun/day_one_rim/pallas_call | solution.py:407
  64.8 1.5 %collective-permute-done.3 = f32[28,8,256]{2,1,0:T(8,128)S(1)} collective-permute-done((f32[28,8,256]{2,1,0:T(8,128)S(1)}, f32[28,8,256]{2,1,0:T(8,128)S(1)}, u32[]{:S(2)}, u32[]{:S(2)}) %collective-permute-start.3) | collective-permute-done | bytes 229408 | tf_op jit(solution)/shard_map/cond/branch_1_fun/ppermute | solution.py:647
  66.4 1.6 %collective-permute-start.4 = (f32[28,8,256]{2,1,0:T(8,128)S(1)}, f32[28,8,256]{2,1,0:T(8,128)S(1)}, u32[]{:S(2)}, u32[]{:S(2)}) collective-permute-start(f32[28,8,256]{2,1,0:T(8,128)S(1)} %add.10), channel_id=1, source_target_pairs={{0,2},{1,3},{2,0},{3,1},{4,6},{5,7},{6,4},{7,5},{8,10},{9,11},{10,... | collective-permute-start | bytes 688136 | tf_op jit(solution)/shard_map/cond/branch_1_fun/ppermute | solution.py:647
  67.9 6.1 %collective-permute-done.4 = f32[28,8,256]{2,1,0:T(8,128)S(1)} collective-permute-done((f32[28,8,256]{2,1,0:T(8,128)S(1)}, f32[28,8,256]{2,1,0:T(8,128)S(1)}, u32[]{:S(2)}, u32[]{:S(2)}) %collective-permute-start.4) | collective-permute-done | bytes 229408 | tf_op jit(solution)/shard_map/cond/branch_1_fun/ppermute | solution.py:647
  74.2 1.5 %collective-permute-done.5.refs_1_ = f32[28,8,256]{2,1,0:T(8,128)S(1)} collective-permute-done((f32[28,8,256]{2,1,0:T(8,128)S(1)}, f32[28,8,256]{2,1,0:T(8,128)S(1)}, u32[]{:S(2)}, u32[]{:S(2)}) %collective-permute-start.5) | collective-permute-done | bytes 229408 | tf_op jit(solution)/shard_map/cond/branch_1_fun/ppermute | solution.py:647
  75.7 1.7 %cell_update.3 = (f32[40,8,256]{2,1,0:T(8,128)}, f32[12,8,256]{2,1,0:T(8,128)}, f32[14,8,256]{2,1,0:T(8,128)}, f32[8,16,256]{2,1,0:T(8,128)}) custom-call(f32[28,8,256]{2,1,0:T(8,128)S(1)} %add.11.refs_0_, f32[28,8,256]{2,1,0:T(8,128)S(1)} %collective-permute-done.5.refs_1_, f32[40,8,256]{2,1,0:T(8,128)S(1)} %get-tuple-element.102.refs_2_, ...), custom_call_target="tpu_custom_call" | custom-call | flops 1000 | bytes 1000 | tf_op jit(solution)/shard_map/cond/branch_1_fun/cell_update/pallas_call | solution.py:259
  77.3 4.7 %day_one_beyond.1.near_low.near_high = f32[4,512,256]{2,1,0:T(8,128)S(1)} custom-call(f32[2,512,256]{2,1,0:T(8,128)} %collective-permute-done.6.low, f32[2,512,256]{2,1,0:T(8,128)} %collective-permute-done.7.high, f32[2,512,256]{2,1,0:T(8,128)S(1)} %copy-done, f32[2,512,256]{2,1,0:T(8,128)S(1)} %copy-done.1, f32[8,16,256]{2,1,0:T(8,128)} %copy-done.11, ...), custom_call_target="tpu_custom_call" | custom-call | flops 1000 | bytes 1000 | tf_op jit(solution)/shard_map/day_one_beyond/pallas_call | solution.py:456
  82.1 4.8 %collective-permute-start.14 = (f32[2,16,256]{2,1,0:T(8,128)S(1)}, f32[2,16,256]{2,1,0:T(8,128)S(1)}, u32[]{:S(2)}, u32[]{:S(2)}) collective-permute-start(f32[2,16,256]{2,1,0:T(8,128)S(1)} %get-tuple-element.196), channel_id=1, source_target_pairs={{4,0},{8,4},{12,8},{16,12},{20,16},{24,20},{28,24},{0,28},{5,1},{9... | collective-permute-start | bytes 98312 | tf_op jit(solution)/shard_map/ppermute | solution.py:690
  86.9 7.2 %day_two.1 = (f32[512,8,256]{2,1,0:T(8,128)}, f32[4,512,256]{2,1,0:T(8,128)S(1)}) custom-call(f32[8,512,256]{2,1,0:T(8,128)S(1)} %copy-done.5, f32[8,512,256]{2,1,0:T(8,128)S(1)} %copy-done.5, f32[4,512,256]{2,1,0:T(8,128)S(1)} %copy-done.8, f32[8,16,256]{2,1,0:T(8,128)S(1)} %copy-done.13, bf16[512,96]{1,0:T(8,128)(2,1)S(1)} %get-tuple-element.158.refs_5_.gain_w.refs_4_, ...), custom_call_target="tpu_custom_call" | custom-call | flops 1000 | bytes 1000 | tf_op jit(solution)/shard_map/day_two/pallas_call | solution.py:525
  94.1 9.7 %collective-permute-done.14.after = f32[2,16,256]{2,1,0:T(8,128)S(1)} collective-permute-done((f32[2,16,256]{2,1,0:T(8,128)S(1)}, f32[2,16,256]{2,1,0:T(8,128)S(1)}, u32[]{:S(2)}, u32[]{:S(2)}) %collective-permute-start.14) | collective-permute-done | bytes 32800 | tf_op jit(solution)/shard_map/ppermute | solution.py:690
  103.8 3.8 %edges.1 = f32[512,8,256]{2,1,0:T(8,128)} custom-call(f32[2,256,256]{2,1,0:T(8,128)} %collective-permute-done.10.early, f32[2,256,256]{2,1,0:T(8,128)S(1)} %collective-permute-done.11.late, f32[2,512,256]{2,1,0:T(8,128)S(1)} %collective-permute-done.12.high, f32[4,512,256]{2,1,0:T(8,128)S(1)} %day_one_beyond.1.near_low.near_high, ...), custom_call_target="tpu_custom_call", output_to_operand_aliasing={{}: (11, {})} | custom-call | flops 1000 | bytes 1000 | tf_op jit(solution)/shard_map/edges/pallas_call | solution.py:599
  (88 shorter events, 0.6 us)
Async XLA Ops:
  4.1 51.8 %collective-permute-start.6 = (f32[2,512,256]{2,1,0:T(8,128)}, f32[2,512,256]{2,1,0:T(8,128)}, u32[]{:S(2)}, u32[]{:S(2)}) collective-permute-start(f32[2,512,256]{2,1,0:T(8,128)} %get-tuple-element.153.refs_3_.last), channel_id=1, source_target_pairs={{0,4},{4,8},{8,12},{12,16},{16,20},{20,24},{24,28},{28,0},{1,5},{5... | collective-permute-start | bytes 3145736 | tf_op jit(solution)/shard_map/ppermute | solution.py:687
  7.1 48.8 %collective-permute-start.7 = (f32[2,512,256]{2,1,0:T(8,128)}, f32[2,512,256]{2,1,0:T(8,128)}, u32[]{:S(2)}, u32[]{:S(2)}) collective-permute-start(f32[2,512,256]{2,1,0:T(8,128)} %get-tuple-element.154.refs_0_.first), channel_id=1, source_target_pairs={{4,0},{8,4},{12,8},{16,12},{20,16},{24,20},{28,24},{0,28},{5,1},{9... | collective-permute-start | bytes 3145736 | tf_op jit(solution)/shard_map/ppermute | solution.py:690
  11.5 20.0 %copy-start.2 = (f32[512]{0:T(512)S(1)}, f32[512]{0:T(512)}, u32[]{:S(2)}) copy-start(f32[512]{0:T(512)} %param.29) | copy-start | bytes 6148
  11.5 20.0 %copy-start.3 = (f32[512]{0:T(512)S(1)}, f32[512]{0:T(512)}, u32[]{:S(2)}) copy-start(f32[512]{0:T(512)} %param.30) | copy-start | bytes 6148
  11.5 21.7 %copy-start = (f32[2,512,256]{2,1,0:T(8,128)S(1)}, f32[2,512,256]{2,1,0:T(8,128)}, u32[]{:S(2)}) copy-start(f32[2,512,256]{2,1,0:T(8,128)} %get-tuple-element.154.refs_0_.first) | copy-start | bytes 3145732
  11.5 21.7 %copy-start.1 = (f32[2,512,256]{2,1,0:T(8,128)S(1)}, f32[2,512,256]{2,1,0:T(8,128)}, u32[]{:S(2)}) copy-start(f32[2,512,256]{2,1,0:T(8,128)} %get-tuple-element.153.refs_3_.last) | copy-start | bytes 3145732
  11.6 15.5 %copy-start.16 = (f32[40,8,256]{2,1,0:T(8,128)S(1)}, f32[40,8,256]{2,1,0:T(8,128)}, u32[]{:S(2)}) copy-start(f32[40,8,256]{2,1,0:T(8,128)} %get-tuple-element.191.refs_2_) | copy-start | bytes 983044 | tf_op jit(solution)/shard_map/cond
  11.6 15.5 %copy-start.20 = (f32[12,8,256]{2,1,0:T(8,128)S(1)}, f32[12,8,256]{2,1,0:T(8,128)}, u32[]{:S(2)}) copy-start(f32[12,8,256]{2,1,0:T(8,128)} %get-tuple-element.192.refs_3_) | copy-start | bytes 294916 | tf_op jit(solution)/shard_map/cond
  16.3 1.5 %collective-permute-start = (f32[28,8,256]{2,1,0:T(8,128)S(1)}, f32[28,8,256]{2,1,0:T(8,128)S(1)}, u32[]{:S(2)}, u32[]{:S(2)}) collective-permute-start(f32[28,8,256]{2,1,0:T(8,128)S(1)} %get-tuple-element.75), channel_id=1, source_target_pairs={{0,1},{1,0},{2,3},{3,2},{4,5},{5,4},{6,7},{7,6},{8,9},{9,8},{10,11... | collective-permute-start | bytes 688136 | tf_op jit(solution)/shard_map/cond/branch_1_fun/ppermute | solution.py:647
  17.8 7.7 %collective-permute-start.1 = (f32[28,8,256]{2,1,0:T(8,128)S(1)}, f32[28,8,256]{2,1,0:T(8,128)S(1)}, u32[]{:S(2)}, u32[]{:S(2)}) collective-permute-start(f32[28,8,256]{2,1,0:T(8,128)S(1)} %add.8), channel_id=1, source_target_pairs={{0,2},{1,3},{2,0},{3,1},{4,6},{5,7},{6,4},{7,5},{8,10},{9,11},{10,... | collective-permute-start | bytes 688136 | tf_op jit(solution)/shard_map/cond/branch_1_fun/ppermute | solution.py:647
  25.6 1.6 %collective-permute-start.2 = (f32[28,8,256]{2,1,0:T(8,128)S(1)}, f32[28,8,256]{2,1,0:T(8,128)S(1)}, u32[]{:S(2)}, u32[]{:S(2)}) collective-permute-start(f32[28,8,256]{2,1,0:T(8,128)S(1)} %add.9.refs_0_), channel_id=1, source_target_pairs={{0,1},{1,0},{2,3},{3,2},{4,5},{5,4},{6,7},{7,6},{8,9},{9,8},{10,11... | collective-permute-start | bytes 688136 | tf_op jit(solution)/shard_map/cond/branch_1_fun/ppermute | solution.py:647
  29.4 26.5 %collective-permute-start.9 = (f32[2,16,256]{2,1,0:T(8,128)}, f32[2,16,256]{2,1,0:T(8,128)}, u32[]{:S(2)}, u32[]{:S(2)}) collective-permute-start(f32[2,16,256]{2,1,0:T(8,128)} %get-tuple-element.198), channel_id=1, source_target_pairs={{4,0},{8,4},{12,8},{16,12},{20,16},{24,20},{28,24},{0,28},{5,1},{9... | collective-permute-start | bytes 98312 | tf_op jit(solution)/shard_map/ppermute | solution.py:690
  31.4 24.6 %collective-permute-start.8 = (f32[2,16,256]{2,1,0:T(8,128)}, f32[2,16,256]{2,1,0:T(8,128)}, u32[]{:S(2)}, u32[]{:S(2)}) collective-permute-start(f32[2,16,256]{2,1,0:T(8,128)} %get-tuple-element.199), channel_id=1, source_target_pairs={{0,4},{4,8},{8,12},{12,16},{16,20},{20,24},{24,28},{28,0},{1,5},{5... | collective-permute-start | bytes 98312 | tf_op jit(solution)/shard_map/ppermute | solution.py:687
  33.2 26.1 %copy-start.6 = (bf16[1280,256]{1,0:T(8,128)(2,1)}, bf16[1280,256]{1,0:T(8,128)(2,1)S(1)}, u32[]{:S(2)}) copy-start(bf16[1280,256]{1,0:T(8,128)(2,1)S(1)} %get-tuple-element.160.refs_7_.circ.refs_6_) | copy-start | bytes 1966084
  46.2 13.1 %copy-start.4 = (f32[8,512,256]{2,1,0:T(8,128)}, f32[8,512,256]{2,1,0:T(8,128)S(1)}, u32[]{:S(2)}) copy-start(f32[8,512,256]{2,1,0:T(8,128)S(1)} %get-tuple-element.168.refs_0_.refs_1_) | copy-start | bytes 12582916
  46.3 13.0 %copy-start.10 = (bf16[128,512]{1,0:T(8,128)(2,1)S(1)}, bf16[128,512]{1,0:T(8,128)(2,1)}, u32[]{:S(2)}) copy-start(bf16[128,512]{1,0:T(8,128)(2,1)} %get-tuple-element.161.refs_8_) | copy-start | bytes 393220
  46.3 13.0 %copy-start.12 = (f32[40,8,256]{2,1,0:T(8,128)S(1)}, f32[40,8,256]{2,1,0:T(8,128)}, u32[]{:S(2)}) copy-start(f32[40,8,256]{2,1,0:T(8,128)} %get-tuple-element.172) | copy-start | bytes 983044
  46.3 13.0 %copy-start.14 = (f32[14,8,256]{2,1,0:T(8,128)S(1)}, f32[14,8,256]{2,1,0:T(8,128)}, u32[]{:S(2)}) copy-start(f32[14,8,256]{2,1,0:T(8,128)} %get-tuple-element.174) | copy-start | bytes 344068
  46.3 13.0 %copy-start.15 = (f32[12,8,256]{2,1,0:T(8,128)S(1)}, f32[12,8,256]{2,1,0:T(8,128)}, u32[]{:S(2)}) copy-start(f32[12,8,256]{2,1,0:T(8,128)} %get-tuple-element.173) | copy-start | bytes 294916
  46.3 13.0 %copy-start.24 = (f32[40]{0:T(128)S(1)}, f32[40]{0:T(128)}, u32[]{:S(2)}) copy-start(f32[40]{0:T(128)} %param.31) | copy-start | bytes 484
  46.3 13.0 %copy-start.26 = (f32[40]{0:T(128)S(1)}, f32[40]{0:T(128)}, u32[]{:S(2)}) copy-start(f32[40]{0:T(128)} %param.32) | copy-start | bytes 484
  46.3 13.0 %copy-start.28 = (f32[40]{0:T(128)S(1)}, f32[40]{0:T(128)}, u32[]{:S(2)}) copy-start(f32[40]{0:T(128)} %param.33) | copy-start | bytes 484
  46.3 13.0 %copy-start.30 = (f32[14]{0:T(128)S(1)}, f32[14]{0:T(128)}, u32[]{:S(2)}) copy-start(f32[14]{0:T(128)} %param.34) | copy-start | bytes 172
  46.3 13.0 %copy-start.32 = (s32[40]{0:T(128)S(1)}, s32[40]{0:T(128)}, u32[]{:S(2)}) copy-start(s32[40]{0:T(128)} %param.26) | copy-start | bytes 484
  56.0 47.9 %collective-permute-start.12 = (f32[2,512,256]{2,1,0:T(8,128)}, f32[2,512,256]{2,1,0:T(8,128)S(1)}, u32[]{:S(2)}, u32[]{:S(2)}) collective-permute-start(f32[2,512,256]{2,1,0:T(8,128)} %get-tuple-element.179), channel_id=1, source_target_pairs={{4,0},{8,4},{12,8},{16,12},{20,16},{24,20},{28,24},{0,28},{5,1},{9... | collective-permute-start | bytes 3145736 | tf_op jit(solution)/shard_map/ppermute | solution.py:690
  59.3 44.5 %collective-permute-start.10 = (f32[2,256,256]{2,1,0:T(8,128)}, f32[2,256,256]{2,1,0:T(8,128)}, u32[]{:S(2)}, u32[]{:S(2)}) collective-permute-start(f32[2,256,256]{2,1,0:T(8,128)} %get-tuple-element.165), channel_id=1, source_target_pairs={{0,4},{4,8},{8,12},{12,16},{16,20},{20,24},{24,28},{28,0},{1,5},{5... | collective-permute-start | bytes 1572872 | tf_op jit(solution)/shard_map/ppermute | solution.py:687
  64.8 1.5 %collective-permute-start.3 = (f32[28,8,256]{2,1,0:T(8,128)S(1)}, f32[28,8,256]{2,1,0:T(8,128)S(1)}, u32[]{:S(2)}, u32[]{:S(2)}) collective-permute-start(f32[28,8,256]{2,1,0:T(8,128)S(1)} %get-tuple-element.101), channel_id=1, source_target_pairs={{0,1},{1,0},{2,3},{3,2},{4,5},{5,4},{6,7},{7,6},{8,9},{9,8},{10,11... | collective-permute-start | bytes 688136 | tf_op jit(solution)/shard_map/cond/branch_1_fun/ppermute | solution.py:647
  66.4 7.7 %collective-permute-start.4 = (f32[28,8,256]{2,1,0:T(8,128)S(1)}, f32[28,8,256]{2,1,0:T(8,128)S(1)}, u32[]{:S(2)}, u32[]{:S(2)}) collective-permute-start(f32[28,8,256]{2,1,0:T(8,128)S(1)} %add.10), channel_id=1, source_target_pairs={{0,2},{1,3},{2,0},{3,1},{4,6},{5,7},{6,4},{7,5},{8,10},{9,11},{10,... | collective-permute-start | bytes 688136 | tf_op jit(solution)/shard_map/cond/branch_1_fun/ppermute | solution.py:647
  74.1 1.6 %collective-permute-start.5 = (f32[28,8,256]{2,1,0:T(8,128)S(1)}, f32[28,8,256]{2,1,0:T(8,128)S(1)}, u32[]{:S(2)}, u32[]{:S(2)}) collective-permute-start(f32[28,8,256]{2,1,0:T(8,128)S(1)} %add.11.refs_0_), channel_id=1, source_target_pairs={{0,1},{1,0},{2,3},{3,2},{4,5},{5,4},{6,7},{7,6},{8,9},{9,8},{10,11... | collective-permute-start | bytes 688136 | tf_op jit(solution)/shard_map/cond/branch_1_fun/ppermute | solution.py:647
  82.0 21.8 %collective-permute-start.11 = (f32[2,256,256]{2,1,0:T(8,128)}, f32[2,256,256]{2,1,0:T(8,128)S(1)}, u32[]{:S(2)}, u32[]{:S(2)}) collective-permute-start(f32[2,256,256]{2,1,0:T(8,128)} %get-tuple-element.178), channel_id=1, source_target_pairs={{0,4},{4,8},{8,12},{12,16},{16,20},{20,24},{24,28},{28,0},{1,5},{5... | collective-permute-start | bytes 1572872 | tf_op jit(solution)/shard_map/ppermute | solution.py:687
  82.1 21.7 %collective-permute-start.14 = (f32[2,16,256]{2,1,0:T(8,128)S(1)}, f32[2,16,256]{2,1,0:T(8,128)S(1)}, u32[]{:S(2)}, u32[]{:S(2)}) collective-permute-start(f32[2,16,256]{2,1,0:T(8,128)S(1)} %get-tuple-element.196), channel_id=1, source_target_pairs={{4,0},{8,4},{12,8},{16,12},{20,16},{24,20},{28,24},{0,28},{5,1},{9... | collective-permute-start | bytes 98312 | tf_op jit(solution)/shard_map/ppermute | solution.py:690
  86.9 16.9 %collective-permute-start.13 = (f32[2,16,256]{2,1,0:T(8,128)S(1)}, f32[2,16,256]{2,1,0:T(8,128)S(1)}, u32[]{:S(2)}, u32[]{:S(2)}) collective-permute-start(f32[2,16,256]{2,1,0:T(8,128)S(1)} %get-tuple-element.197), channel_id=1, source_target_pairs={{0,4},{4,8},{8,12},{12,16},{16,20},{20,24},{24,28},{28,0},{1,5},{5... | collective-permute-start | bytes 98312 | tf_op jit(solution)/shard_map/ppermute | solution.py:687
  (17 other events, 158.2 us)
